TPU v7x, 512 devices: a whole 4x4x16 slice. The times are simulated.
512 devices in a mesh: crop: 16 (over x, z_hi, core), seq: 32 (over y, z_lo).
Axes of the slice: x: 4, y: 4, z: 16 (z_hi: 2, z_lo: 8; z = z_hi * 8 + z_lo), core: 2. Of those that a mesh axis runs over, the one named last changes fastest.
Arguments:
- queries: bfloat16 [65536, 2048], P(('crop', 'seq')), parts along dimension 0, may hold values from -13 to 13
- keys: bfloat16 [65536, 2048], P(('crop', 'seq')), parts along dimension 0, may hold values from -6 to 6
- values: bfloat16 [65536, 2048], P(('crop', 'seq')), parts along dimension 0, may hold values from -6 to 6
- proj_weight: bfloat16 [2048, 256], replicated, may hold values from -0.125 to 0.125
- norm_gain: float32 [256], replicated, may hold values from 0.1 to 1.9
- conv_weight: bfloat16 [9, 256, 256], replicated, may hold values from -0.125 to 0.125
- conv_bias: float32 [256], replicated, may hold values from -3 to 3
- class_weight: bfloat16 [9, 16, 256], replicated, may hold values from -4.5 to 4.5
- class_bias: float32 [16], replicated, may hold values from -4 to 4
- labels: int32 [4096, 256], P(('crop', 'seq')), parts along dimension 0, may hold values from 0 to 15
Outputs:
- logits: float32 [16, 4096, 256], P(None, ('crop', 'seq')), parts along dimension 1
- pixel_loss: float32 [4096, 256], P(('crop', 'seq')), parts along dimension 0
- loss: float32 [16], P('crop'), parts along dimension 0
There are 16 independent parts, one for each index of `crop`. A program takes and returns all parts, laid end to end along the dimension named above; an argument that names none is the same for every part. Nothing has to cross between parts.
All inputs are finite; a program needn't handle non-finite values.
Results may differ from a plain program's by a relative error of at most 0.0085.
The roundings to bfloat16 on the way count: a program that leaves them out, or rounds other values in their place, can miss the bound.
Values may be sent and summed in bfloat16 or wider, within the bound.
No kernel may reach another device: no remote copies, remote signals or barrier semaphores. Data moves between devices by JAX's collectives and lax.ppermute only.
A program may use at most 64 MiB of HBM per device.

v0:
```python
import math

import jax
import jax.numpy as jnp
from jax import lax
from jax.sharding import PartitionSpec as P

HEADS = 16
HEAD_DIM = 128
UPSCALE = 4
GRID_COLS = 64


EPSILON = 1e-05


def partner_2(shard, axis, bit):
    return lax.ppermute(shard, axis, [(i, i ^ 1 << bit) for i in range(lax.axis_size(axis))])


def extended_2(block, sides, width):
    for axis, dim in sides:
        count = lax.axis_size(axis)
        forward = [(i, i + 1) for i in range(count - 1)]
        backward = [(target, source) for source, target in forward]
        low = lax.ppermute(
            lax.slice_in_dim(block, block.shape[dim] - width, None, axis=dim), axis, forward
        )
        high = lax.ppermute(lax.slice_in_dim(block, 0, width, axis=dim), axis, backward)
        block = jnp.concatenate([low, block, high], axis=dim)
    return block


def from_everyone(shard, axis):
    devices = lax.axis_size(axis)
    return lax.all_to_all(
        jnp.broadcast_to(shard[None], (devices, *shard.shape)), axis, 0, 0, tiled=True
    )


def of_everyone(shard, axis):
    return from_everyone(shard, axis).sum(axis=0)


def rotate(packed, row_ids, col_ids):
    count_rows = packed.shape[0]
    head_rows = packed.reshape(count_rows, HEADS, HEAD_DIM).astype(jnp.float32)
    quarter = HEAD_DIM // 4
    omegas = jnp.power(jnp.float32(100.0), -jnp.arange(quarter, dtype=jnp.float32) / quarter)
    pieces = []
    for coords, offset in ((row_ids, 0), (col_ids, 2 * quarter)):
        angles = coords.astype(jnp.float32)[:, None, None] * omegas[None, None, :]
        cosine = jnp.cos(angles)
        sine_part = jnp.sin(angles)
        first_half = head_rows[:, :, offset : offset + quarter]
        second_half = head_rows[:, :, offset + quarter : offset + 2 * quarter]
        pieces.append(first_half * cosine - second_half * sine_part)
        pieces.append(second_half * cosine + first_half * sine_part)
    return (
        jnp.concatenate(pieces, axis=2).reshape(count_rows, HEADS * HEAD_DIM).astype(jnp.bfloat16)
    )


def attend(queries, keys, values):
    total_rows = queries.shape[0]
    block = math.gcd(512, total_rows)
    scale = queries.shape[2] ** (-0.5)

    def one_block(query_block):
        scores = (
            jnp.einsum("qhd,khd->hqk", query_block, keys, preferred_element_type=jnp.float32)
            * scale
        )
        highest = jnp.max(scores, axis=2, keepdims=True)
        exponent = jnp.exp(scores - highest)
        weights = (exponent / jnp.sum(exponent, axis=2, keepdims=True)).astype(jnp.bfloat16)
        mixed = jnp.einsum("hqk,khd->qhd", weights, values, preferred_element_type=jnp.float32)
        return mixed.astype(jnp.bfloat16)

    blocked = queries.reshape(total_rows // block, block, queries.shape[1], queries.shape[2])
    return lax.map(one_block, blocked).reshape(queries.shape)


def normalize(features, gain):
    center = jnp.mean(features, axis=-1, keepdims=True)
    spread = jnp.mean((features - center) ** 2, axis=-1, keepdims=True)
    return (features - center) / jnp.sqrt(spread + EPSILON) * gain


def convolve(padded, weight):
    out_rows = padded.shape[0] - 2
    out_cols = padded.shape[1] - 2
    summed = jnp.zeros((out_rows * out_cols, weight.shape[2]), jnp.float32)
    for tap_index in range(9):
        tap_row, tap_col = (tap_index // 3, tap_index % 3)
        window = padded[tap_row : tap_row + out_rows, tap_col : tap_col + out_cols].reshape(
            -1, padded.shape[2]
        )
        summed = summed + jnp.dot(window, weight[tap_index], preferred_element_type=jnp.float32)
    return summed.reshape(out_rows, out_cols, weight.shape[2])


def classify(padded, class_weight):
    out_rows = padded.shape[0] - 2
    out_cols = padded.shape[1] - 2
    summed = jnp.zeros((class_weight.shape[1], out_rows * out_cols), jnp.float32)
    for tap_index in range(9):
        tap_row, tap_col = (tap_index // 3, tap_index % 3)
        window = padded[tap_row : tap_row + out_rows, tap_col : tap_col + out_cols].reshape(
            -1, padded.shape[2]
        )
        summed = summed + lax.dot_general(
            class_weight[tap_index],
            window,
            (((1,), (1,)), ((), ())),
            preferred_element_type=jnp.float32,
        )
    return summed.reshape(class_weight.shape[1], out_rows, out_cols)


def pixel_losses(logits, labels):
    highest = jnp.max(logits, axis=0)
    log_total = highest + jnp.log(jnp.sum(jnp.exp(logits - highest[None]), axis=0))
    class_ids = jnp.arange(logits.shape[0], dtype=jnp.int32)[:, None, None]
    picked = jnp.sum(jnp.where(class_ids == labels[None], logits, jnp.zeros_like(logits)), axis=0)
    return log_total - picked


def body(
    queries,
    keys,
    values,
    proj_weight,
    norm_gain,
    conv_weight,
    conv_bias,
    class_weight,
    class_bias,
    labels,
):
    devices = lax.axis_size("seq")
    place = lax.axis_index("seq")
    local_tokens = queries.shape[0]
    strip = local_tokens // GRID_COLS
    positions = jnp.arange(local_tokens, dtype=jnp.int32)
    row_ids = place * strip + positions // GRID_COLS
    col_ids = positions % GRID_COLS
    rotated_queries = rotate(queries, row_ids, col_ids)
    rotated_keys = rotate(keys, row_ids, col_ids)
    per_device = 1
    split = devices // HEADS
    groups = HEADS // per_device
    width = per_device * HEAD_DIM
    part_rows = local_tokens // split
    query_send = (
        rotated_queries.reshape(split, part_rows, groups, width)
        .transpose(1, 2, 0, 3)
        .reshape(part_rows, devices, width)
    )
    key_grouped = rotated_keys.reshape(local_tokens, groups, width)
    value_grouped = values.reshape(local_tokens, groups, width)
    stacked = jnp.stack([key_grouped, value_grouped], axis=2).reshape(local_tokens, devices, width)
    query_recv, mine = (
        lax.all_to_all(query_send, "seq", split_axis=1, concat_axis=0, tiled=True),
        lax.all_to_all(stacked, "seq", split_axis=1, concat_axis=0, tiled=True),
    )
    partner = partner_2(mine, "seq", 0)
    even_place = place % 2 == 0
    key_recv = jnp.where(even_place, mine, partner)
    value_recv = jnp.where(even_place, partner, mine)
    attended = attend(query_recv, key_recv, value_recv)
    outgoing = attended.reshape(devices, part_rows, width)
    returned = lax.all_to_all(outgoing, "seq", split_axis=0, concat_axis=0, tiled=True)
    mixed = (
        returned.reshape(groups, split, part_rows, width)
        .transpose(1, 2, 0, 3)
        .reshape(local_tokens, HEADS * HEAD_DIM)
    )
    features = jnp.dot(mixed, proj_weight, preferred_element_type=jnp.float32)
    activated = jax.nn.gelu(normalize(features, norm_gain), approximate=False).astype(jnp.bfloat16)
    activated = activated.reshape(strip, GRID_COLS, -1)
    extended = extended_2(activated, (("seq", 0),), 2)
    padded = jnp.pad(extended, ((0, 0), (1, 1), (0, 0)))
    hidden = jax.nn.gelu(convolve(padded, conv_weight) + conv_bias, approximate=False)
    grid_rows = place * strip - 1 + jnp.arange(strip + 2, dtype=jnp.int32)
    inside = (grid_rows >= 0) & (grid_rows < strip * devices)
    hidden_ext = jnp.where(inside[:, None, None], hidden, jnp.zeros_like(hidden)).astype(
        jnp.bfloat16
    )
    upsampled = jnp.repeat(hidden_ext, UPSCALE, axis=0)[
        UPSCALE - 1 : UPSCALE - 1 + UPSCALE * strip + 2
    ]
    upsampled = jnp.repeat(upsampled, UPSCALE, axis=1)
    logits = (
        classify(jnp.pad(upsampled, ((0, 0), (1, 1), (0, 0))), class_weight)
        + class_bias[:, None, None]
    )
    losses = pixel_losses(logits, labels)
    summed_loss = of_everyone(jnp.sum(losses), "seq")
    loss = (summed_loss / (losses.shape[0] * losses.shape[1] * devices)).reshape(1)
    return (logits, losses, loss)


def solution(mesh):
    in_specs = (
        P(("crop", "seq"), None),
        P(("crop", "seq"), None),
        P(("crop", "seq"), None),
        P(),
        P(),
        P(),
        P(),
        P(),
        P(),
        P(("crop", "seq"), None),
    )
    out_specs = (P(None, ("crop", "seq"), None), P(("crop", "seq"), None), P("crop"))
    return jax.shard_map(body, mesh=mesh, in_specs=in_specs, out_specs=out_specs, check_vma=False)
```

profile of v0, /device:TPU:6, one launch (start us, length us, event | category | flops | bytes accessed | tf_op | source)
XLA Modules:
  0.0 252.8 jit_solution(7579905752646927469)
XLA Ops:
  5.3 2.8 %fusion.13 = (bf16[128,16,1,32]{3,0,2,1:T(8,128)(2,1)S(1)}, bf16[128,16,1,32]{3,0,2,1:T(8,128)(2,1)S(1)}, bf16[128,16,32]{2,0,1:T(8,128)(2,1)S(1)}, bf16[128,16,...) fusion(f32[128,16,32]{2,1,0:T(8,128)S(1)} %get-tuple-element.83, ...), kind=kLoop, calls=%fused_computation.50 | loop fusion | flops 2097152 | bytes 3211264 | tf_op jit(solution)/shard_map/concatenate | solution.py:60
  8.8 66.5 %all_to_all.44 = bf16[128,32,128]{2,0,1:T(8,128)(2,1)S(1)} all-to-all(bf16[128,32,128]{2,0,1:T(8,128)(2,1)S(1)} %bitcast.199), channel_id=1, replica_groups=mesh['crop'=16,'seq'=32] {'seq'}, dimensions={1} | all-to-all | bytes 2097152 | tf_op jit(solution)/shard_map/all_to_all | solution.py:165
  75.3 4.2 %collective-permute-start = (bf16[4096,1,128]{2,0,1:T(8,128)(2,1)S(1)}, bf16[4096,1,128]{2,0,1:T(8,128)(2,1)S(1)}, u32[]{:S(2)}, u32[]{:S(2)}) collective-permute-start(bf16[4096,1,128]{2,0,1:T(8,128)(2,1)S(1)} %bitcast.197), channel_id=1, source_target_pairs={{0,1},{1,0},{2,3},{3,2},{4,5},{5,4},{6,7},{7,6},{8,9},{9,8},{10,11... | collective-permute-start | bytes 3145736 | tf_op jit(solution)/shard_map/ppermute | solution.py:18
  81.0 5.6 %all-to-all-start = ((bf16[64,32,128]{2,0,1:T(8,128)(2,1)}), bf16[64,32,128]{2,0,1:T(8,128)(2,1)}, u32[]{:S(2)}, u32[]{:S(2)}) async-start(bf16[64,32,128]{2,0,1:T(8,128)(2,1)} %bitcast.9), calls=%async_computation | async-start | bytes 1048576 | tf_op jit(solution)/shard_map/all_to_all | solution.py:164
  86.6 20.5 %collective-permute-done = bf16[4096,1,128]{2,0,1:T(8,128)(2,1)S(1)} collective-permute-done((bf16[4096,1,128]{2,0,1:T(8,128)(2,1)S(1)}, bf16[4096,1,128]{2,0,1:T(8,128)(2,1)S(1)}, u32[]{:S(2)}, u32[]{:S(2)}) %collective-permute-start) | collective-permute-done | bytes 1048608 | tf_op jit(solution)/shard_map/ppermute | solution.py:18
  108.1 2.4 broadcast_select_fusion
  110.5 13.2 %all-to-all-done = bf16[64,32,128]{2,0,1:T(8,128)(2,1)} async-done(((bf16[64,32,128]{2,0,1:T(8,128)(2,1)}), bf16[64,32,128]{2,0,1:T(8,128)(2,1)}, u32[]{:S(2)}, u32[]{:S(2)}) %all-to-all-start) | async-done | bytes 524320 | tf_op jit(solution)/shard_map/all_to_all | solution.py:164
  123.7 27.5 %while.10 = (s32[]{:T(128)}, bf16[4,512,1,128]{3,1,2,0:T(8,128)(2,1)}, bf16[4,512,1,128]{3,1,2,0:T(8,128)(2,1)}, bf16[4096,1,128]{2,0,1:T(8,128)(2,1)S(1)}, bf16[4096,1,128]{2,0,1:T(8,128)(2,1)}, /*index=5*/s32[]{:T(128)}) while((s32[]{:T(128)}, bf16[4,512,1,128]{3,1,2,0:T(8,128)(2,1)}, bf16[4,512,1,128]{3,1,2,0:T(8,128)(2,1)}, ...), condition=%wide.region_3.4_spmd, body=%wide.region_0.3_spmd.sunk | while | flops 1092680704 | bytes 31730784 | solution.py:81
  123.7 2.2 multiply_reduce_fusion.3
  127.5 3.1 %fusion.113 = bf16[4,512,1,128]{3,1,2,0:T(8,128)(2,1)} fusion(bf16[4,512,1,128]{3,1,2,0:T(8,128)(2,1)} %get-tuple-element.162, s32[]{:T(128)} %get-tuple-element.161, f32[512,4096]{1,0:T(8,128)S(1)} %get-tuple-element.153, f32[512]{0:T(512)S(1)} %fusion.112, f32[512]{0:T(512)S(1)} %get-tuple-element.154, bf16[4096,1,128]{2,0,1:T(8,128)(2,1)S(1)} %copy-done.7), kind=kOutput, calls=%fused_computation.7.clone.1 | convolution fusion | flops 545325056 | bytes 9572864 | tf_op jit(solution)/shard_map/while/body/eval_jaxpr/hqk,khd->qhd/dot_general | solution.py:77
  130.6 2.2 multiply_reduce_fusion.3
  134.4 3.1 %fusion.113 = bf16[4,512,1,128]{3,1,2,0:T(8,128)(2,1)} fusion(bf16[4,512,1,128]{3,1,2,0:T(8,128)(2,1)} %get-tuple-element.162, s32[]{:T(128)} %get-tuple-element.161, f32[512,4096]{1,0:T(8,128)S(1)} %get-tuple-element.153, f32[512]{0:T(512)S(1)} %fusion.112, f32[512]{0:T(512)S(1)} %get-tuple-element.154, bf16[4096,1,128]{2,0,1:T(8,128)(2,1)S(1)} %copy-done.7), kind=kOutput, calls=%fused_computation.7.clone.1 | convolution fusion | flops 545325056 | bytes 9572864 | tf_op jit(solution)/shard_map/while/body/eval_jaxpr/hqk,khd->qhd/dot_general | solution.py:77
  137.5 2.2 multiply_reduce_fusion.3
  141.2 3.1 %fusion.113 = bf16[4,512,1,128]{3,1,2,0:T(8,128)(2,1)} fusion(bf16[4,512,1,128]{3,1,2,0:T(8,128)(2,1)} %get-tuple-element.162, s32[]{:T(128)} %get-tuple-element.161, f32[512,4096]{1,0:T(8,128)S(1)} %get-tuple-element.153, f32[512]{0:T(512)S(1)} %fusion.112, f32[512]{0:T(512)S(1)} %get-tuple-element.154, bf16[4096,1,128]{2,0,1:T(8,128)(2,1)S(1)} %copy-done.7), kind=kOutput, calls=%fused_computation.7.clone.1 | convolution fusion | flops 545325056 | bytes 9572864 | tf_op jit(solution)/shard_map/while/body/eval_jaxpr/hqk,khd->qhd/dot_general | solution.py:77
  144.4 2.2 multiply_reduce_fusion.3
  148.1 3.1 %fusion.113 = bf16[4,512,1,128]{3,1,2,0:T(8,128)(2,1)} fusion(bf16[4,512,1,128]{3,1,2,0:T(8,128)(2,1)} %get-tuple-element.162, s32[]{:T(128)} %get-tuple-element.161, f32[512,4096]{1,0:T(8,128)S(1)} %get-tuple-element.153, f32[512]{0:T(512)S(1)} %fusion.112, f32[512]{0:T(512)S(1)} %get-tuple-element.154, bf16[4096,1,128]{2,0,1:T(8,128)(2,1)S(1)} %copy-done.7), kind=kOutput, calls=%fused_computation.7.clone.1 | convolution fusion | flops 545325056 | bytes 9572864 | tf_op jit(solution)/shard_map/while/body/eval_jaxpr/hqk,khd->qhd/dot_general | solution.py:77
  151.3 6.5 %all-to-all-start.2 = ((bf16[32,64,128]{2,1,0:T(8,128)(2,1)}), bf16[32,64,128]{2,1,0:T(8,128)(2,1)S(1)}, u32[]{:S(2)}, u32[]{:S(2)}) async-start(bf16[32,64,128]{2,1,0:T(8,128)(2,1)} %bitcast.27), calls=%async_computation.2 | async-start | bytes 1048576 | tf_op jit(solution)/shard_map/all_to_all | solution.py:173
  157.8 27.3 %all-to-all-done.2 = bf16[32,64,128]{2,1,0:T(8,128)(2,1)S(1)} async-done(((bf16[32,64,128]{2,1,0:T(8,128)(2,1)}), bf16[32,64,128]{2,1,0:T(8,128)(2,1)S(1)}, u32[]{:S(2)}, u32[]{:S(2)}) %all-to-all-start.2) | async-done | bytes 524320 | tf_op jit(solution)/shard_map/all_to_all | solution.py:173
  186.5 3.0 %collective-permute-start.1 = (bf16[2,64,256]{2,1,0:T(8,128)(2,1)S(1)}, bf16[2,64,256]{2,1,0:T(8,128)(2,1)S(1)}, u32[]{:S(2)}, u32[]{:S(2)}) collective-permute-start(bf16[2,64,256]{2,1,0:T(8,128)(2,1)S(1)} %bitcast.214), channel_id=1, source_target_pairs={{0,1},{1,2},{2,3},{3,4},{4,5},{5,6},{6,7},{7,8},{8,9},{9,10},{10,1... | collective-permute-start | bytes 196616 | tf_op jit(solution)/shard_map/ppermute | solution.py:26
  191.3 4.6 %collective-permute-done.2 = bf16[2,64,256]{2,1,0:T(8,128)(2,1)S(1)} collective-permute-done((bf16[2,64,256]{2,1,0:T(8,128)(2,1)S(1)}, bf16[2,64,256]{2,1,0:T(8,128)(2,1)S(1)}, u32[]{:S(2)}, u32[]{:S(2)}) %collective-permute-start.2) | collective-permute-done | bytes 65568 | tf_op jit(solution)/shard_map/ppermute | solution.py:29
  200.3 6.9 %pad_slice_fusion = (bf16[8,256,256]{2,1,0:T(8,128)(2,1)}, bf16[8,256,256]{2,1,0:T(8,128)(2,1)}, bf16[8,256,256]{2,1,0:T(8,128)(2,1)}, bf16[8,256,256]{2,1,0:T(8...) fusion(bf16[10,256,256]{2,1,0:T(8,128)(2,1)} %reshape.386), kind=kLoop, calls=%fused_computation.44 | loop fusion | bytes 7602176 | tf_op jit(solution)/shard_map/slice | solution.py:109
  212.0 1.7 fusion.70
  220.3 17.5 %all-to-all-start.3 = ((f32[32,1,1]{2,1,0:T(1,128)}), f32[32,1,1]{2,1,0:T(1,128)S(1)}, u32[]{:S(2)}, u32[]{:S(2)}) async-start(f32[32,1,1]{2,1,0:T(1,128)} %broadcast_in_dim.66), calls=%async_computation.3 | async-start | bytes 32768 | tf_op jit(solution)/shard_map/all_to_all | solution.py:36
  239.3 11.1 %all-to-all-done.3 = f32[32,1,1]{2,1,0:T(1,128)S(1)} async-done(((f32[32,1,1]{2,1,0:T(1,128)}), f32[32,1,1]{2,1,0:T(1,128)S(1)}, u32[]{:S(2)}, u32[]{:S(2)}) %all-to-all-start.3) | async-done | bytes 160 | tf_op jit(solution)/shard_map/all_to_all | solution.py:36
  (111 shorter events, 34.4 us)
Async XLA Ops:
  0.6 184.8 %copy-start = (bf16[2048,256]{1,0:T(8,128)(2,1)S(1)}, bf16[2048,256]{1,0:T(8,128)(2,1)}, u32[]{:S(2)}) copy-start(bf16[2048,256]{1,0:T(8,128)(2,1)} %param.15) | copy-start | bytes 3145732
  2.1 1.0 copy-start.10
  75.3 31.9 %collective-permute-start = (bf16[4096,1,128]{2,0,1:T(8,128)(2,1)S(1)}, bf16[4096,1,128]{2,0,1:T(8,128)(2,1)S(1)}, u32[]{:S(2)}, u32[]{:S(2)}) collective-permute-start(bf16[4096,1,128]{2,0,1:T(8,128)(2,1)S(1)} %bitcast.197), channel_id=1, source_target_pairs={{0,1},{1,0},{2,3},{3,2},{4,5},{5,4},{6,7},{7,6},{8,9},{9,8},{10,11... | collective-permute-start | bytes 3145736 | tf_op jit(solution)/shard_map/ppermute | solution.py:18
  81.0 42.7 %all-to-all-start = ((bf16[64,32,128]{2,0,1:T(8,128)(2,1)}), bf16[64,32,128]{2,0,1:T(8,128)(2,1)}, u32[]{:S(2)}, u32[]{:S(2)}) async-start(bf16[64,32,128]{2,0,1:T(8,128)(2,1)} %bitcast.9), calls=%async_computation | async-start | bytes 1048576 | tf_op jit(solution)/shard_map/all_to_all | solution.py:164
  123.7 34.0 %copy-start.13 = (s32[8,256]{1,0:T(8,128)S(1)}, s32[8,256]{1,0:T(8,128)}, u32[]{:S(2)}) copy-start(s32[8,256]{1,0:T(8,128)} %param.21) | copy-start | bytes 24580
  126.0 1.5 copy-start.7
  132.8 1.5 copy-start.7
  139.7 1.5 copy-start.7
  146.6 1.5 copy-start.7
  151.3 34.8 %copy-start.15 = (f32[256]{0:T(256)S(1)}, f32[256]{0:T(256)}, u32[]{:S(2)}) copy-start(f32[256]{0:T(256)} %param.16) | copy-start | bytes 3076
  151.3 33.8 %all-to-all-start.2 = ((bf16[32,64,128]{2,1,0:T(8,128)(2,1)}), bf16[32,64,128]{2,1,0:T(8,128)(2,1)S(1)}, u32[]{:S(2)}, u32[]{:S(2)}) async-start(bf16[32,64,128]{2,1,0:T(8,128)(2,1)} %bitcast.27), calls=%async_computation.2 | async-start | bytes 1048576 | tf_op jit(solution)/shard_map/all_to_all | solution.py:173
  185.4 10.7 %copy-start.6 = (bf16[9,256,256]{2,1,0:T(8,128)(2,1)S(1)}, bf16[9,256,256]{2,1,0:T(8,128)(2,1)}, u32[]{:S(2)}) copy-start(bf16[9,256,256]{2,1,0:T(8,128)(2,1)} %param.17) | copy-start | bytes 3538948
  186.5 4.9 %collective-permute-start.1 = (bf16[2,64,256]{2,1,0:T(8,128)(2,1)S(1)}, bf16[2,64,256]{2,1,0:T(8,128)(2,1)S(1)}, u32[]{:S(2)}, u32[]{:S(2)}) collective-permute-start(bf16[2,64,256]{2,1,0:T(8,128)(2,1)S(1)} %bitcast.214), channel_id=1, source_target_pairs={{0,1},{1,2},{2,3},{3,4},{4,5},{5,6},{6,7},{7,8},{8,9},{9,10},{10,1... | collective-permute-start | bytes 196616 | tf_op jit(solution)/shard_map/ppermute | solution.py:26
  189.5 6.5 %collective-permute-start.2 = (bf16[2,64,256]{2,1,0:T(8,128)(2,1)S(1)}, bf16[2,64,256]{2,1,0:T(8,128)(2,1)S(1)}, u32[]{:S(2)}, u32[]{:S(2)}) collective-permute-start(bf16[2,64,256]{2,1,0:T(8,128)(2,1)S(1)} %bitcast.215), channel_id=1, source_target_pairs={{1,0},{2,1},{3,2},{4,3},{5,4},{6,5},{7,6},{8,7},{9,8},{10,9},{11,1... | collective-permute-start | bytes 196616 | tf_op jit(solution)/shard_map/ppermute | solution.py:29
  198.5 1.8 copy-start.9
  207.2 1.4 slice-start
  209.3 2.8 %copy-start.12 = (bf16[9,16,256]{2,1,0:T(8,128)(2,1)S(1)}, bf16[9,16,256]{2,1,0:T(8,128)(2,1)}, u32[]{:S(2)}) copy-start(bf16[9,16,256]{2,1,0:T(8,128)(2,1)} %param.19) | copy-start | bytes 221188
  212.0 3.4 %copy-start.4 = (bf16[8,256,256]{2,1,0:T(8,128)(2,1)S(1)}, bf16[8,256,256]{2,1,0:T(8,128)(2,1)}, u32[]{:S(2)}) copy-start(bf16[8,256,256]{2,1,0:T(8,128)(2,1)} %get-tuple-element.78) | copy-start | bytes 3145732
  212.0 3.8 %copy-start.3 = (bf16[8,256,256]{2,1,0:T(8,128)(2,1)S(1)}, bf16[8,256,256]{2,1,0:T(8,128)(2,1)}, u32[]{:S(2)}) copy-start(bf16[8,256,256]{2,1,0:T(8,128)(2,1)} %get-tuple-element.79) | copy-start | bytes 3145732
  215.4 1.2 copy-start.2
  215.8 1.3 copy-start.1
  216.6 1.3 copy-start.5
  216.6 1.3 copy-start.14
  220.3 30.1 %all-to-all-start.3 = ((f32[32,1,1]{2,1,0:T(1,128)}), f32[32,1,1]{2,1,0:T(1,128)S(1)}, u32[]{:S(2)}, u32[]{:S(2)}) async-start(f32[32,1,1]{2,1,0:T(1,128)} %broadcast_in_dim.66), calls=%async_computation.3 | async-start | bytes 32768 | tf_op jit(solution)/shard_map/all_to_all | solution.py:36
  (3 other events, 3.0 us)
where the time goes:
time: 254 us; the launch traced here: 253 us
  waiting for transfers between devices  77.4 us (30%)
  blocking collectives  66.5 us (26%)
  starting transfers between devices  38.1 us (15%)
  matrix products  29.6 us (12%)
  local copies, waits for them, and re-layouts  19.7 us (8%)
  other arithmetic  18.5 us (7%)
  between operations  2.95 us (1%)
    all_to_all x1, blocking collectives, body(): lax.all_to_all(stacked, 'seq', split_axis=1, concat_axis=0, tiled=True)  66.5 us
    all_to_all x1, waiting for transfers between devices, body(): lax.all_to_all(outgoing, 'seq', split_axis=0, concat_axis=0, tiled=True)  27.3 us
    ppermute x1, waiting for transfers between devices, partner_2(): lax.ppermute(shard, axis, [(i, i ^ 1 << bit) for i in range(lax.axis_size...  20.5 us
    all_to_all x1, starting transfers between devices, from_everyone(): lax.all_to_all(jnp.broadcast_to(shard[None], (devices, *shard.shape)), ax...  17.5 us
    all_to_all x1, waiting for transfers between devices, body(): lax.all_to_all(query_send, 'seq', split_axis=1, concat_axis=0, tiled=True)  13.2 us
    dot_general x4, matrix products, one_block(): jnp.einsum('hqk,khd->qhd', weights, values, preferred_element_type=jnp.fl...  12.5 us
    all_to_all x1, waiting for transfers between devices, from_everyone(): lax.all_to_all(jnp.broadcast_to(shard[None], (devices, *shard.shape)), ax...  11.1 us
    dot_general x4, matrix products, one_block(): jnp.einsum('qhd,khd->hqk', query_block, keys, preferred_element_type=jnp....  8.95 us
  transfers between devices with their start and end apart: 6, of which 6 were waited for; matrix products, arithmetic and copies ran while one was open for 2% of the time, Pallas kernels for 0%

commit v1 on v0

v1 whole, which is shorter than its diff:
```python
import functools
import math

import jax
import jax.numpy as jnp
import numpy as np
from jax import lax
from jax.experimental import pallas as pl
from jax.experimental.pallas import tpu as pltpu
from jax.sharding import Mesh, PartitionSpec as P

HEADS = 16
HEAD_DIM = 128
UPSCALE = 4
COLS = 64
CHANNELS = 256
CLASSES = 16
YS = 4
ZS = 8
SEQ = YS * ZS
EPSILON = 1e-05
EXP_SCALE = HEAD_DIM**-0.5 * math.log2(math.e)
VMEM = pl.BlockSpec(memory_space=pltpu.VMEM)
SMEM = pl.BlockSpec(memory_space=pltpu.SMEM)
BF16 = jnp.bfloat16
F32 = jnp.float32


def rotary_tables():
    quarter = HEAD_DIM // 4
    omegas = np.power(np.float32(100.0), -np.arange(quarter, dtype=np.float32) / np.float32(quarter))
    angles = np.arange(COLS, dtype=np.float32)[:, None] * omegas[None, :].astype(np.float32)
    cosine = np.cos(angles).astype(np.float32)
    sine = np.sin(angles).astype(np.float32)
    wide_cos = np.concatenate([cosine] * 4, axis=1)
    wide_sin = np.concatenate([-sine, sine, -sine, sine], axis=1)
    return wide_cos, wide_sin


def gelu(x):
    return x * (0.5 * (1.0 + lax.erf(x * np.float32(math.sqrt(0.5)))))


def pack_kernel(info, q_ref, k_ref, v_ref, cos_ref, sin_ref, out_ref):
    core = info[0]
    place = info[1]
    lane = lax.broadcasted_iota(jnp.int32, (COLS, HEAD_DIM), 1)
    by_row = lane < HEAD_DIM // 2
    first = (lane % (HEAD_DIM // 2)) < HEAD_DIM // 4
    for half in range(2):
        row_id = 2 * place + half
        cosine = jnp.where(by_row, cos_ref[pl.ds(row_id, 1), :], cos_ref[...])
        sine = jnp.where(by_row, sin_ref[pl.ds(row_id, 1), :], sin_ref[...])
        rows = slice(half * COLS, (half + 1) * COLS)
        for sub in range(2):
            lanes = slice(sub * HEAD_DIM, (sub + 1) * HEAD_DIM)
            y = lax.rem(2 * sub + half + core, YS)
            for index, ref in ((0, q_ref), (1, k_ref)):
                x = ref[rows, lanes].astype(F32)
                partner = jnp.where(
                    first,
                    pltpu.roll(x, HEAD_DIM - HEAD_DIM // 4, 1),
                    pltpu.roll(x, HEAD_DIM // 4, 1),
                )
                out_ref[y, 0, index * COLS : (index + 1) * COLS, :] = (
                    x * cosine + partner * sine
                ).astype(BF16)
            out_ref[y, 0, 2 * COLS :, :] = v_ref[rows, lanes]


def pack(info, queries, keys, values, cosine, sine):
    tokens = queries.shape[0]
    wide = 2 * HEAD_DIM
    return pl.pallas_call(
        pack_kernel,
        grid_spec=pltpu.PrefetchScalarGridSpec(
            num_scalar_prefetch=1,
            grid=(ZS,),
            in_specs=[pl.BlockSpec((tokens, wide), lambda z, info: (0, z))] * 3
            + [pl.BlockSpec((COLS, HEAD_DIM), lambda z, info: (0, 0))] * 2,
            out_specs=pl.BlockSpec((YS, 1, 3 * COLS, HEAD_DIM), lambda z, info: (0, z, 0, 0)),
        ),
        out_shape=jax.ShapeDtypeStruct((YS, ZS, 3 * COLS, HEAD_DIM), BF16),
        name="pack",
    )(info, queries, keys, values, cosine, sine)


BLOCK = 4


def scores_of(query, key):
    return lax.dot_general(query, key, (((1,), (1,)), ((), ())), preferred_element_type=F32)


def with_ones(value):
    return jnp.concatenate([value, jnp.ones_like(value)], axis=1)


def own_kernel(mine_ref, acc_ref, top_ref):
    rows = BLOCK * COLS
    key = mine_ref[:, COLS : 2 * COLS, :].reshape(SEQ * COLS, HEAD_DIM)
    value = with_ones(mine_ref[:, 2 * COLS :, :].reshape(SEQ * COLS, HEAD_DIM))

    def step(i, carry):
        query = mine_ref[pl.ds(i * BLOCK, BLOCK), :COLS, :].reshape(rows, HEAD_DIM)
        scores = scores_of(query, key)
        top = jnp.max(scores, axis=1, keepdims=True)
        weights = jnp.exp2((scores - top) * EXP_SCALE).astype(BF16)
        out = pl.ds(pl.multiple_of(i * rows, rows), rows)
        acc_ref[out, :] = jnp.dot(weights, value, preferred_element_type=F32)
        top_ref[out, :] = jnp.broadcast_to(top, (rows, HEAD_DIM))
        return carry

    lax.fori_loop(0, SEQ // BLOCK, step, 0)


def other_kernel(mine_ref, other_ref, acc_ref, top_ref, out_ref):
    rows = BLOCK * COLS
    key = other_ref[:, :COLS, :].reshape(SEQ * COLS, HEAD_DIM)
    value = with_ones(other_ref[:, COLS:, :].reshape(SEQ * COLS, HEAD_DIM))

    def step(i, carry):
        query = mine_ref[pl.ds(i * BLOCK, BLOCK), :COLS, :].reshape(rows, HEAD_DIM)
        scores = scores_of(query, key)
        place = pl.ds(pl.multiple_of(i * rows, rows), rows)
        before = top_ref[place, :1]
        top = jnp.maximum(before, jnp.max(scores, axis=1, keepdims=True))
        weights = jnp.exp2((scores - top) * EXP_SCALE).astype(BF16)
        fade = jnp.exp2((before - top) * EXP_SCALE)
        total = acc_ref[place, :] * fade + jnp.dot(weights, value, preferred_element_type=F32)
        mixed = total[:, :HEAD_DIM] / total[:, HEAD_DIM:]
        out_ref[pl.ds(i * BLOCK, BLOCK), :, :] = mixed.astype(BF16).reshape(BLOCK, COLS, HEAD_DIM)
        return carry

    lax.fori_loop(0, SEQ // BLOCK, step, 0)


def attend(mine, swap):
    tokens = SEQ * COLS
    half_flops = 2 * tokens * tokens * HEAD_DIM * 3
    cost = pl.CostEstimate(flops=half_flops, bytes_accessed=4 << 20, transcendentals=tokens * tokens)
    other = swap(mine[:, COLS:, :])
    acc, top = pl.pallas_call(
        own_kernel,
        in_specs=[VMEM],
        out_specs=[VMEM, VMEM],
        out_shape=[
            jax.ShapeDtypeStruct((tokens, 2 * HEAD_DIM), F32),
            jax.ShapeDtypeStruct((tokens, HEAD_DIM), F32),
        ],
        cost_estimate=cost,
        name="own_keys",
    )(mine)
    return pl.pallas_call(
        other_kernel,
        in_specs=[VMEM] * 4,
        out_specs=VMEM,
        out_shape=jax.ShapeDtypeStruct((SEQ, COLS, HEAD_DIM), BF16),
        cost_estimate=cost,
        name="other_keys",
    )(mine, other, acc, top)


def features_kernel(info, mixed_ref, proj_ref, gain_ref, out_ref):
    core = info[0]
    strips = []
    for half in range(2):
        pieces = []
        for head in range(HEADS):
            y = lax.rem(2 * (head % 2) + half + core, YS)
            pieces.append(mixed_ref[y * ZS + head // 2])
        strips.append(jnp.concatenate(pieces, axis=1))
    mixed = jnp.concatenate(strips, axis=0)
    features = jnp.dot(mixed, proj_ref[...], preferred_element_type=F32)
    center = jnp.mean(features, axis=-1, keepdims=True)
    spread = jnp.mean((features - center) ** 2, axis=-1, keepdims=True)
    normal = (features - center) / jnp.sqrt(spread + EPSILON) * gain_ref[...]
    out_ref[...] = gelu(normal).astype(BF16)


def head_kernel(
    info, low_ref, mid_ref, high_ref, weight_ref, bias_ref, class_ref, class_bias_ref, labels_ref,
    logits_ref, losses_ref, sum_ref,
):
    place = info[1]
    strip = 2
    act = jnp.concatenate([low_ref[...], mid_ref[...], high_ref[...]], axis=0)
    count = (strip + 2) * COLS
    stacked = jnp.concatenate([act[r * COLS : r * COLS + count] for r in range(3)], axis=1)
    products = []
    for s in range(3):
        weight = jnp.concatenate([weight_ref[3 * r + s] for r in range(3)], axis=0)
        products.append(jnp.dot(stacked, weight, preferred_element_type=F32))
    position = lax.broadcasted_iota(jnp.int32, (count, CHANNELS), 0)
    col = position % COLS
    total = products[1]
    total = total + jnp.where(col == 0, 0.0, pltpu.roll(products[0], 1, 0))
    total = total + jnp.where(col == COLS - 1, 0.0, pltpu.roll(products[2], count - 1, 0))
    hidden = gelu(total + bias_ref[...])
    grid_row = place * strip - 1 + position // COLS
    inside = (grid_row >= 0) & (grid_row < strip * SEQ)
    hidden = jnp.where(inside, hidden, 0.0).astype(BF16)

    taps = lax.dot_general(
        class_ref[...], hidden, (((1,), (1,)), ((), ())), preferred_element_type=F32
    )

    def tap(r, s, row):
        start = (3 * r + s) * CLASSES
        return taps[start : start + CLASSES, row * COLS : (row + 1) * COLS]

    sides = []
    for s in range(3):
        combos = []
        for row in (1, 2):
            t = [tap(r, s, row) for r in range(3)]
            combos.append(tap(0, s, row - 1) + t[1] + t[2])
            combos.append(t[0] + t[1] + t[2])
            combos.append(t[0] + t[1] + tap(2, s, row + 1))
        sides.append(jnp.concatenate(combos, axis=0))
    pixels = UPSCALE * COLS
    source = lax.broadcasted_iota(jnp.int32, (COLS, pixels), 0)
    target = lax.broadcasted_iota(jnp.int32, (COLS, pixels), 1)
    spread_sum = None
    for s, side in enumerate(sides):
        first = UPSCALE * source - s + 1
        expand = jnp.where((target >= first) & (target < first + UPSCALE), 1.0, 0.0).astype(BF16)
        for _ in range(3):
            part = side.astype(BF16)
            side = side - part.astype(F32)
            term = jnp.dot(part, expand, preferred_element_type=F32)
            spread_sum = term if spread_sum is None else spread_sum + term
    class_ids = lax.broadcasted_iota(jnp.int32, (CLASSES, pixels), 0)
    loss_sum = jnp.zeros((1, pixels), F32)
    for y in range(UPSCALE * strip):
        combo = 3 * (y // UPSCALE) + (0, 1, 1, 2)[y % UPSCALE]
        logits = spread_sum[combo * CLASSES : (combo + 1) * CLASSES] + class_bias_ref[...]
        logits_ref[:, y, :] = logits
        highest = jnp.max(logits, axis=0, keepdims=True)
        log_total = highest + jnp.log(jnp.sum(jnp.exp(logits - highest), axis=0, keepdims=True))
        chosen = class_ids == labels_ref[y : y + 1, :]
        picked = jnp.sum(jnp.where(chosen, logits, 0.0), axis=0, keepdims=True)
        loss = log_total - picked
        losses_ref[y : y + 1, :] = loss
        loss_sum = loss_sum + loss
    total_loss = jnp.sum(loss_sum, axis=1, keepdims=True)
    sum_ref[...] = jnp.broadcast_to(total_loss[None], sum_ref.shape)


def body(
    mesh_shape, queries, keys, values, proj_weight, norm_gain, conv_weight, conv_bias, class_weight,
    class_bias, labels,
):
    place = lax.axis_index(("y", "z"))
    core = lax.rem(lax.axis_index("crop"), 2)
    info = jnp.stack([core, place]).astype(jnp.int32)
    cosine, sine = rotary_tables()
    crops = mesh_shape["crop"]
    seq = ("y", "z")

    swaps = []
    for crop in range(crops):
        for y in range(YS):
            slot = (y - crop % 2) % YS
            swaps.append((crop * YS + y, crop * YS + ((slot ^ 1) + crop % 2) % YS))

    send = pack(info, queries, keys, values, cosine, sine).reshape(SEQ, 3 * COLS, HEAD_DIM)
    mine = lax.all_to_all(send, seq, 0, 0, tiled=True)
    attended = attend(mine, lambda x: lax.ppermute(x, ("crop", "y"), swaps))
    returned = lax.all_to_all(attended, seq, 0, 0, tiled=True)

    strip_tokens = queries.shape[0]
    act = pl.pallas_call(
        features_kernel,
        in_specs=[SMEM] + [VMEM] * 3,
        out_specs=VMEM,
        out_shape=jax.ShapeDtypeStruct((strip_tokens, CHANNELS), BF16),
        name="features",
    )(info, returned, proj_weight, norm_gain.reshape(1, CHANNELS))
    low = lax.ppermute(act, seq, [(i, i + 1) for i in range(SEQ - 1)])
    high = lax.ppermute(act, seq, [(i + 1, i) for i in range(SEQ - 1)])
    rows, pixels = labels.shape
    logits, losses, sums = pl.pallas_call(
        head_kernel,
        in_specs=[SMEM] + [VMEM] * 8,
        out_specs=[VMEM] * 3,
        out_shape=[
            jax.ShapeDtypeStruct((CLASSES, rows, pixels), F32),
            jax.ShapeDtypeStruct((rows, pixels), F32),
            jax.ShapeDtypeStruct((SEQ, 1, HEAD_DIM), F32),
        ],
        name="head",
    )(
        info, low, act, high, conv_weight, conv_bias.reshape(1, CHANNELS),
        class_weight.reshape(9 * CLASSES, CHANNELS), class_bias.reshape(CLASSES, 1), labels,
    )
    everyone = lax.all_to_all(sums, seq, 0, 0, tiled=True)
    loss = (jnp.sum(everyone[:, 0, 0]) / (rows * pixels * SEQ)).reshape(1)
    return logits, losses, loss


def solution(mesh):
    crops = mesh.shape["crop"]
    split = Mesh(mesh.devices.reshape(crops, YS, ZS), ("crop", "y", "z"))
    rows = P(("crop", "y", "z"), None)
    in_specs = (rows, rows, rows, P(), P(), P(), P(), P(), P(), rows)
    out_specs = (P(None, ("crop", "y", "z"), None), rows, P("crop"))
    return jax.shard_map(
        functools.partial(body, dict(split.shape)),
        mesh=split,
        in_specs=in_specs,
        out_specs=out_specs,
        check_vma=False,
    )
```

time: 254 us -> 215 us (0.85)
  blocking collectives: 66.5 us -> 155 us
  waiting for transfers between devices: 77.4 us -> 5.46 us
  Pallas kernels: 0 us -> 42 us
  starting transfers between devices: 38.1 us -> 6.83 us
  matrix products: 29.6 us -> 0 us
  local copies, waits for them, and re-layouts: 19.7 us -> 1.39 us
  other arithmetic: 18.5 us -> 1.24 us
    all_to_all x1 -> x3, blocking collectives: 66.5 us -> 155 us  [the longest x1 89.1 us: body(): mine = lax.all_to_all(send, seq, 0, 0, tiled=True)]
    all_to_all x3 -> x0, waiting for transfers between devices: 51.7 us -> none  [the longest x1 27.3 us: body(): lax.all_to_all(outgoing, 'seq', split_axis=0, concat_axis=0, tiled=True)]
    pallas_call x0 -> x5, Pallas kernels: none -> 42 us  [the longest x1 15.8 us: attend(): pl.pallas_call(other_kernel, in_specs=[VMEM] * 4, out_specs=VMEM, out_sha...]
    all_to_all x3 -> x0, starting transfers between devices: 29.6 us -> none  [the longest x1 17.5 us: from_everyone(): lax.all_to_all(jnp.broadcast_to(shard[None], (devices, *shard.shape)), ax...]
    dot_general x27 -> x0, matrix products: 29.6 us -> none  [the longest x4 12.5 us: one_block(): jnp.einsum('hqk,khd->qhd', weights, values, preferred_element_type=jnp.fl...]
    ppermute x3, waiting for transfers between devices: 25.7 us -> 5.46 us  [the longest x1 4.87 us: body(): high = lax.ppermute(act, seq, [(i + 1, i) for i in range(SEQ - 1)])]
    slice x8 -> x1, local copies, waits for them, and re-layouts: 8.87 us -> 0.08 us  [attend(): other = swap(mine[:, COLS:, :])]
    reduce_sum x8 -> x1, other arithmetic: 7.57 us -> 0.63 us  [body(): loss = (jnp.sum(everyone[:, 0, 0]) / (rows * pixels * SEQ)).reshape(1)]
  transfers between devices with their start and end apart: 6 -> 3, of which waited for: 6 -> 3; matrix products, arithmetic and copies ran while one was open for 2% -> 0% of each run, Pallas kernels for 0% -> 6%
where the time goes in v1:
time: 215 us; the launch traced here: 214 us
  blocking collectives  155 us (72%)
  Pallas kernels  42 us (20%)
  starting transfers between devices  6.83 us (3%)
  waiting for transfers between devices  5.46 us (3%)
  between operations  2.47 us (1%)
    all_to_all x1, blocking collectives, body(): mine = lax.all_to_all(send, seq, 0, 0, tiled=True)  89.1 us
    all_to_all x1, blocking collectives, body(): returned = lax.all_to_all(attended, seq, 0, 0, tiled=True)  36.1 us
    all_to_all x1, blocking collectives, body(): everyone = lax.all_to_all(sums, seq, 0, 0, tiled=True)  29.7 us
    pallas_call x1, Pallas kernels, attend(): pl.pallas_call(other_kernel, in_specs=[VMEM] * 4, out_specs=VMEM, out_sha...  15.8 us
    pallas_call x1, Pallas kernels, attend(): pl.pallas_call(own_kernel, in_specs=[VMEM], out_specs=[VMEM, VMEM], out_s...  13.8 us
    pallas_call x1, Pallas kernels, pack(): pl.pallas_call(pack_kernel, grid_spec=pltpu.PrefetchScalarGridSpec(num_sc...  6.47 us
    ppermute x1, waiting for transfers between devices, body(): high = lax.ppermute(act, seq, [(i + 1, i) for i in range(SEQ - 1)])  4.87 us
  transfers between devices with their start and end apart: 3, of which 3 were waited for; matrix products, arithmetic and copies ran while one was open for 0% of the time, Pallas kernels for 6%

profile of v1, /device:TPU:6, one launch (start us, length us, event | category | flops | bytes accessed | tf_op | source)
XLA Modules:
  0.0 214.3 jit_solution(16356462570124118039)
XLA Ops:
  0.6 0.6 pad_add_fusion.info
  1.2 6.5 %pack.1 = bf16[4,8,192,128]{3,2,1,0:T(8,128)(2,1)} custom-call(s32[2]{0:T(128)} %pad_add_fusion.info, bf16[128,2048]{1,0:T(8,128)(2,1)} %q_ref.1, bf16[128,2048]{1,0:T(8,128)(2,1)} %k_ref.1, bf16[128,2048]{1,0:T(8,128)(2,1)} %v_ref.1, f32[64,128]{1,0:T(8,128)} %constant.30.clone.cos_ref, f32[64,128]{1,0:T(8,128)} %constant.31.clone.sin_ref), custom_call_target="tpu_custom_call" | custom-call | tf_op jit(solution)/shard_map/pack/pallas_call | solution.py:74
  7.7 89.1 %all_to_all.15.mine_ref = bf16[32,192,128]{2,1,0:T(8,128)(2,1)S(1)} all-to-all(bf16[32,192,128]{2,1,0:T(8,128)(2,1)} %bitcast.8), channel_id=1, replica_groups=mesh['crop'=16,'y'=4,'z'=8] {'y','z'}, dimensions={0} | all-to-all | bytes 3145728 | tf_op jit(solution)/shard_map/all_to_all | solution.py:268
  96.9 0.0 copy-start
  96.9 0.1 slice.8
  97.0 2.6 %collective-permute-start = (bf16[32,128,128]{2,1,0:T(8,128)(2,1)S(1)}, bf16[32,128,128]{2,1,0:T(8,128)(2,1)}, u32[]{:S(2)}, u32[]{:S(2)}) collective-permute-start(bf16[32,128,128]{2,1,0:T(8,128)(2,1)S(1)} %slice.8), channel_id=1, source_target_pairs={{0,8},{8,0},{16,24},{24,16},{32,56},{40,48},{48,40},{56,32},{64,72... | collective-permute-start | bytes 3145736 | tf_op jit(solution)/shard_map/ppermute | solution.py:269
  99.5 0.0 copy-done
  99.5 13.8 %own_keys.1 = (f32[2048,256]{1,0:T(8,128)}, f32[2048,128]{1,0:T(8,128)}) custom-call(bf16[32,192,128]{2,1,0:T(8,128)(2,1)} %copy-done), custom_call_target="tpu_custom_call" | custom-call | flops 3221225472 | bytes 4194304 | tf_op jit(solution)/shard_map/own_keys/pallas_call | solution.py:143
  113.4 0.4 collective-permute-done.other_ref
  113.8 15.8 %other_keys.1 = bf16[32,64,128]{2,1,0:T(8,128)(2,1)} custom-call(bf16[32,192,128]{2,1,0:T(8,128)(2,1)} %copy-done, bf16[32,128,128]{2,1,0:T(8,128)(2,1)} %collective-permute-done.other_ref, f32[2048,256]{1,0:T(8,128)} %get-tuple-element.8.acc_ref, f32[2048,128]{1,0:T(8,128)} %get-tuple-element.9.top_ref), custom_call_target="tpu_custom_call" | custom-call | flops 3221225472 | bytes 4194304 | tf_op jit(solution)/shard_map/other_keys/pallas_call | solution.py:154
  129.6 0.0 copy-start.3
  129.6 36.1 %all_to_all.16.mixed_ref = bf16[32,64,128]{2,1,0:T(8,128)(2,1)} all-to-all(bf16[32,64,128]{2,1,0:T(8,128)(2,1)} %other_keys.1), channel_id=1, replica_groups=mesh['crop'=16,'y'=4,'z'=8] {'y','z'}, dimensions={0} | all-to-all | bytes 1048576 | tf_op jit(solution)/shard_map/all_to_all | solution.py:270
  165.7 2.5 %features.1.mid_ref = bf16[128,256]{1,0:T(8,128)(2,1)} custom-call(s32[2]{0:T(128)} %pad_add_fusion.info, bf16[32,64,128]{2,1,0:T(8,128)(2,1)} %all_to_all.16.mixed_ref, bf16[2048,256]{1,0:T(8,128)(2,1)} %proj_ref.1, f32[1,256]{1,0:T(1,128)} %bitcast.11), custom_call_target="tpu_custom_call" | custom-call | tf_op jit(solution)/shard_map/features/pallas_call | solution.py:273
  168.2 3.0 %collective-permute-start.1 = (bf16[128,256]{1,0:T(8,128)(2,1)}, bf16[128,256]{1,0:T(8,128)(2,1)S(1)}, u32[]{:S(2)}, u32[]{:S(2)}) collective-permute-start(bf16[128,256]{1,0:T(8,128)(2,1)} %features.1.mid_ref), channel_id=1, source_target_pairs={{0,1},{1,2},{2,3},{3,4},{4,5},{5,6},{6,7},{7,8},{8,9},{9,10},{10,1... | collective-permute-start | bytes 196616 | tf_op jit(solution)/shard_map/ppermute | solution.py:280
  171.2 1.3 collective-permute-start.2
  172.5 0.0 copy-done.3
  172.5 0.7 copy.15.class_bias_ref
  173.2 0.2 collective-permute-done.1.low_ref
  173.4 4.9 %collective-permute-done.2.high_ref = bf16[128,256]{1,0:T(8,128)(2,1)S(1)} collective-permute-done((bf16[128,256]{1,0:T(8,128)(2,1)}, bf16[128,256]{1,0:T(8,128)(2,1)S(1)}, u32[]{:S(2)}, u32[]{:S(2)}) %collective-permute-start.2) | collective-permute-done | bytes 65568 | tf_op jit(solution)/shard_map/ppermute | solution.py:281
  178.3 0.0 copy-done.1
  178.3 0.6 copy-done.2
  178.9 3.4 %head.1 = (f32[16,8,256]{2,1,0:T(8,128)}, f32[8,256]{1,0:T(8,128)}, f32[32,1,128]{2,1,0:T(1,128)}) custom-call(s32[2]{0:T(128)} %pad_add_fusion.info, bf16[128,256]{1,0:T(8,128)(2,1)} %copy-done.1, bf16[128,256]{1,0:T(8,128)(2,1)} %features.1.mid_ref, bf16[128,256]{1,0:T(8,128)(2,1)} %copy-done.2, bf16[9,256,256]{2,1,0:T(8,128)(2,1)} %weight_ref.1, ...), custom_call_target="tpu_custom_call" | custom-call | tf_op jit(solution)/shard_map/head/pallas_call | solution.py:283
  182.3 29.7 %all_to_all.17 = f32[32,1,128]{2,1,0:T(1,128)S(1)} all-to-all(f32[32,1,128]{2,1,0:T(1,128)} %get-tuple-element.12), channel_id=1, replica_groups=mesh['crop'=16,'y'=4,'z'=8] {'y','z'}, dimensions={0} | all-to-all | bytes 32768 | tf_op jit(solution)/shard_map/all_to_all | solution.py:297
  211.9 0.6 slice_reduce_fusion
  (2 shorter events, 0.0 us)
Async XLA Ops:
  96.9 2.7 %copy-start = (bf16[32,192,128]{2,1,0:T(8,128)(2,1)}, bf16[32,192,128]{2,1,0:T(8,128)(2,1)S(1)}, u32[]{:S(2)}) copy-start(bf16[32,192,128]{2,1,0:T(8,128)(2,1)S(1)} %all_to_all.15.mine_ref) | copy-start | bytes 4718596
  97.0 16.8 %collective-permute-start = (bf16[32,128,128]{2,1,0:T(8,128)(2,1)S(1)}, bf16[32,128,128]{2,1,0:T(8,128)(2,1)}, u32[]{:S(2)}, u32[]{:S(2)}) collective-permute-start(bf16[32,128,128]{2,1,0:T(8,128)(2,1)S(1)} %slice.8), channel_id=1, source_target_pairs={{0,8},{8,0},{16,24},{24,16},{32,56},{40,48},{48,40},{56,32},{64,72... | collective-permute-start | bytes 3145736 | tf_op jit(solution)/shard_map/ppermute | solution.py:269
  129.6 42.9 %copy-start.3 = (f32[16]{0:T(128)S(1)}, f32[16]{0:T(128)}, u32[]{:S(2)}) copy-start(f32[16]{0:T(128)} %param.20) | copy-start | bytes 196
  168.2 5.2 %collective-permute-start.1 = (bf16[128,256]{1,0:T(8,128)(2,1)}, bf16[128,256]{1,0:T(8,128)(2,1)S(1)}, u32[]{:S(2)}, u32[]{:S(2)}) collective-permute-start(bf16[128,256]{1,0:T(8,128)(2,1)} %features.1.mid_ref), channel_id=1, source_target_pairs={{0,1},{1,2},{2,3},{3,4},{4,5},{5,6},{6,7},{7,8},{8,9},{9,10},{10,1... | collective-permute-start | bytes 196616 | tf_op jit(solution)/shard_map/ppermute | solution.py:280
  171.2 7.1 %collective-permute-start.2 = (bf16[128,256]{1,0:T(8,128)(2,1)}, bf16[128,256]{1,0:T(8,128)(2,1)S(1)}, u32[]{:S(2)}, u32[]{:S(2)}) collective-permute-start(bf16[128,256]{1,0:T(8,128)(2,1)} %features.1.mid_ref), channel_id=1, source_target_pairs={{1,0},{2,1},{3,2},{4,3},{5,4},{6,5},{7,6},{8,7},{9,8},{10,9},{11,1... | collective-permute-start | bytes 196616 | tf_op jit(solution)/shard_map/ppermute | solution.py:281
  173.4 4.9 %copy-start.1 = (bf16[128,256]{1,0:T(8,128)(2,1)}, bf16[128,256]{1,0:T(8,128)(2,1)S(1)}, u32[]{:S(2)}) copy-start(bf16[128,256]{1,0:T(8,128)(2,1)S(1)} %collective-permute-done.1.low_ref) | copy-start | bytes 196612
  178.3 0.6 copy-start.2

commit v2 on v1

--- a/solution.py
+++ b/solution.py
@@ -8,6 +8,7 @@
 from jax.experimental import pallas as pl
 from jax.experimental.pallas import tpu as pltpu
 from jax.sharding import Mesh, PartitionSpec as P
+
 
 HEADS = 16
 HEAD_DIM = 128
@@ -21,9 +22,12 @@
 EPSILON = 1e-05
 EXP_SCALE = HEAD_DIM**-0.5 * math.log2(math.e)
 VMEM = pl.BlockSpec(memory_space=pltpu.VMEM)
-SMEM = pl.BlockSpec(memory_space=pltpu.SMEM)
 BF16 = jnp.bfloat16
 F32 = jnp.float32
+
+
+def limit(mib):
+    return pltpu.CompilerParams(vmem_limit_bytes=mib << 20)
 
 
 def rotary_tables():
@@ -41,48 +45,55 @@
     return x * (0.5 * (1.0 + lax.erf(x * np.float32(math.sqrt(0.5)))))
 
 
-def pack_kernel(info, q_ref, k_ref, v_ref, cos_ref, sin_ref, out_ref):
-    core = info[0]
-    place = info[1]
+def positions():
+    place = lax.axis_index("y") * ZS + lax.axis_index("z")
+    return lax.rem(lax.axis_index("crop"), 2), place
+
+
+def pack_kernel(q_ref, k_ref, v_ref, cos_ref, sin_ref, out_ref):
+    core, place = positions()
     lane = lax.broadcasted_iota(jnp.int32, (COLS, HEAD_DIM), 1)
     by_row = lane < HEAD_DIM // 2
     first = (lane % (HEAD_DIM // 2)) < HEAD_DIM // 4
+    tables = []
     for half in range(2):
-        row_id = 2 * place + half
-        cosine = jnp.where(by_row, cos_ref[pl.ds(row_id, 1), :], cos_ref[...])
-        sine = jnp.where(by_row, sin_ref[pl.ds(row_id, 1), :], sin_ref[...])
-        rows = slice(half * COLS, (half + 1) * COLS)
+        row = pl.ds(2 * place + half, 1)
+        tables.append(
+            [jnp.where(by_row, ref[row, :], ref[...]) for ref in (cos_ref, sin_ref)]
+        )
+
+    def step(z, carry):
         for sub in range(2):
-            lanes = slice(sub * HEAD_DIM, (sub + 1) * HEAD_DIM)
-            y = lax.rem(2 * sub + half + core, YS)
-            for index, ref in ((0, q_ref), (1, k_ref)):
-                x = ref[rows, lanes].astype(F32)
-                partner = jnp.where(
-                    first,
-                    pltpu.roll(x, HEAD_DIM - HEAD_DIM // 4, 1),
-                    pltpu.roll(x, HEAD_DIM // 4, 1),
-                )
-                out_ref[y, 0, index * COLS : (index + 1) * COLS, :] = (
-                    x * cosine + partner * sine
-                ).astype(BF16)
-            out_ref[y, 0, 2 * COLS :, :] = v_ref[rows, lanes]
-
-
-def pack(info, queries, keys, values, cosine, sine):
-    tokens = queries.shape[0]
-    wide = 2 * HEAD_DIM
+            lanes = pl.ds(pl.multiple_of((2 * z + sub) * HEAD_DIM, HEAD_DIM), HEAD_DIM)
+            for half in range(2):
+                cosine, sine = tables[half]
+                rows = slice(half * COLS, (half + 1) * COLS)
+                y = lax.rem(2 * sub + half + core, YS)
+                for index, ref in ((0, q_ref), (1, k_ref)):
+                    x = ref[rows, lanes].astype(F32)
+                    partner = jnp.where(
+                        first,
+                        pltpu.roll(x, HEAD_DIM - HEAD_DIM // 4, 1),
+                        pltpu.roll(x, HEAD_DIM // 4, 1),
+                    )
+                    out_ref[y, z, index * COLS : (index + 1) * COLS, :] = (
+                        x * cosine + partner * sine
+                    ).astype(BF16)
+                out_ref[y, z, 2 * COLS :, :] = v_ref[rows, lanes]
+        return carry
+
+    lax.fori_loop(0, ZS, step, 0, unroll=2)
+
+
+def pack(queries, keys, values, cosine, sine):
     return pl.pallas_call(
         pack_kernel,
-        grid_spec=pltpu.PrefetchScalarGridSpec(
-            num_scalar_prefetch=1,
-            grid=(ZS,),
-            in_specs=[pl.BlockSpec((tokens, wide), lambda z, info: (0, z))] * 3
-            + [pl.BlockSpec((COLS, HEAD_DIM), lambda z, info: (0, 0))] * 2,
-            out_specs=pl.BlockSpec((YS, 1, 3 * COLS, HEAD_DIM), lambda z, info: (0, z, 0, 0)),
-        ),
+        in_specs=[VMEM] * 5,
+        out_specs=VMEM,
         out_shape=jax.ShapeDtypeStruct((YS, ZS, 3 * COLS, HEAD_DIM), BF16),
+        compiler_params=limit(8),
         name="pack",
-    )(info, queries, keys, values, cosine, sine)
+    )(queries, keys, values, cosine, sine)
 
 
 BLOCK = 4
@@ -94,6 +105,21 @@
 
 def with_ones(value):
     return jnp.concatenate([value, jnp.ones_like(value)], axis=1)
+
+
+CHUNK = 512
+
+
+def sweep(query, key_ref, value, top, total):
+    for start in range(0, SEQ * COLS, CHUNK):
+        scores = scores_of(query, key_ref[start : start + CHUNK])
+        before, top = top, jnp.max(scores, axis=1, keepdims=True)
+        if before is not None:
+            top = jnp.maximum(before, top)
+        weights = jnp.exp2((scores - top) * EXP_SCALE).astype(BF16)
+        part = jnp.dot(weights, value[start : start + CHUNK], preferred_element_type=F32)
+        total = part if before is None else total * jnp.exp2((before - top) * EXP_SCALE) + part
+    return top, total
 
 
 def own_kernel(mine_ref, acc_ref, top_ref):
@@ -103,15 +129,13 @@
 
     def step(i, carry):
         query = mine_ref[pl.ds(i * BLOCK, BLOCK), :COLS, :].reshape(rows, HEAD_DIM)
-        scores = scores_of(query, key)
-        top = jnp.max(scores, axis=1, keepdims=True)
-        weights = jnp.exp2((scores - top) * EXP_SCALE).astype(BF16)
+        top, total = sweep(query, key, value, None, None)
         out = pl.ds(pl.multiple_of(i * rows, rows), rows)
-        acc_ref[out, :] = jnp.dot(weights, value, preferred_element_type=F32)
+        acc_ref[out, :] = total
         top_ref[out, :] = jnp.broadcast_to(top, (rows, HEAD_DIM))
         return carry
 
-    lax.fori_loop(0, SEQ // BLOCK, step, 0)
+    lax.fori_loop(0, SEQ // BLOCK, step, 0, unroll=4)
 
 
 def other_kernel(mine_ref, other_ref, acc_ref, top_ref, out_ref):
@@ -121,18 +145,13 @@
 
     def step(i, carry):
         query = mine_ref[pl.ds(i * BLOCK, BLOCK), :COLS, :].reshape(rows, HEAD_DIM)
-        scores = scores_of(query, key)
         place = pl.ds(pl.multiple_of(i * rows, rows), rows)
-        before = top_ref[place, :1]
-        top = jnp.maximum(before, jnp.max(scores, axis=1, keepdims=True))
-        weights = jnp.exp2((scores - top) * EXP_SCALE).astype(BF16)
-        fade = jnp.exp2((before - top) * EXP_SCALE)
-        total = acc_ref[place, :] * fade + jnp.dot(weights, value, preferred_element_type=F32)
+        _, total = sweep(query, key, value, top_ref[place, :1], acc_ref[place, :])
         mixed = total[:, :HEAD_DIM] / total[:, HEAD_DIM:]
         out_ref[pl.ds(i * BLOCK, BLOCK), :, :] = mixed.astype(BF16).reshape(BLOCK, COLS, HEAD_DIM)
         return carry
 
-    lax.fori_loop(0, SEQ // BLOCK, step, 0)
+    lax.fori_loop(0, SEQ // BLOCK, step, 0, unroll=4)
 
 
 def attend(mine, swap):
@@ -149,6 +168,7 @@
             jax.ShapeDtypeStruct((tokens, HEAD_DIM), F32),
         ],
         cost_estimate=cost,
+        compiler_params=limit(28),
         name="own_keys",
     )(mine)
     return pl.pallas_call(
@@ -157,12 +177,13 @@
         out_specs=VMEM,
         out_shape=jax.ShapeDtypeStruct((SEQ, COLS, HEAD_DIM), BF16),
         cost_estimate=cost,
+        compiler_params=limit(28),
         name="other_keys",
     )(mine, other, acc, top)
 
 
-def features_kernel(info, mixed_ref, proj_ref, gain_ref, out_ref):
-    core = info[0]
+def features_kernel(mixed_ref, proj_ref, gain_ref, out_ref):
+    core, _ = positions()
     strips = []
     for half in range(2):
         pieces = []
@@ -179,12 +200,16 @@
 
 
 def head_kernel(
-    info, low_ref, mid_ref, high_ref, weight_ref, bias_ref, class_ref, class_bias_ref, labels_ref,
-    logits_ref, losses_ref, sum_ref,
+    pair_ref, mid_ref, far_ref, weight_ref, bias_ref, class_ref, class_bias_ref, labels_ref,
+    logits_ref, losses_ref, sum_ref, act,
 ):
-    place = info[1]
+    _, place = positions()
     strip = 2
-    act = jnp.concatenate([low_ref[...], mid_ref[...], high_ref[...]], axis=0)
+    odd = lax.rem(place, 2)
+    edge = 2 * strip * COLS
+    act[pl.ds(pl.multiple_of((1 - odd) * edge, strip * COLS), strip * COLS), :] = pair_ref[...]
+    act[strip * COLS : edge, :] = mid_ref[...]
+    act[pl.ds(pl.multiple_of(odd * edge, strip * COLS), strip * COLS), :] = far_ref[...]
     count = (strip + 2) * COLS
     stacked = jnp.concatenate([act[r * COLS : r * COLS + count] for r in range(3)], axis=1)
     products = []
@@ -251,9 +276,6 @@
     mesh_shape, queries, keys, values, proj_weight, norm_gain, conv_weight, conv_bias, class_weight,
     class_bias, labels,
 ):
-    place = lax.axis_index(("y", "z"))
-    core = lax.rem(lax.axis_index("crop"), 2)
-    info = jnp.stack([core, place]).astype(jnp.int32)
     cosine, sine = rotary_tables()
     crops = mesh_shape["crop"]
     seq = ("y", "z")
@@ -264,7 +286,7 @@
             slot = (y - crop % 2) % YS
             swaps.append((crop * YS + y, crop * YS + ((slot ^ 1) + crop % 2) % YS))
 
-    send = pack(info, queries, keys, values, cosine, sine).reshape(SEQ, 3 * COLS, HEAD_DIM)
+    send = pack(queries, keys, values, cosine, sine).reshape(SEQ, 3 * COLS, HEAD_DIM)
     mine = lax.all_to_all(send, seq, 0, 0, tiled=True)
     attended = attend(mine, lambda x: lax.ppermute(x, ("crop", "y"), swaps))
     returned = lax.all_to_all(attended, seq, 0, 0, tiled=True)
@@ -272,26 +294,29 @@
     strip_tokens = queries.shape[0]
     act = pl.pallas_call(
         features_kernel,
-        in_specs=[SMEM] + [VMEM] * 3,
+        in_specs=[VMEM] * 3,
         out_specs=VMEM,
         out_shape=jax.ShapeDtypeStruct((strip_tokens, CHANNELS), BF16),
+        compiler_params=limit(12),
         name="features",
-    )(info, returned, proj_weight, norm_gain.reshape(1, CHANNELS))
-    low = lax.ppermute(act, seq, [(i, i + 1) for i in range(SEQ - 1)])
-    high = lax.ppermute(act, seq, [(i + 1, i) for i in range(SEQ - 1)])
+    )(returned, proj_weight, norm_gain.reshape(1, CHANNELS))
+    far = lax.ppermute(act, seq, [(i, ((i + 1) ^ 1) - 1) for i in range(1, SEQ - 1)])
+    pair = lax.ppermute(act, seq, [(i, i ^ 1) for i in range(SEQ)])
     rows, pixels = labels.shape
     logits, losses, sums = pl.pallas_call(
         head_kernel,
-        in_specs=[SMEM] + [VMEM] * 8,
+        in_specs=[VMEM] * 8,
         out_specs=[VMEM] * 3,
         out_shape=[
             jax.ShapeDtypeStruct((CLASSES, rows, pixels), F32),
             jax.ShapeDtypeStruct((rows, pixels), F32),
             jax.ShapeDtypeStruct((SEQ, 1, HEAD_DIM), F32),
         ],
+        scratch_shapes=[pltpu.VMEM((3 * strip_tokens, CHANNELS), BF16)],
+        compiler_params=limit(12),
         name="head",
     )(
-        info, low, act, high, conv_weight, conv_bias.reshape(1, CHANNELS),
+        pair, act, far, conv_weight, conv_bias.reshape(1, CHANNELS),
         class_weight.reshape(9 * CLASSES, CHANNELS), class_bias.reshape(CLASSES, 1), labels,
     )
     everyone = lax.all_to_all(sums, seq, 0, 0, tiled=True)

time: 215 us -> 196 us (0.912)
  Pallas kernels: 42 us -> 17.4 us
  waiting for transfers between devices: 5.46 us -> 11 us
  local copies, waits for them, and re-layouts: 1.39 us -> 4.84 us
  blocking collectives: 155 us -> 152 us
    pallas_call x3, Pallas kernels: 12.3 us -> 3.46 us  [the longest x1 2.01 us: body(): pl.pallas_call(head_kernel, in_specs=[VMEM] * 8, out_specs=[VMEM] * 3, ou...]
    pallas_call x1, Pallas kernels: 13.8 us -> 5.53 us  [attend(): pl.pallas_call(own_kernel, in_specs=[VMEM], out_specs=[VMEM, VMEM], out_s...]
    ppermute x1, waiting for transfers between devices: 0.38 us -> 8.58 us  [body(): attended = attend(mine, lambda x: lax.ppermute(x, ('crop', 'y'), swaps))]
    pallas_call x1, Pallas kernels: 15.8 us -> 8.43 us  [attend(): pl.pallas_call(other_kernel, in_specs=[VMEM] * 4, out_specs=VMEM, out_sha...]
    unnamed x8 -> x24, local copies, waits for them, and re-layouts: 0.63 us -> 4.67 us
    ppermute x2, waiting for transfers between devices: 5.08 us -> 2.4 us  [the longest x1 2.4 us: body(): pair = lax.ppermute(act, seq, [(i, i ^ 1) for i in range(SEQ)])]
  transfers between devices with their start and end apart: 3 -> 3, of which waited for: 3 -> 2; matrix products, arithmetic and copies ran while one was open for 0% -> 0% of each run, Pallas kernels for 6% -> 3%
where the time goes in v2:
time: 196 us; the launch traced here: 195 us
  blocking collectives  152 us (78%)
  Pallas kernels  17.4 us (9%)
  waiting for transfers between devices  11 us (6%)
  starting transfers between devices  6.22 us (3%)
  local copies, waits for them, and re-layouts  4.84 us (2%)
  between operations  2.56 us (1%)
    all_to_all x1, blocking collectives, body(): mine = lax.all_to_all(send, seq, 0, 0, tiled=True)  88.9 us
    all_to_all x1, blocking collectives, body(): returned = lax.all_to_all(attended, seq, 0, 0, tiled=True)  35.5 us
    all_to_all x1, blocking collectives, body(): everyone = lax.all_to_all(sums, seq, 0, 0, tiled=True)  27.9 us
    ppermute x1, waiting for transfers between devices, body(): attended = attend(mine, lambda x: lax.ppermute(x, ('crop', 'y'), swaps))  8.58 us
    pallas_call x1, Pallas kernels, attend(): pl.pallas_call(other_kernel, in_specs=[VMEM] * 4, out_specs=VMEM, out_sha...  8.43 us
    pallas_call x1, Pallas kernels, attend(): pl.pallas_call(own_kernel, in_specs=[VMEM], out_specs=[VMEM, VMEM], out_s...  5.53 us
    unnamed x24, local copies, waits for them, and re-layouts  4.67 us
  transfers between devices with their start and end apart: 3, of which 2 were waited for; matrix products, arithmetic and copies ran while one was open for 0% of the time, Pallas kernels for 3%

profile of v2, /device:TPU:6, one launch (start us, length us, event | category | flops | bytes accessed | tf_op | source)
XLA Modules:
  0.0 194.9 jit_solution(12514447412031408389)
XLA Ops:
  0.6 1.0 copy-done.2
  1.7 1.0 copy-done.3
  2.7 1.0 copy-done.4
  3.8 0.8 copy-done.6
  4.5 0.8 copy-done.7
  5.3 0.9 pack.1
  6.2 88.9 %all_to_all.15.mine_ref = bf16[32,192,128]{2,1,0:T(8,128)(2,1)S(1)} all-to-all(bf16[32,192,128]{2,1,0:T(8,128)(2,1)S(1)} %bitcast.6), channel_id=1, replica_groups=mesh['crop'=16,'y'=4,'z'=8] {'y','z'}, dimensions={0} | all-to-all | bytes 3145728 | tf_op jit(solution)/shard_map/all_to_all | solution.py:290
  95.2 0.1 slice.8
  95.3 2.6 %collective-permute-start = (bf16[32,128,128]{2,1,0:T(8,128)(2,1)S(1)}, bf16[32,128,128]{2,1,0:T(8,128)(2,1)S(1)}, u32[]{:S(2)}, u32[]{:S(2)}) collective-permute-start(bf16[32,128,128]{2,1,0:T(8,128)(2,1)S(1)} %slice.8), channel_id=1, source_target_pairs={{0,8},{8,0},{16,24},{24,16},{32,56},{40,48},{48,40},{56,32},{64,72... | collective-permute-start | bytes 3145736 | tf_op jit(solution)/shard_map/ppermute | solution.py:291
  97.8 5.5 %own_keys.1 = (f32[2048,256]{1,0:T(8,128)S(1)}, f32[2048,128]{1,0:T(8,128)S(1)}) custom-call(bf16[32,192,128]{2,1,0:T(8,128)(2,1)S(1)} %all_to_all.15.mine_ref), custom_call_target="tpu_custom_call" | custom-call | flops 3221225472 | bytes 4194304 | tf_op jit(solution)/shard_map/own_keys/pallas_call | solution.py:162
  103.4 8.6 %collective-permute-done.other_ref = bf16[32,128,128]{2,1,0:T(8,128)(2,1)S(1)} collective-permute-done((bf16[32,128,128]{2,1,0:T(8,128)(2,1)S(1)}, bf16[32,128,128]{2,1,0:T(8,128)(2,1)S(1)}, u32[]{:S(2)}, u32[]{:S(2)}) %collective-permute-start) | collective-permute-done | bytes 1048608 | tf_op jit(solution)/shard_map/ppermute | solution.py:291
  112.0 8.4 %other_keys.1 = bf16[32,64,128]{2,1,0:T(8,128)(2,1)S(1)} custom-call(bf16[32,192,128]{2,1,0:T(8,128)(2,1)S(1)} %all_to_all.15.mine_ref, bf16[32,128,128]{2,1,0:T(8,128)(2,1)S(1)} %collective-permute-done.other_ref, f32[2048,256]{1,0:T(8,128)S(1)} %get-tuple-element.8.acc_ref, f32[2048,128]{1,0:T(8,128)S(1)} %get-tuple-element.9.top_ref), custom_call_target="tpu_custom_call" | custom-call | flops 3221225472 | bytes 4194304 | tf_op jit(solution)/shard_map/other_keys/pallas_call | solution.py:174
  120.4 0.0 copy-start.11
  120.4 0.0 copy-start
  120.4 0.0 copy-start.5
  120.5 35.5 %all_to_all.16.mixed_ref = bf16[32,64,128]{2,1,0:T(8,128)(2,1)S(1)} all-to-all(bf16[32,64,128]{2,1,0:T(8,128)(2,1)S(1)} %other_keys.1), channel_id=1, replica_groups=mesh['crop'=16,'y'=4,'z'=8] {'y','z'}, dimensions={0} | all-to-all | bytes 1048576 | tf_op jit(solution)/shard_map/all_to_all | solution.py:292
  155.9 0.5 features.1.mid_ref
  156.4 3.0 %collective-permute-start.1 = (bf16[128,256]{1,0:T(8,128)(2,1)S(1)}, bf16[128,256]{1,0:T(8,128)(2,1)S(1)}, u32[]{:S(2)}, u32[]{:S(2)}) collective-permute-start(bf16[128,256]{1,0:T(8,128)(2,1)S(1)} %features.1.mid_ref), channel_id=1, source_target_pairs={{0,1},{1,0},{2,3},{3,2},{4,5},{5,4},{6,7},{7,6},{8,9},{9,8},{10,11... | collective-permute-start | bytes 196616 | tf_op jit(solution)/shard_map/ppermute | solution.py:304
  159.4 0.7 collective-permute-start.2
  160.1 0.1 copy.15.class_bias_ref
  160.2 2.4 %collective-permute-done.1.pair_ref = bf16[128,256]{1,0:T(8,128)(2,1)S(1)} collective-permute-done((bf16[128,256]{1,0:T(8,128)(2,1)S(1)}, bf16[128,256]{1,0:T(8,128)(2,1)S(1)}, u32[]{:S(2)}, u32[]{:S(2)}) %collective-permute-start.1) | collective-permute-done | bytes 65568 | tf_op jit(solution)/shard_map/ppermute | solution.py:304
  162.6 2.0 %head.1 = (f32[16,8,256]{2,1,0:T(8,128)}, f32[8,256]{1,0:T(8,128)}, f32[32,1,128]{2,1,0:T(1,128)S(1)}) custom-call(bf16[128,256]{1,0:T(8,128)(2,1)S(1)} %collective-permute-done.1.pair_ref, bf16[128,256]{1,0:T(8,128)(2,1)S(1)} %features.1.mid_ref, bf16[128,256]{1,0:T(8,128)(2,1)S(1)} %collective-permute-done.2.far_ref, bf16[9,256,256]{2,1,0:T(8,128)(2,1)S(1)} %copy-done, ...), custom_call_target="tpu_custom_call" | custom-call | tf_op jit(solution)/shard_map/head/pallas_call | solution.py:306
  164.6 27.9 %all_to_all.17 = f32[32,1,128]{2,1,0:T(1,128)S(1)} all-to-all(f32[32,1,128]{2,1,0:T(1,128)S(1)} %get-tuple-element.12), channel_id=1, replica_groups=mesh['crop'=16,'y'=4,'z'=8] {'y','z'}, dimensions={0} | all-to-all | bytes 32768 | tf_op jit(solution)/shard_map/all_to_all | solution.py:322
  192.5 0.6 slice_reduce_fusion
  (17 shorter events, 0.0 us)
Async XLA Ops:
  0.6 1.0 copy-start.2
  1.7 1.0 copy-start.3
  2.7 1.0 copy-start.4
  3.8 0.8 copy-start.6
  4.5 0.8 copy-start.7
  95.3 16.7 %collective-permute-start = (bf16[32,128,128]{2,1,0:T(8,128)(2,1)S(1)}, bf16[32,128,128]{2,1,0:T(8,128)(2,1)S(1)}, u32[]{:S(2)}, u32[]{:S(2)}) collective-permute-start(bf16[32,128,128]{2,1,0:T(8,128)(2,1)S(1)} %slice.8), channel_id=1, source_target_pairs={{0,8},{8,0},{16,24},{24,16},{32,56},{40,48},{48,40},{56,32},{64,72... | collective-permute-start | bytes 3145736 | tf_op jit(solution)/shard_map/ppermute | solution.py:291
  112.0 44.0 %copy-start.1 = (bf16[2048,256]{1,0:T(8,128)(2,1)S(1)}, bf16[2048,256]{1,0:T(8,128)(2,1)}, u32[]{:S(2)}) copy-start(bf16[2048,256]{1,0:T(8,128)(2,1)} %proj_ref.1) | copy-start | bytes 3145732
  112.0 44.0 %copy-start.10 = (f32[256]{0:T(256)S(1)}, f32[256]{0:T(256)}, u32[]{:S(2)}) copy-start(f32[256]{0:T(256)} %param.16) | copy-start | bytes 3076
  120.4 39.7 %copy-start.11 = (f32[16]{0:T(128)S(1)}, f32[16]{0:T(128)}, u32[]{:S(2)}) copy-start(f32[16]{0:T(128)} %param.20) | copy-start | bytes 196
  120.4 42.2 %copy-start = (bf16[9,256,256]{2,1,0:T(8,128)(2,1)S(1)}, bf16[9,256,256]{2,1,0:T(8,128)(2,1)}, u32[]{:S(2)}) copy-start(bf16[9,256,256]{2,1,0:T(8,128)(2,1)} %weight_ref.1) | copy-start | bytes 3538948
  120.4 42.2 %copy-start.5 = (bf16[9,16,256]{2,1,0:T(8,128)(2,1)S(1)}, bf16[9,16,256]{2,1,0:T(8,128)(2,1)}, u32[]{:S(2)}) copy-start(bf16[9,16,256]{2,1,0:T(8,128)(2,1)} %param.19) | copy-start | bytes 221188
  120.4 42.2 %copy-start.8 = (s32[8,256]{1,0:T(8,128)S(1)}, s32[8,256]{1,0:T(8,128)}, u32[]{:S(2)}) copy-start(s32[8,256]{1,0:T(8,128)} %labels_ref.1) | copy-start | bytes 24580
  120.4 42.2 %copy-start.9 = (f32[256]{0:T(256)S(1)}, f32[256]{0:T(256)}, u32[]{:S(2)}) copy-start(f32[256]{0:T(256)} %param.18) | copy-start | bytes 3076
  156.4 6.2 %collective-permute-start.1 = (bf16[128,256]{1,0:T(8,128)(2,1)S(1)}, bf16[128,256]{1,0:T(8,128)(2,1)S(1)}, u32[]{:S(2)}, u32[]{:S(2)}) collective-permute-start(bf16[128,256]{1,0:T(8,128)(2,1)S(1)} %features.1.mid_ref), channel_id=1, source_target_pairs={{0,1},{1,0},{2,3},{3,2},{4,5},{5,4},{6,7},{7,6},{8,9},{9,8},{10,11... | collective-permute-start | bytes 196616 | tf_op jit(solution)/shard_map/ppermute | solution.py:304
  159.4 3.2 %collective-permute-start.2 = (bf16[128,256]{1,0:T(8,128)(2,1)S(1)}, bf16[128,256]{1,0:T(8,128)(2,1)S(1)}, u32[]{:S(2)}, u32[]{:S(2)}) collective-permute-start(bf16[128,256]{1,0:T(8,128)(2,1)S(1)} %features.1.mid_ref), channel_id=1, source_target_pairs={{1,2},{2,1},{3,4},{4,3},{5,6},{6,5},{7,8},{8,7},{9,10},{10,9},{11,... | collective-permute-start | bytes 196616 | tf_op jit(solution)/shard_map/ppermute | solution.py:303

commit v3 on v2

--- a/solution.py
+++ b/solution.py
@@ -50,27 +50,53 @@
     return lax.rem(lax.axis_index("crop"), 2), place
 
 
-def pack_kernel(q_ref, k_ref, v_ref, cos_ref, sin_ref, out_ref):
+PARTS = 4
+PART = HEADS * HEAD_DIM // PARTS
+
+
+def pack_kernel(q_hbm, k_hbm, v_hbm, cos_hbm, sin_hbm, out_ref, q_ref, k_ref, v_ref, cos_ref, sin_ref, sems, table_sems):
     core, place = positions()
+    tables_in = [
+        pltpu.make_async_copy(cos_hbm, cos_ref, table_sems.at[0]),
+        pltpu.make_async_copy(sin_hbm, sin_ref, table_sems.at[1]),
+    ]
+    for copy in tables_in:
+        copy.start()
+    copies = []
+    for part in range(PARTS):
+        lanes = pl.ds(part * PART, PART)
+        copies.append(
+            [
+                pltpu.make_async_copy(hbm.at[:, lanes], ref.at[part], sems.at[part, which])
+                for which, (hbm, ref) in enumerate(((q_hbm, q_ref), (k_hbm, k_ref), (v_hbm, v_ref)))
+            ]
+        )
+        for copy in copies[-1]:
+            copy.start()
     lane = lax.broadcasted_iota(jnp.int32, (COLS, HEAD_DIM), 1)
     by_row = lane < HEAD_DIM // 2
     first = (lane % (HEAD_DIM // 2)) < HEAD_DIM // 4
+    for copy in tables_in:
+        copy.wait()
     tables = []
     for half in range(2):
         row = pl.ds(2 * place + half, 1)
         tables.append(
             [jnp.where(by_row, ref[row, :], ref[...]) for ref in (cos_ref, sin_ref)]
         )
-
-    def step(z, carry):
-        for sub in range(2):
-            lanes = pl.ds(pl.multiple_of((2 * z + sub) * HEAD_DIM, HEAD_DIM), HEAD_DIM)
+    for part in range(PARTS):
+        for copy in copies[part]:
+            copy.wait()
+        for inner in range(HEADS // PARTS):
+            head = part * (HEADS // PARTS) + inner
+            z = head // 2
+            lanes = slice(inner * HEAD_DIM, (inner + 1) * HEAD_DIM)
             for half in range(2):
                 cosine, sine = tables[half]
                 rows = slice(half * COLS, (half + 1) * COLS)
-                y = lax.rem(2 * sub + half + core, YS)
+                y = lax.rem(2 * (head % 2) + half + core, YS)
                 for index, ref in ((0, q_ref), (1, k_ref)):
-                    x = ref[rows, lanes].astype(F32)
+                    x = ref[part, rows, lanes].astype(F32)
                     partner = jnp.where(
                         first,
                         pltpu.roll(x, HEAD_DIM - HEAD_DIM // 4, 1),
@@ -79,21 +105,22 @@
                     out_ref[y, z, index * COLS : (index + 1) * COLS, :] = (
                         x * cosine + partner * sine
                     ).astype(BF16)
-                out_ref[y, z, 2 * COLS :, :] = v_ref[rows, lanes]
-        return carry
-
-    lax.fori_loop(0, ZS, step, 0, unroll=2)
+                out_ref[y, z, 2 * COLS :, :] = v_ref[part, rows, lanes]
 
 
 def pack(queries, keys, values, cosine, sine):
+    tokens = queries.shape[0]
     return pl.pallas_call(
         pack_kernel,
-        in_specs=[VMEM] * 5,
+        in_specs=[pl.BlockSpec(memory_space=pltpu.HBM)] * 5,
         out_specs=VMEM,
         out_shape=jax.ShapeDtypeStruct((YS, ZS, 3 * COLS, HEAD_DIM), BF16),
+        scratch_shapes=[pltpu.VMEM((PARTS, tokens, PART), BF16)] * 3
+        + [pltpu.VMEM((COLS, HEAD_DIM), F32)] * 2
+        + [pltpu.SemaphoreType.DMA((PARTS, 3)), pltpu.SemaphoreType.DMA((2,))],
         compiler_params=limit(8),
         name="pack",
-    )(queries, keys, values, cosine, sine)
+    )(*(pltpu.with_memory_space_constraint(x, pltpu.HBM) for x in (queries, keys, values, cosine, sine)))
 
 
 BLOCK = 4
@@ -110,16 +137,17 @@
 CHUNK = 512
 
 
-def sweep(query, key_ref, value, top, total):
-    for start in range(0, SEQ * COLS, CHUNK):
-        scores = scores_of(query, key_ref[start : start + CHUNK])
+def sweep(query, key, value):
+    top = total = None
+    for start in range(0, key.shape[0], CHUNK):
+        scores = scores_of(query, key[start : start + CHUNK])
         before, top = top, jnp.max(scores, axis=1, keepdims=True)
         if before is not None:
             top = jnp.maximum(before, top)
         weights = jnp.exp2((scores - top) * EXP_SCALE).astype(BF16)
         part = jnp.dot(weights, value[start : start + CHUNK], preferred_element_type=F32)
         total = part if before is None else total * jnp.exp2((before - top) * EXP_SCALE) + part
-    return top, total
+    return jnp.broadcast_to(top, (query.shape[0], HEAD_DIM)), total
 
 
 def own_kernel(mine_ref, acc_ref, top_ref):
@@ -129,13 +157,11 @@
 
     def step(i, carry):
         query = mine_ref[pl.ds(i * BLOCK, BLOCK), :COLS, :].reshape(rows, HEAD_DIM)
-        top, total = sweep(query, key, value, None, None)
         out = pl.ds(pl.multiple_of(i * rows, rows), rows)
-        acc_ref[out, :] = total
-        top_ref[out, :] = jnp.broadcast_to(top, (rows, HEAD_DIM))
+        top_ref[out, :], acc_ref[out, :] = sweep(query, key, value)
         return carry
 
-    lax.fori_loop(0, SEQ // BLOCK, step, 0, unroll=4)
+    lax.fori_loop(0, SEQ // BLOCK, step, 0, unroll=SEQ // BLOCK)
 
 
 def other_kernel(mine_ref, other_ref, acc_ref, top_ref, out_ref):
@@ -146,12 +172,19 @@
     def step(i, carry):
         query = mine_ref[pl.ds(i * BLOCK, BLOCK), :COLS, :].reshape(rows, HEAD_DIM)
         place = pl.ds(pl.multiple_of(i * rows, rows), rows)
-        _, total = sweep(query, key, value, top_ref[place, :1], acc_ref[place, :])
-        mixed = total[:, :HEAD_DIM] / total[:, HEAD_DIM:]
-        out_ref[pl.ds(i * BLOCK, BLOCK), :, :] = mixed.astype(BF16).reshape(BLOCK, COLS, HEAD_DIM)
+        top_here, here = sweep(query, key, value)
+        top_there, there = top_ref[place, :], acc_ref[place, :]
+        top = jnp.maximum(top_here, top_there)
+        fade_here = jnp.exp2((top_here - top) * EXP_SCALE)
+        fade_there = jnp.exp2((top_there - top) * EXP_SCALE)
+        mixed = here[:, :HEAD_DIM] * fade_here + there[:, :HEAD_DIM] * fade_there
+        norm = here[:, HEAD_DIM:] * fade_here + there[:, HEAD_DIM:] * fade_there
+        out_ref[pl.ds(i * BLOCK, BLOCK), :, :] = (
+            (mixed / norm).astype(BF16).reshape(BLOCK, COLS, HEAD_DIM)
+        )
         return carry
 
-    lax.fori_loop(0, SEQ // BLOCK, step, 0, unroll=4)
+    lax.fori_loop(0, SEQ // BLOCK, step, 0, unroll=SEQ // BLOCK)
 
 
 def attend(mine, swap):

time: 196 us -> 189 us (0.964)
  local copies, waits for them, and re-layouts: 4.84 us -> 0.2 us
  Pallas kernels: 17.4 us -> 15.2 us
    unnamed x24 -> x14, local copies, waits for them, and re-layouts: 4.67 us -> 0.04 us
    pallas_call x1, Pallas kernels: 8.43 us -> 5.24 us  [attend(): pl.pallas_call(other_kernel, in_specs=[VMEM] * 4, out_specs=VMEM, out_sha...]
where the time goes in v3:
time: 189 us
  blocking collectives  152 us (80%)
  Pallas kernels  15.2 us (8%)
  waiting for transfers between devices  11.5 us (6%)
  starting transfers between devices  6.22 us (3%)
  between operations  2.54 us (1%)
    all_to_all x1, blocking collectives, body(): mine = lax.all_to_all(send, seq, 0, 0, tiled=True)  88.9 us
    all_to_all x1, blocking collectives, body(): returned = lax.all_to_all(attended, seq, 0, 0, tiled=True)  35.5 us
    all_to_all x1, blocking collectives, body(): everyone = lax.all_to_all(sums, seq, 0, 0, tiled=True)  27.9 us
    ppermute x1, waiting for transfers between devices, body(): attended = attend(mine, lambda x: lax.ppermute(x, ('crop', 'y'), swaps))  9.05 us
    pallas_call x1, Pallas kernels, attend(): pl.pallas_call(other_kernel, in_specs=[VMEM] * 4, out_specs=VMEM, out_sha...  5.24 us
    pallas_call x1, Pallas kernels, attend(): pl.pallas_call(own_kernel, in_specs=[VMEM], out_specs=[VMEM, VMEM], out_s...  5.06 us
  transfers between devices with their start and end apart: 3, of which 2 were waited for; matrix products, arithmetic and copies ran while one was open for 0% of the time, Pallas kernels for 3%

profile of v3, /device:TPU:6, one launch (start us, length us, event | category | flops | bytes accessed | tf_op | source)
XLA Modules:
  0.0 188.5 jit_solution(2505917726560155662)
XLA Ops:
  0.6 2.4 %pack.1 = bf16[4,8,192,128]{3,2,1,0:T(8,128)(2,1)S(1)} custom-call(bf16[128,2048]{1,0:T(8,128)(2,1)} %q_hbm.1, bf16[128,2048]{1,0:T(8,128)(2,1)} %k_hbm.1, bf16[128,2048]{1,0:T(8,128)(2,1)} %v_hbm.1, f32[64,128]{1,0:T(8,128)} %constant.9.clone.cos_hbm, f32[64,128]{1,0:T(8,128)} %constant.10.clone.sin_hbm), custom_call_target="tpu_custom_call" | custom-call | tf_op jit(solution)/shard_map/pack/pallas_call | solution.py:113
  3.0 88.9 %all_to_all.15.mine_ref = bf16[32,192,128]{2,1,0:T(8,128)(2,1)S(1)} all-to-all(bf16[32,192,128]{2,1,0:T(8,128)(2,1)S(1)} %bitcast.6), channel_id=1, replica_groups=mesh['crop'=16,'y'=4,'z'=8] {'y','z'}, dimensions={0} | all-to-all | bytes 3145728 | tf_op jit(solution)/shard_map/all_to_all | solution.py:323
  91.9 0.1 slice.8
  92.0 2.6 %collective-permute-start = (bf16[32,128,128]{2,1,0:T(8,128)(2,1)S(1)}, bf16[32,128,128]{2,1,0:T(8,128)(2,1)S(1)}, u32[]{:S(2)}, u32[]{:S(2)}) collective-permute-start(bf16[32,128,128]{2,1,0:T(8,128)(2,1)S(1)} %slice.8), channel_id=1, source_target_pairs={{0,8},{8,0},{16,24},{24,16},{32,56},{40,48},{48,40},{56,32},{64,72... | collective-permute-start | bytes 3145736 | tf_op jit(solution)/shard_map/ppermute | solution.py:324
  94.6 5.1 %own_keys.1 = (f32[2048,256]{1,0:T(8,128)S(1)}, f32[2048,128]{1,0:T(8,128)S(1)}) custom-call(bf16[32,192,128]{2,1,0:T(8,128)(2,1)S(1)} %all_to_all.15.mine_ref), custom_call_target="tpu_custom_call" | custom-call | flops 3221225472 | bytes 4194304 | tf_op jit(solution)/shard_map/own_keys/pallas_call | solution.py:195
  99.7 9.1 %collective-permute-done.other_ref = bf16[32,128,128]{2,1,0:T(8,128)(2,1)S(1)} collective-permute-done((bf16[32,128,128]{2,1,0:T(8,128)(2,1)S(1)}, bf16[32,128,128]{2,1,0:T(8,128)(2,1)S(1)}, u32[]{:S(2)}, u32[]{:S(2)}) %collective-permute-start) | collective-permute-done | bytes 1048608 | tf_op jit(solution)/shard_map/ppermute | solution.py:324
  108.7 5.2 %other_keys.1 = bf16[32,64,128]{2,1,0:T(8,128)(2,1)S(1)} custom-call(bf16[32,192,128]{2,1,0:T(8,128)(2,1)S(1)} %all_to_all.15.mine_ref, bf16[32,128,128]{2,1,0:T(8,128)(2,1)S(1)} %collective-permute-done.other_ref, f32[2048,256]{1,0:T(8,128)S(1)} %get-tuple-element.8.acc_ref, f32[2048,128]{1,0:T(8,128)S(1)} %get-tuple-element.9.top_ref), custom_call_target="tpu_custom_call" | custom-call | flops 3221225472 | bytes 4194304 | tf_op jit(solution)/shard_map/other_keys/pallas_call | solution.py:207
  114.0 0.0 copy-start.6
  114.0 0.0 copy-start
  114.0 0.0 copy-start.2
  114.0 0.0 copy-start.3
  114.0 0.0 copy-start.4
  114.0 35.5 %all_to_all.16.mixed_ref = bf16[32,64,128]{2,1,0:T(8,128)(2,1)S(1)} all-to-all(bf16[32,64,128]{2,1,0:T(8,128)(2,1)S(1)} %other_keys.1), channel_id=1, replica_groups=mesh['crop'=16,'y'=4,'z'=8] {'y','z'}, dimensions={0} | all-to-all | bytes 1048576 | tf_op jit(solution)/shard_map/all_to_all | solution.py:325
  149.5 0.0 copy-done.1
  149.5 0.5 features.1.mid_ref
  150.0 3.0 %collective-permute-start.1 = (bf16[128,256]{1,0:T(8,128)(2,1)S(1)}, bf16[128,256]{1,0:T(8,128)(2,1)S(1)}, u32[]{:S(2)}, u32[]{:S(2)}) collective-permute-start(bf16[128,256]{1,0:T(8,128)(2,1)S(1)} %features.1.mid_ref), channel_id=1, source_target_pairs={{0,1},{1,0},{2,3},{3,2},{4,5},{5,4},{6,7},{7,6},{8,9},{9,8},{10,11... | collective-permute-start | bytes 196616 | tf_op jit(solution)/shard_map/ppermute | solution.py:337
  153.0 0.7 collective-permute-start.2
  153.7 0.1 copy.15.class_bias_ref
  153.8 2.4 %collective-permute-done.1.pair_ref = bf16[128,256]{1,0:T(8,128)(2,1)S(1)} collective-permute-done((bf16[128,256]{1,0:T(8,128)(2,1)S(1)}, bf16[128,256]{1,0:T(8,128)(2,1)S(1)}, u32[]{:S(2)}, u32[]{:S(2)}) %collective-permute-start.1) | collective-permute-done | bytes 65568 | tf_op jit(solution)/shard_map/ppermute | solution.py:337
  156.2 0.0 collective-permute-done.2.far_ref
  156.2 0.0 copy-done.2
  156.2 2.0 %head.1 = (f32[16,8,256]{2,1,0:T(8,128)}, f32[8,256]{1,0:T(8,128)}, f32[32,1,128]{2,1,0:T(1,128)S(1)}) custom-call(bf16[128,256]{1,0:T(8,128)(2,1)S(1)} %collective-permute-done.1.pair_ref, bf16[128,256]{1,0:T(8,128)(2,1)S(1)} %features.1.mid_ref, bf16[128,256]{1,0:T(8,128)(2,1)S(1)} %collective-permute-done.2.far_ref, bf16[9,256,256]{2,1,0:T(8,128)(2,1)S(1)} %copy-done, ...), custom_call_target="tpu_custom_call" | custom-call | tf_op jit(solution)/shard_map/head/pallas_call | solution.py:339
  158.2 27.9 %all_to_all.17 = f32[32,1,128]{2,1,0:T(1,128)S(1)} all-to-all(f32[32,1,128]{2,1,0:T(1,128)S(1)} %get-tuple-element.12), channel_id=1, replica_groups=mesh['crop'=16,'y'=4,'z'=8] {'y','z'}, dimensions={0} | all-to-all | bytes 32768 | tf_op jit(solution)/shard_map/all_to_all | solution.py:355
  186.1 0.6 slice_reduce_fusion
  (7 shorter events, 0.0 us)
Async XLA Ops:
  92.0 16.7 %collective-permute-start = (bf16[32,128,128]{2,1,0:T(8,128)(2,1)S(1)}, bf16[32,128,128]{2,1,0:T(8,128)(2,1)S(1)}, u32[]{:S(2)}, u32[]{:S(2)}) collective-permute-start(bf16[32,128,128]{2,1,0:T(8,128)(2,1)S(1)} %slice.8), channel_id=1, source_target_pairs={{0,8},{8,0},{16,24},{24,16},{32,56},{40,48},{48,40},{56,32},{64,72... | collective-permute-start | bytes 3145736 | tf_op jit(solution)/shard_map/ppermute | solution.py:324
  108.7 40.8 %copy-start.1 = (bf16[2048,256]{1,0:T(8,128)(2,1)S(1)}, bf16[2048,256]{1,0:T(8,128)(2,1)}, u32[]{:S(2)}) copy-start(bf16[2048,256]{1,0:T(8,128)(2,1)} %proj_ref.1) | copy-start | bytes 3145732
  108.7 40.8 %copy-start.5 = (f32[256]{0:T(256)S(1)}, f32[256]{0:T(256)}, u32[]{:S(2)}) copy-start(f32[256]{0:T(256)} %param.16) | copy-start | bytes 3076
  114.0 39.7 %copy-start.6 = (f32[16]{0:T(128)S(1)}, f32[16]{0:T(128)}, u32[]{:S(2)}) copy-start(f32[16]{0:T(128)} %param.20) | copy-start | bytes 196
  114.0 42.2 %copy-start = (bf16[9,256,256]{2,1,0:T(8,128)(2,1)S(1)}, bf16[9,256,256]{2,1,0:T(8,128)(2,1)}, u32[]{:S(2)}) copy-start(bf16[9,256,256]{2,1,0:T(8,128)(2,1)} %weight_ref.1) | copy-start | bytes 3538948
  114.0 42.2 %copy-start.2 = (bf16[9,16,256]{2,1,0:T(8,128)(2,1)S(1)}, bf16[9,16,256]{2,1,0:T(8,128)(2,1)}, u32[]{:S(2)}) copy-start(bf16[9,16,256]{2,1,0:T(8,128)(2,1)} %param.19) | copy-start | bytes 221188
  114.0 42.2 %copy-start.3 = (s32[8,256]{1,0:T(8,128)S(1)}, s32[8,256]{1,0:T(8,128)}, u32[]{:S(2)}) copy-start(s32[8,256]{1,0:T(8,128)} %labels_ref.1) | copy-start | bytes 24580
  114.0 42.2 %copy-start.4 = (f32[256]{0:T(256)S(1)}, f32[256]{0:T(256)}, u32[]{:S(2)}) copy-start(f32[256]{0:T(256)} %param.18) | copy-start | bytes 3076
  150.0 6.2 %collective-permute-start.1 = (bf16[128,256]{1,0:T(8,128)(2,1)S(1)}, bf16[128,256]{1,0:T(8,128)(2,1)S(1)}, u32[]{:S(2)}, u32[]{:S(2)}) collective-permute-start(bf16[128,256]{1,0:T(8,128)(2,1)S(1)} %features.1.mid_ref), channel_id=1, source_target_pairs={{0,1},{1,0},{2,3},{3,2},{4,5},{5,4},{6,7},{7,6},{8,9},{9,8},{10,11... | collective-permute-start | bytes 196616 | tf_op jit(solution)/shard_map/ppermute | solution.py:337
  153.0 3.2 %collective-permute-start.2 = (bf16[128,256]{1,0:T(8,128)(2,1)S(1)}, bf16[128,256]{1,0:T(8,128)(2,1)S(1)}, u32[]{:S(2)}, u32[]{:S(2)}) collective-permute-start(bf16[128,256]{1,0:T(8,128)(2,1)S(1)} %features.1.mid_ref), channel_id=1, source_target_pairs={{1,2},{2,1},{3,4},{4,3},{5,6},{6,5},{7,8},{8,7},{9,10},{10,9},{11,... | collective-permute-start | bytes 196616 | tf_op jit(solution)/shard_map/ppermute | solution.py:336

commit v4 on v3

--- a/solution.py
+++ b/solution.py
@@ -50,11 +50,13 @@
     return lax.rem(lax.axis_index("crop"), 2), place
 
 
+LATE = 16
+EARLY = COLS - LATE
 PARTS = 4
 PART = HEADS * HEAD_DIM // PARTS
 
 
-def pack_kernel(q_hbm, k_hbm, v_hbm, cos_hbm, sin_hbm, out_ref, q_ref, k_ref, v_ref, cos_ref, sin_ref, sems, table_sems):
+def pack_kernel(q_hbm, k_hbm, v_hbm, cos_hbm, sin_hbm, out_ref, late_ref, q_ref, k_ref, v_ref, cos_ref, sin_ref, sems, table_sems):
     core, place = positions()
     tables_in = [
         pltpu.make_async_copy(cos_hbm, cos_ref, table_sems.at[0]),
@@ -102,10 +104,13 @@
                         pltpu.roll(x, HEAD_DIM - HEAD_DIM // 4, 1),
                         pltpu.roll(x, HEAD_DIM // 4, 1),
                     )
-                    out_ref[y, z, index * COLS : (index + 1) * COLS, :] = (
-                        x * cosine + partner * sine
-                    ).astype(BF16)
-                out_ref[y, z, 2 * COLS :, :] = v_ref[part, rows, lanes]
+                    turned = (x * cosine + partner * sine).astype(BF16)
+                    if index == 0:
+                        out_ref[y, z, :EARLY, :] = turned[:EARLY]
+                        late_ref[y, z, :, :] = turned[EARLY:]
+                    else:
+                        out_ref[y, z, EARLY : EARLY + COLS, :] = turned
+                out_ref[y, z, EARLY + COLS :, :] = v_ref[part, rows, lanes]
 
 
 def pack(queries, keys, values, cosine, sine):
@@ -113,8 +118,11 @@
     return pl.pallas_call(
         pack_kernel,
         in_specs=[pl.BlockSpec(memory_space=pltpu.HBM)] * 5,
-        out_specs=VMEM,
-        out_shape=jax.ShapeDtypeStruct((YS, ZS, 3 * COLS, HEAD_DIM), BF16),
+        out_specs=[VMEM, VMEM],
+        out_shape=[
+            jax.ShapeDtypeStruct((YS, ZS, EARLY + 2 * COLS, HEAD_DIM), BF16),
+            jax.ShapeDtypeStruct((YS, ZS, LATE, HEAD_DIM), BF16),
+        ],
         scratch_shapes=[pltpu.VMEM((PARTS, tokens, PART), BF16)] * 3
         + [pltpu.VMEM((COLS, HEAD_DIM), F32)] * 2
         + [pltpu.SemaphoreType.DMA((PARTS, 3)), pltpu.SemaphoreType.DMA((2,))],
@@ -150,13 +158,29 @@
     return jnp.broadcast_to(top, (query.shape[0], HEAD_DIM)), total
 
 
+def keys_values(ref, first):
+    tokens = SEQ * COLS
+    key = ref[:, first : first + COLS, :].reshape(tokens, HEAD_DIM)
+    value = ref[:, first + COLS : first + 2 * COLS, :].reshape(tokens, HEAD_DIM)
+    return key, with_ones(value)
+
+
+def joined(one, two):
+    top = jnp.maximum(one[0], two[0])
+    fades = [jnp.exp2((side[0] - top) * EXP_SCALE) for side in (one, two)]
+    mixed, norm = [
+        sum(side[1][:, lanes] * fade for side, fade in zip((one, two), fades))
+        for lanes in (slice(0, HEAD_DIM), slice(HEAD_DIM, 2 * HEAD_DIM))
+    ]
+    return (mixed / norm).astype(BF16)
+
+
 def own_kernel(mine_ref, acc_ref, top_ref):
-    rows = BLOCK * COLS
-    key = mine_ref[:, COLS : 2 * COLS, :].reshape(SEQ * COLS, HEAD_DIM)
-    value = with_ones(mine_ref[:, 2 * COLS :, :].reshape(SEQ * COLS, HEAD_DIM))
+    rows = BLOCK * EARLY
+    key, value = keys_values(mine_ref, EARLY)
 
     def step(i, carry):
-        query = mine_ref[pl.ds(i * BLOCK, BLOCK), :COLS, :].reshape(rows, HEAD_DIM)
+        query = mine_ref[pl.ds(i * BLOCK, BLOCK), :EARLY, :].reshape(rows, HEAD_DIM)
         out = pl.ds(pl.multiple_of(i * rows, rows), rows)
         top_ref[out, :], acc_ref[out, :] = sweep(query, key, value)
         return carry
@@ -165,33 +189,44 @@
 
 
 def other_kernel(mine_ref, other_ref, acc_ref, top_ref, out_ref):
-    rows = BLOCK * COLS
-    key = other_ref[:, :COLS, :].reshape(SEQ * COLS, HEAD_DIM)
-    value = with_ones(other_ref[:, COLS:, :].reshape(SEQ * COLS, HEAD_DIM))
+    rows = BLOCK * EARLY
+    key, value = keys_values(other_ref, 0)
 
     def step(i, carry):
-        query = mine_ref[pl.ds(i * BLOCK, BLOCK), :COLS, :].reshape(rows, HEAD_DIM)
+        query = mine_ref[pl.ds(i * BLOCK, BLOCK), :EARLY, :].reshape(rows, HEAD_DIM)
         place = pl.ds(pl.multiple_of(i * rows, rows), rows)
-        top_here, here = sweep(query, key, value)
-        top_there, there = top_ref[place, :], acc_ref[place, :]
-        top = jnp.maximum(top_here, top_there)
-        fade_here = jnp.exp2((top_here - top) * EXP_SCALE)
-        fade_there = jnp.exp2((top_there - top) * EXP_SCALE)
-        mixed = here[:, :HEAD_DIM] * fade_here + there[:, :HEAD_DIM] * fade_there
-        norm = here[:, HEAD_DIM:] * fade_here + there[:, HEAD_DIM:] * fade_there
-        out_ref[pl.ds(i * BLOCK, BLOCK), :, :] = (
-            (mixed / norm).astype(BF16).reshape(BLOCK, COLS, HEAD_DIM)
-        )
+        mixed = joined(sweep(query, key, value), (top_ref[place, :], acc_ref[place, :]))
+        out_ref[pl.ds(i * BLOCK, BLOCK), :EARLY, :] = mixed.reshape(BLOCK, EARLY, HEAD_DIM)
         return carry
 
     lax.fori_loop(0, SEQ // BLOCK, step, 0, unroll=SEQ // BLOCK)
 
 
-def attend(mine, swap):
-    tokens = SEQ * COLS
-    half_flops = 2 * tokens * tokens * HEAD_DIM * 3
-    cost = pl.CostEstimate(flops=half_flops, bytes_accessed=4 << 20, transcendentals=tokens * tokens)
-    other = swap(mine[:, COLS:, :])
+LATE_BLOCK = 8
+
+
+def late_kernel(late_ref, mine_ref, other_ref, early_ref, out_ref):
+    rows = LATE_BLOCK * LATE
+    own = keys_values(mine_ref, EARLY)
+    other = keys_values(other_ref, 0)
+    del early_ref
+    for i in range(SEQ // LATE_BLOCK):
+        block = slice(i * LATE_BLOCK, (i + 1) * LATE_BLOCK)
+        query = late_ref[block].reshape(rows, HEAD_DIM)
+        mixed = joined(sweep(query, *own), sweep(query, *other))
+        out_ref[block, EARLY:, :] = mixed.reshape(LATE_BLOCK, LATE, HEAD_DIM)
+
+
+def attend(send, late, swap, everyone):
+    tokens = SEQ * EARLY
+    cost = pl.CostEstimate(
+        flops=6 * tokens * SEQ * COLS * HEAD_DIM,
+        bytes_accessed=4 << 20,
+        transcendentals=tokens * SEQ * COLS,
+    )
+    mine = everyone(send)
+    other = swap(mine[:, EARLY:, :])
+    late = everyone(late)
     acc, top = pl.pallas_call(
         own_kernel,
         in_specs=[VMEM],
@@ -204,7 +239,7 @@
         compiler_params=limit(28),
         name="own_keys",
     )(mine)
-    return pl.pallas_call(
+    early = pl.pallas_call(
         other_kernel,
         in_specs=[VMEM] * 4,
         out_specs=VMEM,
@@ -213,6 +248,15 @@
         compiler_params=limit(28),
         name="other_keys",
     )(mine, other, acc, top)
+    return pl.pallas_call(
+        late_kernel,
+        in_specs=[VMEM] * 4,
+        out_specs=VMEM,
+        out_shape=jax.ShapeDtypeStruct((SEQ, COLS, HEAD_DIM), BF16),
+        input_output_aliases={3: 0},
+        compiler_params=limit(28),
+        name="late_queries",
+    )(late, mine, other, early)
 
 
 def features_kernel(mixed_ref, proj_ref, gain_ref, out_ref):
@@ -319,9 +363,15 @@
             slot = (y - crop % 2) % YS
             swaps.append((crop * YS + y, crop * YS + ((slot ^ 1) + crop % 2) % YS))
 
-    send = pack(queries, keys, values, cosine, sine).reshape(SEQ, 3 * COLS, HEAD_DIM)
-    mine = lax.all_to_all(send, seq, 0, 0, tiled=True)
-    attended = attend(mine, lambda x: lax.ppermute(x, ("crop", "y"), swaps))
+    send, late = (
+        x.reshape(SEQ, x.shape[2], HEAD_DIM) for x in pack(queries, keys, values, cosine, sine)
+    )
+    attended = attend(
+        send,
+        late,
+        lambda x: lax.ppermute(x, ("crop", "y"), swaps),
+        lambda x: lax.all_to_all(x, seq, 0, 0, tiled=True),
+    )
     returned = lax.all_to_all(attended, seq, 0, 0, tiled=True)
 
     strip_tokens = queries.shape[0]

time: 189 us -> 189 us (level)
  starting transfers between devices: 6.22 us -> 12.8 us
  blocking collectives: 152 us -> 147 us
  waiting for transfers between devices: 11.5 us -> 8.32 us
    all_to_all x0 -> x1, starting transfers between devices: none -> 6.67 us  [body(): lax.all_to_all(x, seq, 0, 0, tiled=True)]
    all_to_all x1, blocking collectives: 88.9 us -> 84.1 us  [body(): lax.all_to_all(x, seq, 0, 0, tiled=True)]
    ppermute x1, waiting for transfers between devices: 9.05 us -> 4.64 us  [body(): lax.ppermute(x, ('crop', 'y'), swaps)]
    pallas_call x0 -> x1, Pallas kernels: none -> 2.71 us  [attend(): pl.pallas_call(late_kernel, in_specs=[VMEM] * 4, out_specs=VMEM, out_shap...]
  transfers between devices with their start and end apart: 3 -> 4, of which waited for: 2 -> 3; matrix products, arithmetic and copies ran while one was open for 0% -> 0% of each run, Pallas kernels for 3% -> 4%
where the time goes in v4:
time: 189 us
  blocking collectives  147 us (78%)
  Pallas kernels  16.1 us (9%)
  starting transfers between devices  12.8 us (7%)
  waiting for transfers between devices  8.32 us (4%)
  between operations  2.55 us (1%)
    all_to_all x1, blocking collectives, body(): lax.all_to_all(x, seq, 0, 0, tiled=True)  84.1 us
    all_to_all x1, blocking collectives, body(): returned = lax.all_to_all(attended, seq, 0, 0, tiled=True)  35.4 us
    all_to_all x1, blocking collectives, body(): everyone = lax.all_to_all(sums, seq, 0, 0, tiled=True)  27.9 us
    all_to_all x1, starting transfers between devices, body(): lax.all_to_all(x, seq, 0, 0, tiled=True)  6.67 us
    ppermute x1, waiting for transfers between devices, body(): lax.ppermute(x, ('crop', 'y'), swaps)  4.64 us
    pallas_call x1, Pallas kernels, attend(): pl.pallas_call(other_kernel, in_specs=[VMEM] * 4, out_specs=VMEM, out_sha...  4.03 us
    pallas_call x1, Pallas kernels, attend(): pl.pallas_call(own_kernel, in_specs=[VMEM], out_specs=[VMEM, VMEM], out_s...  3.83 us
  transfers between devices with their start and end apart: 4, of which 3 were waited for; matrix products, arithmetic and copies ran while one was open for 0% of the time, Pallas kernels for 4%

profile of v4, /device:TPU:6, one launch (start us, length us, event | category | flops | bytes accessed | tf_op | source)
XLA Modules:
  0.0 189.0 jit_solution(9112664630593425817)
XLA Ops:
  0.6 3.0 %pack.1 = (bf16[4,8,176,128]{3,2,1,0:T(8,128)(2,1)S(1)}, bf16[4,8,16,128]{3,2,1,0:T(8,128)(2,1)}) custom-call(bf16[128,2048]{1,0:T(8,128)(2,1)} %q_hbm.1, bf16[128,2048]{1,0:T(8,128)(2,1)} %k_hbm.1, bf16[128,2048]{1,0:T(8,128)(2,1)} %v_hbm.1, f32[64,128]{1,0:T(8,128)} %constant.9.clone.cos_hbm, f32[64,128]{1,0:T(8,128)} %constant.10.clone.sin_hbm), custom_call_target="tpu_custom_call" | custom-call | tf_op jit(solution)/shard_map/pack/pallas_call | solution.py:118
  3.6 84.1 %all_to_all.20.mine_ref = bf16[32,176,128]{2,1,0:T(8,128)(2,1)S(1)} all-to-all(bf16[32,176,128]{2,1,0:T(8,128)(2,1)S(1)} %bitcast.7), channel_id=1, replica_groups=mesh['crop'=16,'y'=4,'z'=8] {'y','z'}, dimensions={0} | all-to-all | bytes 2883584 | tf_op jit(solution)/shard_map/all_to_all | solution.py:373
  87.8 1.1 slice.8
  88.9 2.5 %collective-permute-start = (bf16[32,128,128]{2,1,0:T(8,128)(2,1)}, bf16[32,128,128]{2,1,0:T(8,128)(2,1)S(1)}, u32[]{:S(2)}, u32[]{:S(2)}) collective-permute-start(bf16[32,128,128]{2,1,0:T(8,128)(2,1)} %slice.8), channel_id=1, source_target_pairs={{0,8},{8,0},{16,24},{24,16},{32,56},{40,48},{48,40},{56,32},{64,72... | collective-permute-start | bytes 3145736 | tf_op jit(solution)/shard_map/ppermute | solution.py:372
  91.4 6.7 %all-to-all-start = ((bf16[32,16,128]{2,1,0:T(8,128)(2,1)}), bf16[32,16,128]{2,1,0:T(8,128)(2,1)S(1)}, u32[]{:S(2)}, u32[]{:S(2)}) async-start(bf16[32,16,128]{2,1,0:T(8,128)(2,1)} %bitcast), calls=%async_computation | async-start | bytes 262144 | tf_op jit(solution)/shard_map/all_to_all | solution.py:373
  98.1 3.8 %own_keys.1 = (f32[1536,256]{1,0:T(8,128)S(1)}, f32[1536,128]{1,0:T(8,128)S(1)}) custom-call(bf16[32,176,128]{2,1,0:T(8,128)(2,1)S(1)} %all_to_all.20.mine_ref), custom_call_target="tpu_custom_call" | custom-call | flops 2415919104 | bytes 4194304 | tf_op jit(solution)/shard_map/own_keys/pallas_call | solution.py:230
  101.9 4.6 %collective-permute-done.other_ref = bf16[32,128,128]{2,1,0:T(8,128)(2,1)S(1)} collective-permute-done((bf16[32,128,128]{2,1,0:T(8,128)(2,1)}, bf16[32,128,128]{2,1,0:T(8,128)(2,1)S(1)}, u32[]{:S(2)}, u32[]{:S(2)}) %collective-permute-start) | collective-permute-done | bytes 1048608 | tf_op jit(solution)/shard_map/ppermute | solution.py:372
  106.5 4.0 %other_keys.1.early_ref = bf16[32,64,128]{2,1,0:T(8,128)(2,1)S(1)} custom-call(bf16[32,176,128]{2,1,0:T(8,128)(2,1)S(1)} %all_to_all.20.mine_ref, bf16[32,128,128]{2,1,0:T(8,128)(2,1)S(1)} %collective-permute-done.other_ref, f32[1536,256]{1,0:T(8,128)S(1)} %get-tuple-element.12.acc_ref, f32[1536,128]{1,0:T(8,128)S(1)} %get-tuple-element.13.top_ref), custom_call_target="tpu_custom_call" | custom-call | flops 2415919104 | bytes 4194304 | tf_op jit(solution)/shard_map/other_keys/pallas_call | solution.py:242
  110.6 0.0 copy-start.5
  110.6 1.3 all-to-all-done.late_ref
  111.9 2.7 %late_queries.1 = bf16[32,64,128]{2,1,0:T(8,128)(2,1)S(1)} custom-call(bf16[32,16,128]{2,1,0:T(8,128)(2,1)S(1)} %all-to-all-done.late_ref, bf16[32,176,128]{2,1,0:T(8,128)(2,1)S(1)} %all_to_all.20.mine_ref, bf16[32,128,128]{2,1,0:T(8,128)(2,1)S(1)} %collective-permute-done.other_ref, ...), custom_call_target="tpu_custom_call", output_to_operand_aliasing={{}: (3, {})} | custom-call | tf_op jit(solution)/shard_map/late_queries/pallas_call | solution.py:251
  114.6 0.0 copy-start.6
  114.6 0.0 copy-start
  114.6 0.0 copy-start.2
  114.6 0.0 copy-start.4
  114.6 35.4 %all_to_all.21.mixed_ref = bf16[32,64,128]{2,1,0:T(8,128)(2,1)S(1)} all-to-all(bf16[32,64,128]{2,1,0:T(8,128)(2,1)S(1)} %late_queries.1), channel_id=1, replica_groups=mesh['crop'=16,'y'=4,'z'=8] {'y','z'}, dimensions={0} | all-to-all | bytes 1048576 | tf_op jit(solution)/shard_map/all_to_all | solution.py:375
  150.0 0.5 features.1.mid_ref
  150.5 3.0 %collective-permute-start.1 = (bf16[128,256]{1,0:T(8,128)(2,1)S(1)}, bf16[128,256]{1,0:T(8,128)(2,1)S(1)}, u32[]{:S(2)}, u32[]{:S(2)}) collective-permute-start(bf16[128,256]{1,0:T(8,128)(2,1)S(1)} %features.1.mid_ref), channel_id=1, source_target_pairs={{0,1},{1,0},{2,3},{3,2},{4,5},{5,4},{6,7},{7,6},{8,9},{9,8},{10,11... | collective-permute-start | bytes 196616 | tf_op jit(solution)/shard_map/ppermute | solution.py:387
  153.5 0.7 collective-permute-start.2
  154.2 0.1 copy.16.class_bias_ref
  154.3 2.4 %collective-permute-done.1.pair_ref = bf16[128,256]{1,0:T(8,128)(2,1)S(1)} collective-permute-done((bf16[128,256]{1,0:T(8,128)(2,1)S(1)}, bf16[128,256]{1,0:T(8,128)(2,1)S(1)}, u32[]{:S(2)}, u32[]{:S(2)}) %collective-permute-start.1) | collective-permute-done | bytes 65568 | tf_op jit(solution)/shard_map/ppermute | solution.py:387
  156.7 2.0 %head.1 = (f32[16,8,256]{2,1,0:T(8,128)}, f32[8,256]{1,0:T(8,128)}, f32[32,1,128]{2,1,0:T(1,128)S(1)}) custom-call(bf16[128,256]{1,0:T(8,128)(2,1)S(1)} %collective-permute-done.1.pair_ref, bf16[128,256]{1,0:T(8,128)(2,1)S(1)} %features.1.mid_ref, bf16[128,256]{1,0:T(8,128)(2,1)S(1)} %collective-permute-done.2.far_ref, bf16[9,256,256]{2,1,0:T(8,128)(2,1)S(1)} %copy-done, ...), custom_call_target="tpu_custom_call" | custom-call | tf_op jit(solution)/shard_map/head/pallas_call | solution.py:389
  158.7 27.9 %all_to_all.22 = f32[32,1,128]{2,1,0:T(1,128)S(1)} all-to-all(f32[32,1,128]{2,1,0:T(1,128)S(1)} %get-tuple-element.16), channel_id=1, replica_groups=mesh['crop'=16,'y'=4,'z'=8] {'y','z'}, dimensions={0} | all-to-all | bytes 32768 | tf_op jit(solution)/shard_map/all_to_all | solution.py:405
  186.6 0.6 slice_reduce_fusion
  (10 shorter events, 0.0 us)
Async XLA Ops:
  88.9 17.7 %collective-permute-start = (bf16[32,128,128]{2,1,0:T(8,128)(2,1)}, bf16[32,128,128]{2,1,0:T(8,128)(2,1)S(1)}, u32[]{:S(2)}, u32[]{:S(2)}) collective-permute-start(bf16[32,128,128]{2,1,0:T(8,128)(2,1)} %slice.8), channel_id=1, source_target_pairs={{0,8},{8,0},{16,24},{24,16},{32,56},{40,48},{48,40},{56,32},{64,72... | collective-permute-start | bytes 3145736 | tf_op jit(solution)/shard_map/ppermute | solution.py:372
  91.4 20.5 %all-to-all-start = ((bf16[32,16,128]{2,1,0:T(8,128)(2,1)}), bf16[32,16,128]{2,1,0:T(8,128)(2,1)S(1)}, u32[]{:S(2)}, u32[]{:S(2)}) async-start(bf16[32,16,128]{2,1,0:T(8,128)(2,1)} %bitcast), calls=%async_computation | async-start | bytes 262144 | tf_op jit(solution)/shard_map/all_to_all | solution.py:373
  110.6 39.5 %copy-start.5 = (f32[256]{0:T(256)S(1)}, f32[256]{0:T(256)}, u32[]{:S(2)}) copy-start(f32[256]{0:T(256)} %param.16) | copy-start | bytes 3076
  111.9 38.2 %copy-start.1 = (bf16[2048,256]{1,0:T(8,128)(2,1)S(1)}, bf16[2048,256]{1,0:T(8,128)(2,1)}, u32[]{:S(2)}) copy-start(bf16[2048,256]{1,0:T(8,128)(2,1)} %proj_ref.1) | copy-start | bytes 3145732
  114.6 39.6 %copy-start.6 = (f32[16]{0:T(128)S(1)}, f32[16]{0:T(128)}, u32[]{:S(2)}) copy-start(f32[16]{0:T(128)} %param.20) | copy-start | bytes 196
  114.6 42.1 %copy-start = (bf16[9,256,256]{2,1,0:T(8,128)(2,1)S(1)}, bf16[9,256,256]{2,1,0:T(8,128)(2,1)}, u32[]{:S(2)}) copy-start(bf16[9,256,256]{2,1,0:T(8,128)(2,1)} %weight_ref.1) | copy-start | bytes 3538948
  114.6 42.1 %copy-start.2 = (bf16[9,16,256]{2,1,0:T(8,128)(2,1)S(1)}, bf16[9,16,256]{2,1,0:T(8,128)(2,1)}, u32[]{:S(2)}) copy-start(bf16[9,16,256]{2,1,0:T(8,128)(2,1)} %param.19) | copy-start | bytes 221188
  114.6 42.1 %copy-start.3 = (s32[8,256]{1,0:T(8,128)S(1)}, s32[8,256]{1,0:T(8,128)}, u32[]{:S(2)}) copy-start(s32[8,256]{1,0:T(8,128)} %labels_ref.1) | copy-start | bytes 24580
  114.6 42.1 %copy-start.4 = (f32[256]{0:T(256)S(1)}, f32[256]{0:T(256)}, u32[]{:S(2)}) copy-start(f32[256]{0:T(256)} %param.18) | copy-start | bytes 3076
  150.5 6.2 %collective-permute-start.1 = (bf16[128,256]{1,0:T(8,128)(2,1)S(1)}, bf16[128,256]{1,0:T(8,128)(2,1)S(1)}, u32[]{:S(2)}, u32[]{:S(2)}) collective-permute-start(bf16[128,256]{1,0:T(8,128)(2,1)S(1)} %features.1.mid_ref), channel_id=1, source_target_pairs={{0,1},{1,0},{2,3},{3,2},{4,5},{5,4},{6,7},{7,6},{8,9},{9,8},{10,11... | collective-permute-start | bytes 196616 | tf_op jit(solution)/shard_map/ppermute | solution.py:387
  153.5 3.2 %collective-permute-start.2 = (bf16[128,256]{1,0:T(8,128)(2,1)S(1)}, bf16[128,256]{1,0:T(8,128)(2,1)S(1)}, u32[]{:S(2)}, u32[]{:S(2)}) collective-permute-start(bf16[128,256]{1,0:T(8,128)(2,1)S(1)} %features.1.mid_ref), channel_id=1, source_target_pairs={{1,2},{2,1},{3,4},{4,3},{5,6},{6,5},{7,8},{8,7},{9,10},{10,9},{11,... | collective-permute-start | bytes 196616 | tf_op jit(solution)/shard_map/ppermute | solution.py:386

commit v5 on v3

--- a/solution.py
+++ b/solution.py
@@ -150,69 +150,109 @@
     return jnp.broadcast_to(top, (query.shape[0], HEAD_DIM)), total
 
 
+def keys_values(ref, first):
+    tokens = ref.shape[0] * COLS
+    key = ref[:, first : first + COLS, :].reshape(tokens, HEAD_DIM)
+    value = ref[:, first + COLS : first + 2 * COLS, :].reshape(tokens, HEAD_DIM)
+    return key, with_ones(value)
+
+
+def each_block(visit):
+    def step(i, carry):
+        rows = BLOCK * COLS
+        visit(pl.ds(i * BLOCK, BLOCK), pl.ds(pl.multiple_of(i * rows, rows), rows))
+        return carry
+
+    lax.fori_loop(0, SEQ // BLOCK, step, 0, unroll=SEQ // BLOCK)
+
+
+def joined(one, two):
+    top = jnp.maximum(one[0], two[0])
+    fades = [jnp.exp2((side[0] - top) * EXP_SCALE) for side in (one, two)]
+    mixed, norm = [
+        one[1][:, lanes] * fades[0] + two[1][:, lanes] * fades[1]
+        for lanes in (slice(0, HEAD_DIM), slice(HEAD_DIM, 2 * HEAD_DIM))
+    ]
+    return top, mixed, norm
+
+
 def own_kernel(mine_ref, acc_ref, top_ref):
-    rows = BLOCK * COLS
-    key = mine_ref[:, COLS : 2 * COLS, :].reshape(SEQ * COLS, HEAD_DIM)
-    value = with_ones(mine_ref[:, 2 * COLS :, :].reshape(SEQ * COLS, HEAD_DIM))
-
-    def step(i, carry):
-        query = mine_ref[pl.ds(i * BLOCK, BLOCK), :COLS, :].reshape(rows, HEAD_DIM)
-        out = pl.ds(pl.multiple_of(i * rows, rows), rows)
-        top_ref[out, :], acc_ref[out, :] = sweep(query, key, value)
-        return carry
-
-    lax.fori_loop(0, SEQ // BLOCK, step, 0, unroll=SEQ // BLOCK)
-
-
-def other_kernel(mine_ref, other_ref, acc_ref, top_ref, out_ref):
-    rows = BLOCK * COLS
-    key = other_ref[:, :COLS, :].reshape(SEQ * COLS, HEAD_DIM)
-    value = with_ones(other_ref[:, COLS:, :].reshape(SEQ * COLS, HEAD_DIM))
-
-    def step(i, carry):
-        query = mine_ref[pl.ds(i * BLOCK, BLOCK), :COLS, :].reshape(rows, HEAD_DIM)
-        place = pl.ds(pl.multiple_of(i * rows, rows), rows)
-        top_here, here = sweep(query, key, value)
-        top_there, there = top_ref[place, :], acc_ref[place, :]
-        top = jnp.maximum(top_here, top_there)
-        fade_here = jnp.exp2((top_here - top) * EXP_SCALE)
-        fade_there = jnp.exp2((top_there - top) * EXP_SCALE)
-        mixed = here[:, :HEAD_DIM] * fade_here + there[:, :HEAD_DIM] * fade_there
-        norm = here[:, HEAD_DIM:] * fade_here + there[:, HEAD_DIM:] * fade_there
-        out_ref[pl.ds(i * BLOCK, BLOCK), :, :] = (
-            (mixed / norm).astype(BF16).reshape(BLOCK, COLS, HEAD_DIM)
-        )
-        return carry
-
-    lax.fori_loop(0, SEQ // BLOCK, step, 0, unroll=SEQ // BLOCK)
+    key, value = keys_values(mine_ref, COLS)
+
+    def visit(block, rows):
+        query = mine_ref[block, :COLS, :].reshape(BLOCK * COLS, HEAD_DIM)
+        top_ref[rows, :], acc_ref[rows, :] = sweep(query, key, value)
+
+    each_block(visit)
+
+
+def more_kernel(mine_ref, other_ref, acc_ref, top_ref, new_acc_ref, new_top_ref):
+    key, value = keys_values(other_ref, 0)
+
+    def visit(block, rows):
+        query = mine_ref[block, :COLS, :].reshape(BLOCK * COLS, HEAD_DIM)
+        top, mixed, norm = joined(sweep(query, key, value), (top_ref[rows, :], acc_ref[rows, :]))
+        new_top_ref[rows, :] = top
+        new_acc_ref[rows, :HEAD_DIM] = mixed
+        new_acc_ref[rows, HEAD_DIM:] = norm
+
+    each_block(visit)
+
+
+def last_kernel(mine_ref, other_ref, acc_ref, top_ref, out_ref):
+    key, value = keys_values(other_ref, 0)
+
+    def visit(block, rows):
+        query = mine_ref[block, :COLS, :].reshape(BLOCK * COLS, HEAD_DIM)
+        _, mixed, norm = joined(sweep(query, key, value), (top_ref[rows, :], acc_ref[rows, :]))
+        out_ref[block, :, :] = (mixed / norm).astype(BF16).reshape(BLOCK, COLS, HEAD_DIM)
+
+    each_block(visit)
+
+
+FIRST = 16
 
 
 def attend(mine, swap):
     tokens = SEQ * COLS
-    half_flops = 2 * tokens * tokens * HEAD_DIM * 3
-    cost = pl.CostEstimate(flops=half_flops, bytes_accessed=4 << 20, transcendentals=tokens * tokens)
-    other = swap(mine[:, COLS:, :])
+
+    def cost(sources):
+        pairs = tokens * sources * COLS
+        return pl.CostEstimate(flops=6 * pairs * HEAD_DIM, bytes_accessed=4 << 20, transcendentals=pairs)
+
+    running = [
+        jax.ShapeDtypeStruct((tokens, 2 * HEAD_DIM), F32),
+        jax.ShapeDtypeStruct((tokens, HEAD_DIM), F32),
+    ]
+    one = swap(mine[:FIRST, COLS:, :])
+    two = swap(mine[FIRST:, COLS:, :])
     acc, top = pl.pallas_call(
         own_kernel,
         in_specs=[VMEM],
         out_specs=[VMEM, VMEM],
-        out_shape=[
-            jax.ShapeDtypeStruct((tokens, 2 * HEAD_DIM), F32),
-            jax.ShapeDtypeStruct((tokens, HEAD_DIM), F32),
-        ],
-        cost_estimate=cost,
+        out_shape=running,
+        cost_estimate=cost(SEQ),
         compiler_params=limit(28),
         name="own_keys",
     )(mine)
+    acc, top = pl.pallas_call(
+        more_kernel,
+        in_specs=[VMEM] * 4,
+        out_specs=[VMEM, VMEM],
+        out_shape=running,
+        cost_estimate=cost(FIRST),
+        compiler_params=limit(28),
+        name="more_keys",
+    )(mine, one, acc, top)
     return pl.pallas_call(
-        other_kernel,
+        last_kernel,
         in_specs=[VMEM] * 4,
         out_specs=VMEM,
         out_shape=jax.ShapeDtypeStruct((SEQ, COLS, HEAD_DIM), BF16),
-        cost_estimate=cost,
+        cost_estimate=cost(SEQ - FIRST),
         compiler_params=limit(28),
-        name="other_keys",
-    )(mine, other, acc, top)
+        name="last_keys",
+    )(mine, two, acc, top)
 
 
 def features_kernel(mixed_ref, proj_ref, gain_ref, out_ref):

time: 189 us -> 186 us (0.984)
  waiting for transfers between devices: 11.5 us -> 5.23 us
  starting transfers between devices: 6.22 us -> 9.49 us
    ppermute x1 -> x2, waiting for transfers between devices: 9.05 us -> 2.83 us  [body(): attended = attend(mine, lambda x: lax.ppermute(x, ('crop', 'y'), swaps))]
    ppermute x1 -> x2, starting transfers between devices: 2.57 us -> 5.84 us  [body(): attended = attend(mine, lambda x: lax.ppermute(x, ('crop', 'y'), swaps))]
    pallas_call x1 -> x2, Pallas kernels: 5.24 us -> 5.8 us  [the longest x1 2.93 us: attend(): pl.pallas_call(more_kernel, in_specs=[VMEM] * 4, out_specs=[VMEM, VMEM],...]
  transfers between devices with their start and end apart: 3 -> 4, of which waited for: 2 -> 3; matrix products, arithmetic and copies ran while one was open for 0% -> 0% of each run, Pallas kernels for 3% -> 4%
where the time goes in v5:
time: 186 us
  blocking collectives  152 us (82%)
  Pallas kernels  15.7 us (8%)
  starting transfers between devices  9.49 us (5%)
  waiting for transfers between devices  5.23 us (3%)
  between operations  2.56 us (1%)
    all_to_all x1, blocking collectives, body(): mine = lax.all_to_all(send, seq, 0, 0, tiled=True)  88.9 us
    all_to_all x1, blocking collectives, body(): returned = lax.all_to_all(attended, seq, 0, 0, tiled=True)  35.5 us
    all_to_all x1, blocking collectives, body(): everyone = lax.all_to_all(sums, seq, 0, 0, tiled=True)  27.9 us
    ppermute x2, starting transfers between devices, body(): attended = attend(mine, lambda x: lax.ppermute(x, ('crop', 'y'), swaps))  5.84 us
    pallas_call x1, Pallas kernels, attend(): pl.pallas_call(own_kernel, in_specs=[VMEM], out_specs=[VMEM, VMEM], out_s...  5.06 us
  transfers between devices with their start and end apart: 4, of which 3 were waited for; matrix products, arithmetic and copies ran while one was open for 0% of the time, Pallas kernels for 4%

profile of v5, /device:TPU:6, one launch (start us, length us, event | category | flops | bytes accessed | tf_op | source)
XLA Modules:
  0.0 186.1 jit_solution(17739272700345833423)
XLA Ops:
  0.6 2.4 %pack.1 = bf16[4,8,192,128]{3,2,1,0:T(8,128)(2,1)S(1)} custom-call(bf16[128,2048]{1,0:T(8,128)(2,1)} %q_hbm.1, bf16[128,2048]{1,0:T(8,128)(2,1)} %k_hbm.1, bf16[128,2048]{1,0:T(8,128)(2,1)} %v_hbm.1, f32[64,128]{1,0:T(8,128)} %constant.9.clone.cos_hbm, f32[64,128]{1,0:T(8,128)} %constant.10.clone.sin_hbm), custom_call_target="tpu_custom_call" | custom-call | tf_op jit(solution)/shard_map/pack/pallas_call | solution.py:113
  3.0 88.9 %all_to_all.15.mine_ref = bf16[32,192,128]{2,1,0:T(8,128)(2,1)S(1)} all-to-all(bf16[32,192,128]{2,1,0:T(8,128)(2,1)S(1)} %bitcast.6), channel_id=1, replica_groups=mesh['crop'=16,'y'=4,'z'=8] {'y','z'}, dimensions={0} | all-to-all | bytes 3145728 | tf_op jit(solution)/shard_map/all_to_all | solution.py:363
  91.9 0.1 fusion
  92.0 2.6 %collective-permute-start.1 = (bf16[16,128,128]{2,1,0:T(8,128)(2,1)S(1)}, bf16[16,128,128]{2,1,0:T(8,128)(2,1)S(1)}, u32[]{:S(2)}, u32[]{:S(2)}) collective-permute-start(bf16[16,128,128]{2,1,0:T(8,128)(2,1)S(1)} %get-tuple-element.17), channel_id=1, source_target_pairs={{0,8},{8,0},{16,24},{24,16},{32,56},{40,48},{48,40},{56,32},{64,72... | collective-permute-start | bytes 1572872 | tf_op jit(solution)/shard_map/ppermute | solution.py:364
  94.6 3.3 %collective-permute-start = (bf16[16,128,128]{2,1,0:T(8,128)(2,1)S(1)}, bf16[16,128,128]{2,1,0:T(8,128)(2,1)S(1)}, u32[]{:S(2)}, u32[]{:S(2)}) collective-permute-start(bf16[16,128,128]{2,1,0:T(8,128)(2,1)S(1)} %get-tuple-element.18), channel_id=1, source_target_pairs={{0,8},{8,0},{16,24},{24,16},{32,56},{40,48},{48,40},{56,32},{64,72... | collective-permute-start | bytes 1572872 | tf_op jit(solution)/shard_map/ppermute | solution.py:364
  97.9 5.1 %own_keys.1 = (f32[2048,256]{1,0:T(8,128)S(1)}, f32[2048,128]{1,0:T(8,128)S(1)}) custom-call(bf16[32,192,128]{2,1,0:T(8,128)(2,1)S(1)} %all_to_all.15.mine_ref), custom_call_target="tpu_custom_call" | custom-call | flops 3221225472 | bytes 4194304 | tf_op jit(solution)/shard_map/own_keys/pallas_call | solution.py:229
  103.0 0.2 collective-permute-done.1.other_ref
  103.1 2.9 %more_keys.1 = (f32[2048,256]{1,0:T(8,128)S(1)}, f32[2048,128]{1,0:T(8,128)S(1)}) custom-call(bf16[32,192,128]{2,1,0:T(8,128)(2,1)S(1)} %all_to_all.15.mine_ref, bf16[16,128,128]{2,1,0:T(8,128)(2,1)S(1)} %collective-permute-done.1.other_ref, f32[2048,256]{1,0:T(8,128)S(1)} %get-tuple-element.10.acc_ref, f32[2048,128]{1,0:T(8,128)S(1)} %get-tuple-element.11.top_ref), custom_call_target="tpu_custom_call" | custom-call | flops 1610612736 | bytes 4194304 | tf_op jit(solution)/shard_map/more_keys/pallas_call | solution.py:238
  106.0 2.7 %collective-permute-done.other_ref = bf16[16,128,128]{2,1,0:T(8,128)(2,1)S(1)} collective-permute-done((bf16[16,128,128]{2,1,0:T(8,128)(2,1)S(1)}, bf16[16,128,128]{2,1,0:T(8,128)(2,1)S(1)}, u32[]{:S(2)}, u32[]{:S(2)}) %collective-permute-start) | collective-permute-done | bytes 524320 | tf_op jit(solution)/shard_map/ppermute | solution.py:364
  108.7 2.9 %last_keys.1 = bf16[32,64,128]{2,1,0:T(8,128)(2,1)S(1)} custom-call(bf16[32,192,128]{2,1,0:T(8,128)(2,1)S(1)} %all_to_all.15.mine_ref, bf16[16,128,128]{2,1,0:T(8,128)(2,1)S(1)} %collective-permute-done.other_ref, f32[2048,256]{1,0:T(8,128)S(1)} %get-tuple-element.12.acc_ref, f32[2048,128]{1,0:T(8,128)S(1)} %get-tuple-element.13.top_ref), custom_call_target="tpu_custom_call" | custom-call | flops 1610612736 | bytes 4194304 | tf_op jit(solution)/shard_map/last_keys/pallas_call | solution.py:247
  111.6 0.0 copy-start.6
  111.6 0.0 copy-start
  111.6 0.0 copy-start.2
  111.6 0.0 copy-start.3
  111.6 0.0 copy-start.4
  111.7 35.5 %all_to_all.16.mixed_ref = bf16[32,64,128]{2,1,0:T(8,128)(2,1)S(1)} all-to-all(bf16[32,64,128]{2,1,0:T(8,128)(2,1)S(1)} %last_keys.1), channel_id=1, replica_groups=mesh['crop'=16,'y'=4,'z'=8] {'y','z'}, dimensions={0} | all-to-all | bytes 1048576 | tf_op jit(solution)/shard_map/all_to_all | solution.py:365
  147.1 0.5 features.1.mid_ref
  147.7 3.0 %collective-permute-start.2 = (bf16[128,256]{1,0:T(8,128)(2,1)S(1)}, bf16[128,256]{1,0:T(8,128)(2,1)S(1)}, u32[]{:S(2)}, u32[]{:S(2)}) collective-permute-start(bf16[128,256]{1,0:T(8,128)(2,1)S(1)} %features.1.mid_ref), channel_id=1, source_target_pairs={{0,1},{1,0},{2,3},{3,2},{4,5},{5,4},{6,7},{7,6},{8,9},{9,8},{10,11... | collective-permute-start | bytes 196616 | tf_op jit(solution)/shard_map/ppermute | solution.py:377
  150.7 0.7 collective-permute-start.3
  151.3 0.1 copy.15.class_bias_ref
  151.4 2.4 %collective-permute-done.2.pair_ref = bf16[128,256]{1,0:T(8,128)(2,1)S(1)} collective-permute-done((bf16[128,256]{1,0:T(8,128)(2,1)S(1)}, bf16[128,256]{1,0:T(8,128)(2,1)S(1)}, u32[]{:S(2)}, u32[]{:S(2)}) %collective-permute-start.2) | collective-permute-done | bytes 65568 | tf_op jit(solution)/shard_map/ppermute | solution.py:377
  153.8 2.0 %head.1 = (f32[16,8,256]{2,1,0:T(8,128)}, f32[8,256]{1,0:T(8,128)}, f32[32,1,128]{2,1,0:T(1,128)S(1)}) custom-call(bf16[128,256]{1,0:T(8,128)(2,1)S(1)} %collective-permute-done.2.pair_ref, bf16[128,256]{1,0:T(8,128)(2,1)S(1)} %features.1.mid_ref, bf16[128,256]{1,0:T(8,128)(2,1)S(1)} %collective-permute-done.3.far_ref, bf16[9,256,256]{2,1,0:T(8,128)(2,1)S(1)} %copy-done, ...), custom_call_target="tpu_custom_call" | custom-call | tf_op jit(solution)/shard_map/head/pallas_call | solution.py:379
  155.9 27.9 %all_to_all.17 = f32[32,1,128]{2,1,0:T(1,128)S(1)} all-to-all(f32[32,1,128]{2,1,0:T(1,128)S(1)} %get-tuple-element.16), channel_id=1, replica_groups=mesh['crop'=16,'y'=4,'z'=8] {'y','z'}, dimensions={0} | all-to-all | bytes 32768 | tf_op jit(solution)/shard_map/all_to_all | solution.py:395
  183.7 0.6 slice_reduce_fusion
  (10 shorter events, 0.0 us)
Async XLA Ops:
  92.0 11.1 %collective-permute-start.1 = (bf16[16,128,128]{2,1,0:T(8,128)(2,1)S(1)}, bf16[16,128,128]{2,1,0:T(8,128)(2,1)S(1)}, u32[]{:S(2)}, u32[]{:S(2)}) collective-permute-start(bf16[16,128,128]{2,1,0:T(8,128)(2,1)S(1)} %get-tuple-element.17), channel_id=1, source_target_pairs={{0,8},{8,0},{16,24},{24,16},{32,56},{40,48},{48,40},{56,32},{64,72... | collective-permute-start | bytes 1572872 | tf_op jit(solution)/shard_map/ppermute | solution.py:364
  94.6 14.1 %collective-permute-start = (bf16[16,128,128]{2,1,0:T(8,128)(2,1)S(1)}, bf16[16,128,128]{2,1,0:T(8,128)(2,1)S(1)}, u32[]{:S(2)}, u32[]{:S(2)}) collective-permute-start(bf16[16,128,128]{2,1,0:T(8,128)(2,1)S(1)} %get-tuple-element.18), channel_id=1, source_target_pairs={{0,8},{8,0},{16,24},{24,16},{32,56},{40,48},{48,40},{56,32},{64,72... | collective-permute-start | bytes 1572872 | tf_op jit(solution)/shard_map/ppermute | solution.py:364
  108.7 38.4 %copy-start.1 = (bf16[2048,256]{1,0:T(8,128)(2,1)S(1)}, bf16[2048,256]{1,0:T(8,128)(2,1)}, u32[]{:S(2)}) copy-start(bf16[2048,256]{1,0:T(8,128)(2,1)} %proj_ref.1) | copy-start | bytes 3145732
  108.7 38.4 %copy-start.5 = (f32[256]{0:T(256)S(1)}, f32[256]{0:T(256)}, u32[]{:S(2)}) copy-start(f32[256]{0:T(256)} %param.16) | copy-start | bytes 3076
  111.6 39.7 %copy-start.6 = (f32[16]{0:T(128)S(1)}, f32[16]{0:T(128)}, u32[]{:S(2)}) copy-start(f32[16]{0:T(128)} %param.20) | copy-start | bytes 196
  111.6 42.2 %copy-start = (bf16[9,256,256]{2,1,0:T(8,128)(2,1)S(1)}, bf16[9,256,256]{2,1,0:T(8,128)(2,1)}, u32[]{:S(2)}) copy-start(bf16[9,256,256]{2,1,0:T(8,128)(2,1)} %weight_ref.1) | copy-start | bytes 3538948
  111.6 42.2 %copy-start.2 = (bf16[9,16,256]{2,1,0:T(8,128)(2,1)S(1)}, bf16[9,16,256]{2,1,0:T(8,128)(2,1)}, u32[]{:S(2)}) copy-start(bf16[9,16,256]{2,1,0:T(8,128)(2,1)} %param.19) | copy-start | bytes 221188
  111.6 42.2 %copy-start.3 = (s32[8,256]{1,0:T(8,128)S(1)}, s32[8,256]{1,0:T(8,128)}, u32[]{:S(2)}) copy-start(s32[8,256]{1,0:T(8,128)} %labels_ref.1) | copy-start | bytes 24580
  111.6 42.2 %copy-start.4 = (f32[256]{0:T(256)S(1)}, f32[256]{0:T(256)}, u32[]{:S(2)}) copy-start(f32[256]{0:T(256)} %param.18) | copy-start | bytes 3076
  147.7 6.2 %collective-permute-start.2 = (bf16[128,256]{1,0:T(8,128)(2,1)S(1)}, bf16[128,256]{1,0:T(8,128)(2,1)S(1)}, u32[]{:S(2)}, u32[]{:S(2)}) collective-permute-start(bf16[128,256]{1,0:T(8,128)(2,1)S(1)} %features.1.mid_ref), channel_id=1, source_target_pairs={{0,1},{1,0},{2,3},{3,2},{4,5},{5,4},{6,7},{7,6},{8,9},{9,8},{10,11... | collective-permute-start | bytes 196616 | tf_op jit(solution)/shard_map/ppermute | solution.py:377
  150.7 3.2 %collective-permute-start.3 = (bf16[128,256]{1,0:T(8,128)(2,1)S(1)}, bf16[128,256]{1,0:T(8,128)(2,1)S(1)}, u32[]{:S(2)}, u32[]{:S(2)}) collective-permute-start(bf16[128,256]{1,0:T(8,128)(2,1)S(1)} %features.1.mid_ref), channel_id=1, source_target_pairs={{1,2},{2,1},{3,4},{4,3},{5,6},{6,5},{7,8},{8,7},{9,10},{10,9},{11,... | collective-permute-start | bytes 196616 | tf_op jit(solution)/shard_map/ppermute | solution.py:376

commit v6 on v5

--- a/solution.py
+++ b/solution.py
@@ -50,8 +50,7 @@
     return lax.rem(lax.axis_index("crop"), 2), place
 
 
-PARTS = 4
-PART = HEADS * HEAD_DIM // PARTS
+HALVES = 2
 
 
 def pack_kernel(q_hbm, k_hbm, v_hbm, cos_hbm, sin_hbm, out_ref, q_ref, k_ref, v_ref, cos_ref, sin_ref, sems, table_sems):
@@ -60,64 +59,56 @@
         pltpu.make_async_copy(cos_hbm, cos_ref, table_sems.at[0]),
         pltpu.make_async_copy(sin_hbm, sin_ref, table_sems.at[1]),
     ]
-    for copy in tables_in:
-        copy.start()
     copies = []
-    for part in range(PARTS):
-        lanes = pl.ds(part * PART, PART)
+    for half in range(HALVES):
+        rows = pl.ds(half * COLS, COLS)
         copies.append(
             [
-                pltpu.make_async_copy(hbm.at[:, lanes], ref.at[part], sems.at[part, which])
+                pltpu.make_async_copy(hbm.at[rows], ref.at[rows], sems.at[half, which])
                 for which, (hbm, ref) in enumerate(((q_hbm, q_ref), (k_hbm, k_ref), (v_hbm, v_ref)))
             ]
         )
         for copy in copies[-1]:
             copy.start()
+        if half == 0:
+            for copy in tables_in:
+                copy.start()
     lane = lax.broadcasted_iota(jnp.int32, (COLS, HEAD_DIM), 1)
     by_row = lane < HEAD_DIM // 2
     first = (lane % (HEAD_DIM // 2)) < HEAD_DIM // 4
     for copy in tables_in:
         copy.wait()
-    tables = []
-    for half in range(2):
+    for half in range(HALVES):
         row = pl.ds(2 * place + half, 1)
-        tables.append(
-            [jnp.where(by_row, ref[row, :], ref[...]) for ref in (cos_ref, sin_ref)]
-        )
-    for part in range(PARTS):
-        for copy in copies[part]:
-            copy.wait()
-        for inner in range(HEADS // PARTS):
-            head = part * (HEADS // PARTS) + inner
-            z = head // 2
-            lanes = slice(inner * HEAD_DIM, (inner + 1) * HEAD_DIM)
-            for half in range(2):
-                cosine, sine = tables[half]
-                rows = slice(half * COLS, (half + 1) * COLS)
+        cosine, sine = [
+            jnp.where(by_row, ref[row, :], ref[...]) for ref in (cos_ref, sin_ref)
+        ]
+        rows = slice(half * COLS, (half + 1) * COLS)
+        for index, ref in ((0, q_ref), (1, k_ref), (2, v_ref)):
+            copies[half][index].wait()
+            for head in range(HEADS):
                 y = lax.rem(2 * (head % 2) + half + core, YS)
-                for index, ref in ((0, q_ref), (1, k_ref)):
-                    x = ref[part, rows, lanes].astype(F32)
+                x = ref[rows, head * HEAD_DIM : (head + 1) * HEAD_DIM]
+                if index < 2:
+                    x = x.astype(F32)
                     partner = jnp.where(
                         first,
                         pltpu.roll(x, HEAD_DIM - HEAD_DIM // 4, 1),
                         pltpu.roll(x, HEAD_DIM // 4, 1),
                     )
-                    out_ref[y, z, index * COLS : (index + 1) * COLS, :] = (
-                        x * cosine + partner * sine
-                    ).astype(BF16)
-                out_ref[y, z, 2 * COLS :, :] = v_ref[part, rows, lanes]
+                    x = (x * cosine + partner * sine).astype(BF16)
+                out_ref[y, head // 2, index * COLS : (index + 1) * COLS, :] = x
 
 
 def pack(queries, keys, values, cosine, sine):
-    tokens = queries.shape[0]
     return pl.pallas_call(
         pack_kernel,
         in_specs=[pl.BlockSpec(memory_space=pltpu.HBM)] * 5,
         out_specs=VMEM,
         out_shape=jax.ShapeDtypeStruct((YS, ZS, 3 * COLS, HEAD_DIM), BF16),
-        scratch_shapes=[pltpu.VMEM((PARTS, tokens, PART), BF16)] * 3
+        scratch_shapes=[pltpu.VMEM(queries.shape, BF16)] * 3
         + [pltpu.VMEM((COLS, HEAD_DIM), F32)] * 2
-        + [pltpu.SemaphoreType.DMA((PARTS, 3)), pltpu.SemaphoreType.DMA((2,))],
+        + [pltpu.SemaphoreType.DMA((HALVES, 3)), pltpu.SemaphoreType.DMA((2,))],
         compiler_params=limit(8),
         name="pack",
     )(*(pltpu.with_memory_space_constraint(x, pltpu.HBM) for x in (queries, keys, values, cosine, sine)))
@@ -210,7 +201,7 @@
     each_block(visit)
 
 
-FIRST = 16
+FIRST = 20
 
 
 def attend(mine, swap):
@@ -323,25 +314,29 @@
     for s, side in enumerate(sides):
         first = UPSCALE * source - s + 1
         expand = jnp.where((target >= first) & (target < first + UPSCALE), 1.0, 0.0).astype(BF16)
+        parts = []
         for _ in range(3):
-            part = side.astype(BF16)
-            side = side - part.astype(F32)
-            term = jnp.dot(part, expand, preferred_element_type=F32)
-            spread_sum = term if spread_sum is None else spread_sum + term
+            parts.append(side.astype(BF16))
+            side = side - parts[-1].astype(F32)
+        terms = jnp.dot(jnp.concatenate(parts, axis=0), expand, preferred_element_type=F32)
+        count = side.shape[0]
+        term = terms[:count] + terms[count : 2 * count] + terms[2 * count :]
+        spread_sum = term if spread_sum is None else spread_sum + term
     class_ids = lax.broadcasted_iota(jnp.int32, (CLASSES, pixels), 0)
     loss_sum = jnp.zeros((1, pixels), F32)
-    for y in range(UPSCALE * strip):
-        combo = 3 * (y // UPSCALE) + (0, 1, 1, 2)[y % UPSCALE]
+    for combo in range(3 * strip):
         logits = spread_sum[combo * CLASSES : (combo + 1) * CLASSES] + class_bias_ref[...]
-        logits_ref[:, y, :] = logits
         highest = jnp.max(logits, axis=0, keepdims=True)
         log_total = highest + jnp.log(jnp.sum(jnp.exp(logits - highest), axis=0, keepdims=True))
-        chosen = class_ids == labels_ref[y : y + 1, :]
-        picked = jnp.sum(jnp.where(chosen, logits, 0.0), axis=0, keepdims=True)
-        loss = log_total - picked
-        losses_ref[y : y + 1, :] = loss
-        loss_sum = loss_sum + loss
-    total_loss = jnp.sum(loss_sum, axis=1, keepdims=True)
+        for inner in ((0,), (1, 2), (3,))[combo % 3]:
+            y = UPSCALE * (combo // 3) + inner
+            logits_ref[:, y, :] = logits
+            chosen = class_ids == labels_ref[y : y + 1, :]
+            picked = jnp.sum(jnp.where(chosen, logits, 0.0), axis=0, keepdims=True)
+            loss = log_total - picked
+            losses_ref[y : y + 1, :] = loss
+            loss_sum = loss_sum + loss
+    total_loss = jnp.sum(loss_sum, axis=1, keepdims=True) * (1.0 / (SEQ * losses_ref.size))
     sum_ref[...] = jnp.broadcast_to(total_loss[None], sum_ref.shape)
 
 
@@ -393,7 +388,7 @@
         class_weight.reshape(9 * CLASSES, CHANNELS), class_bias.reshape(CLASSES, 1), labels,
     )
     everyone = lax.all_to_all(sums, seq, 0, 0, tiled=True)
-    loss = (jnp.sum(everyone[:, 0, 0]) / (rows * pixels * SEQ)).reshape(1)
+    loss = jnp.sum(everyone[:, 0, 0]).reshape(1)
     return logits, losses, loss
 
 

time: 186 us -> 185 us (level)
  transfers between devices with their start and end apart: 4 -> 4, of which waited for: 3 -> 2; matrix products, arithmetic and copies ran while one was open for 0% -> 0% of each run, Pallas kernels for 4% -> 5%
where the time goes in v6:
time: 185 us
  blocking collectives  152 us (82%)
  Pallas kernels  17.4 us (9%)
  starting transfers between devices  9.49 us (5%)
  waiting for transfers between devices  3.93 us (2%)
    all_to_all x1, blocking collectives, body(): mine = lax.all_to_all(send, seq, 0, 0, tiled=True)  88.9 us
    all_to_all x1, blocking collectives, body(): returned = lax.all_to_all(attended, seq, 0, 0, tiled=True)  35.5 us
    all_to_all x1, blocking collectives, body(): everyone = lax.all_to_all(sums, seq, 0, 0, tiled=True)  27.9 us
    ppermute x2, starting transfers between devices, body(): attended = attend(mine, lambda x: lax.ppermute(x, ('crop', 'y'), swaps))  5.84 us
    pallas_call x1, Pallas kernels, attend(): pl.pallas_call(own_kernel, in_specs=[VMEM], out_specs=[VMEM, VMEM], out_s...  5.06 us
    pallas_call x1, Pallas kernels, attend(): pl.pallas_call(more_kernel, in_specs=[VMEM] * 4, out_specs=[VMEM, VMEM],...  4.33 us
  transfers between devices with their start and end apart: 4, of which 2 were waited for; matrix products, arithmetic and copies ran while one was open for 0% of the time, Pallas kernels for 5%

profile of v6, /device:TPU:6, one launch (start us, length us, event | category | flops | bytes accessed | tf_op | source)
XLA Modules:
  0.0 184.8 jit_solution(13271525019053753725)
XLA Ops:
  0.6 2.2 %pack.1 = bf16[4,8,192,128]{3,2,1,0:T(8,128)(2,1)S(1)} custom-call(bf16[128,2048]{1,0:T(8,128)(2,1)} %q_hbm.1, bf16[128,2048]{1,0:T(8,128)(2,1)} %k_hbm.1, bf16[128,2048]{1,0:T(8,128)(2,1)} %v_hbm.1, f32[64,128]{1,0:T(8,128)} %constant.6.clone.cos_hbm, f32[64,128]{1,0:T(8,128)} %constant.7.clone.sin_hbm), custom_call_target="tpu_custom_call" | custom-call | tf_op jit(solution)/shard_map/pack/pallas_call | solution.py:104
  2.8 88.9 %all_to_all.15.mine_ref = bf16[32,192,128]{2,1,0:T(8,128)(2,1)S(1)} all-to-all(bf16[32,192,128]{2,1,0:T(8,128)(2,1)S(1)} %bitcast.6), channel_id=1, replica_groups=mesh['crop'=16,'y'=4,'z'=8] {'y','z'}, dimensions={0} | all-to-all | bytes 3145728 | tf_op jit(solution)/shard_map/all_to_all | solution.py:358
  91.8 2.6 %collective-permute-start.1 = (bf16[20,128,128]{2,1,0:T(8,128)(2,1)S(1)}, bf16[20,128,128]{2,1,0:T(8,128)(2,1)S(1)}, u32[]{:S(2)}, u32[]{:S(2)}) collective-permute-start(bf16[20,128,128]{2,1,0:T(8,128)(2,1)S(1)} %slice.13), channel_id=1, source_target_pairs={{0,8},{8,0},{16,24},{24,16},{32,56},{40,48},{48,40},{56,32},{64,72... | collective-permute-start | bytes 1966088 | tf_op jit(solution)/shard_map/ppermute | solution.py:359
  94.4 3.3 %collective-permute-start = (bf16[12,128,128]{2,1,0:T(8,128)(2,1)S(1)}, bf16[12,128,128]{2,1,0:T(8,128)(2,1)S(1)}, u32[]{:S(2)}, u32[]{:S(2)}) collective-permute-start(bf16[12,128,128]{2,1,0:T(8,128)(2,1)S(1)} %slice.12), channel_id=1, source_target_pairs={{0,8},{8,0},{16,24},{24,16},{32,56},{40,48},{48,40},{56,32},{64,72... | collective-permute-start | bytes 1179656 | tf_op jit(solution)/shard_map/ppermute | solution.py:359
  97.7 5.1 %own_keys.1 = (f32[2048,256]{1,0:T(8,128)S(1)}, f32[2048,128]{1,0:T(8,128)S(1)}) custom-call(bf16[32,192,128]{2,1,0:T(8,128)(2,1)S(1)} %all_to_all.15.mine_ref), custom_call_target="tpu_custom_call" | custom-call | flops 3221225472 | bytes 4194304 | tf_op jit(solution)/shard_map/own_keys/pallas_call | solution.py:220
  102.8 1.5 collective-permute-done.1.other_ref
  104.3 4.3 %more_keys.1 = (f32[2048,256]{1,0:T(8,128)S(1)}, f32[2048,128]{1,0:T(8,128)S(1)}) custom-call(bf16[32,192,128]{2,1,0:T(8,128)(2,1)S(1)} %all_to_all.15.mine_ref, bf16[20,128,128]{2,1,0:T(8,128)(2,1)S(1)} %collective-permute-done.1.other_ref, f32[2048,256]{1,0:T(8,128)S(1)} %get-tuple-element.10.acc_ref, f32[2048,128]{1,0:T(8,128)S(1)} %get-tuple-element.11.top_ref), custom_call_target="tpu_custom_call" | custom-call | flops 2013265920 | bytes 4194304 | tf_op jit(solution)/shard_map/more_keys/pallas_call | solution.py:229
  108.7 0.0 copy-start.1
  108.7 0.0 copy-start.5
  108.7 3.4 %last_keys.1 = bf16[32,64,128]{2,1,0:T(8,128)(2,1)S(1)} custom-call(bf16[32,192,128]{2,1,0:T(8,128)(2,1)S(1)} %all_to_all.15.mine_ref, bf16[12,128,128]{2,1,0:T(8,128)(2,1)S(1)} %collective-permute-done.other_ref, f32[2048,256]{1,0:T(8,128)S(1)} %get-tuple-element.12.acc_ref, f32[2048,128]{1,0:T(8,128)S(1)} %get-tuple-element.13.top_ref), custom_call_target="tpu_custom_call" | custom-call | flops 1207959552 | bytes 4194304 | tf_op jit(solution)/shard_map/last_keys/pallas_call | solution.py:238
  112.1 0.0 copy-start.6
  112.1 0.0 copy-start
  112.1 0.0 copy-start.2
  112.1 0.0 copy-start.3
  112.1 0.0 copy-start.4
  112.1 35.5 %all_to_all.16.mixed_ref = bf16[32,64,128]{2,1,0:T(8,128)(2,1)S(1)} all-to-all(bf16[32,64,128]{2,1,0:T(8,128)(2,1)S(1)} %last_keys.1), channel_id=1, replica_groups=mesh['crop'=16,'y'=4,'z'=8] {'y','z'}, dimensions={0} | all-to-all | bytes 1048576 | tf_op jit(solution)/shard_map/all_to_all | solution.py:360
  147.6 0.5 features.1.mid_ref
  148.1 3.0 %collective-permute-start.2 = (bf16[128,256]{1,0:T(8,128)(2,1)S(1)}, bf16[128,256]{1,0:T(8,128)(2,1)S(1)}, u32[]{:S(2)}, u32[]{:S(2)}) collective-permute-start(bf16[128,256]{1,0:T(8,128)(2,1)S(1)} %features.1.mid_ref), channel_id=1, source_target_pairs={{0,1},{1,0},{2,3},{3,2},{4,5},{5,4},{6,7},{7,6},{8,9},{9,8},{10,11... | collective-permute-start | bytes 196616 | tf_op jit(solution)/shard_map/ppermute | solution.py:372
  151.1 0.7 collective-permute-start.3
  151.8 0.1 copy.15.class_bias_ref
  151.9 2.4 %collective-permute-done.2.pair_ref = bf16[128,256]{1,0:T(8,128)(2,1)S(1)} collective-permute-done((bf16[128,256]{1,0:T(8,128)(2,1)S(1)}, bf16[128,256]{1,0:T(8,128)(2,1)S(1)}, u32[]{:S(2)}, u32[]{:S(2)}) %collective-permute-start.2) | collective-permute-done | bytes 65568 | tf_op jit(solution)/shard_map/ppermute | solution.py:372
  154.3 2.0 %head.1 = (f32[16,8,256]{2,1,0:T(8,128)}, f32[8,256]{1,0:T(8,128)}, f32[32,1,128]{2,1,0:T(1,128)S(1)}) custom-call(bf16[128,256]{1,0:T(8,128)(2,1)S(1)} %collective-permute-done.2.pair_ref, bf16[128,256]{1,0:T(8,128)(2,1)S(1)} %features.1.mid_ref, bf16[128,256]{1,0:T(8,128)(2,1)S(1)} %collective-permute-done.3.far_ref, bf16[9,256,256]{2,1,0:T(8,128)(2,1)S(1)} %copy-done, ...), custom_call_target="tpu_custom_call" | custom-call | tf_op jit(solution)/shard_map/head/pallas_call | solution.py:374
  156.3 27.9 %all_to_all.17 = f32[32,1,128]{2,1,0:T(1,128)S(1)} all-to-all(f32[32,1,128]{2,1,0:T(1,128)S(1)} %get-tuple-element.16), channel_id=1, replica_groups=mesh['crop'=16,'y'=4,'z'=8] {'y','z'}, dimensions={0} | all-to-all | bytes 32768 | tf_op jit(solution)/shard_map/all_to_all | solution.py:390
  184.2 0.6 slice_reduce_fusion
  (11 shorter events, 0.1 us)
Async XLA Ops:
  91.8 12.5 %collective-permute-start.1 = (bf16[20,128,128]{2,1,0:T(8,128)(2,1)S(1)}, bf16[20,128,128]{2,1,0:T(8,128)(2,1)S(1)}, u32[]{:S(2)}, u32[]{:S(2)}) collective-permute-start(bf16[20,128,128]{2,1,0:T(8,128)(2,1)S(1)} %slice.13), channel_id=1, source_target_pairs={{0,8},{8,0},{16,24},{24,16},{32,56},{40,48},{48,40},{56,32},{64,72... | collective-permute-start | bytes 1966088 | tf_op jit(solution)/shard_map/ppermute | solution.py:359
  94.4 14.2 %collective-permute-start = (bf16[12,128,128]{2,1,0:T(8,128)(2,1)S(1)}, bf16[12,128,128]{2,1,0:T(8,128)(2,1)S(1)}, u32[]{:S(2)}, u32[]{:S(2)}) collective-permute-start(bf16[12,128,128]{2,1,0:T(8,128)(2,1)S(1)} %slice.12), channel_id=1, source_target_pairs={{0,8},{8,0},{16,24},{24,16},{32,56},{40,48},{48,40},{56,32},{64,72... | collective-permute-start | bytes 1179656 | tf_op jit(solution)/shard_map/ppermute | solution.py:359
  108.7 38.9 %copy-start.1 = (bf16[2048,256]{1,0:T(8,128)(2,1)S(1)}, bf16[2048,256]{1,0:T(8,128)(2,1)}, u32[]{:S(2)}) copy-start(bf16[2048,256]{1,0:T(8,128)(2,1)} %proj_ref.1) | copy-start | bytes 3145732
  108.7 38.9 %copy-start.5 = (f32[256]{0:T(256)S(1)}, f32[256]{0:T(256)}, u32[]{:S(2)}) copy-start(f32[256]{0:T(256)} %param.16) | copy-start | bytes 3076
  112.1 39.7 %copy-start.6 = (f32[16]{0:T(128)S(1)}, f32[16]{0:T(128)}, u32[]{:S(2)}) copy-start(f32[16]{0:T(128)} %param.20) | copy-start | bytes 196
  112.1 42.2 %copy-start = (bf16[9,256,256]{2,1,0:T(8,128)(2,1)S(1)}, bf16[9,256,256]{2,1,0:T(8,128)(2,1)}, u32[]{:S(2)}) copy-start(bf16[9,256,256]{2,1,0:T(8,128)(2,1)} %weight_ref.1) | copy-start | bytes 3538948
  112.1 42.2 %copy-start.2 = (bf16[9,16,256]{2,1,0:T(8,128)(2,1)S(1)}, bf16[9,16,256]{2,1,0:T(8,128)(2,1)}, u32[]{:S(2)}) copy-start(bf16[9,16,256]{2,1,0:T(8,128)(2,1)} %param.19) | copy-start | bytes 221188
  112.1 42.2 %copy-start.3 = (s32[8,256]{1,0:T(8,128)S(1)}, s32[8,256]{1,0:T(8,128)}, u32[]{:S(2)}) copy-start(s32[8,256]{1,0:T(8,128)} %labels_ref.1) | copy-start | bytes 24580
  112.1 42.2 %copy-start.4 = (f32[256]{0:T(256)S(1)}, f32[256]{0:T(256)}, u32[]{:S(2)}) copy-start(f32[256]{0:T(256)} %param.18) | copy-start | bytes 3076
  148.1 6.2 %collective-permute-start.2 = (bf16[128,256]{1,0:T(8,128)(2,1)S(1)}, bf16[128,256]{1,0:T(8,128)(2,1)S(1)}, u32[]{:S(2)}, u32[]{:S(2)}) collective-permute-start(bf16[128,256]{1,0:T(8,128)(2,1)S(1)} %features.1.mid_ref), channel_id=1, source_target_pairs={{0,1},{1,0},{2,3},{3,2},{4,5},{5,4},{6,7},{7,6},{8,9},{9,8},{10,11... | collective-permute-start | bytes 196616 | tf_op jit(solution)/shard_map/ppermute | solution.py:372
  151.1 3.2 %collective-permute-start.3 = (bf16[128,256]{1,0:T(8,128)(2,1)S(1)}, bf16[128,256]{1,0:T(8,128)(2,1)S(1)}, u32[]{:S(2)}, u32[]{:S(2)}) collective-permute-start(bf16[128,256]{1,0:T(8,128)(2,1)S(1)} %features.1.mid_ref), channel_id=1, source_target_pairs={{1,2},{2,1},{3,4},{4,3},{5,6},{6,5},{7,8},{8,7},{9,10},{10,9},{11,... | collective-permute-start | bytes 196616 | tf_op jit(solution)/shard_map/ppermute | solution.py:371

commit v7 on v6

--- a/solution.py
+++ b/solution.py
@@ -125,18 +125,20 @@
     return jnp.concatenate([value, jnp.ones_like(value)], axis=1)
 
 
-CHUNK = 512
-
-
-def sweep(query, key, value):
+OWN_CHUNK = 512
+MORE_CHUNK = 256
+LAST_CHUNK = 768
+
+
+def sweep(query, key, value, chunk):
     top = total = None
-    for start in range(0, key.shape[0], CHUNK):
-        scores = scores_of(query, key[start : start + CHUNK])
+    for start in range(0, key.shape[0], chunk):
+        scores = scores_of(query, key[start : start + chunk])
         before, top = top, jnp.max(scores, axis=1, keepdims=True)
         if before is not None:
             top = jnp.maximum(before, top)
         weights = jnp.exp2((scores - top) * EXP_SCALE).astype(BF16)
-        part = jnp.dot(weights, value[start : start + CHUNK], preferred_element_type=F32)
+        part = jnp.dot(weights, value[start : start + chunk], preferred_element_type=F32)
         total = part if before is None else total * jnp.exp2((before - top) * EXP_SCALE) + part
     return jnp.broadcast_to(top, (query.shape[0], HEAD_DIM)), total
 
@@ -172,7 +174,7 @@
 
     def visit(block, rows):
         query = mine_ref[block, :COLS, :].reshape(BLOCK * COLS, HEAD_DIM)
-        top_ref[rows, :], acc_ref[rows, :] = sweep(query, key, value)
+        top_ref[rows, :], acc_ref[rows, :] = sweep(query, key, value, OWN_CHUNK)
 
     each_block(visit)
 
@@ -182,7 +184,7 @@
 
     def visit(block, rows):
         query = mine_ref[block, :COLS, :].reshape(BLOCK * COLS, HEAD_DIM)
-        top, mixed, norm = joined(sweep(query, key, value), (top_ref[rows, :], acc_ref[rows, :]))
+        top, mixed, norm = joined(sweep(query, key, value, MORE_CHUNK), (top_ref[rows, :], acc_ref[rows, :]))
         new_top_ref[rows, :] = top
         new_acc_ref[rows, :HEAD_DIM] = mixed
         new_acc_ref[rows, HEAD_DIM:] = norm
@@ -195,7 +197,7 @@
 
     def visit(block, rows):
         query = mine_ref[block, :COLS, :].reshape(BLOCK * COLS, HEAD_DIM)
-        _, mixed, norm = joined(sweep(query, key, value), (top_ref[rows, :], acc_ref[rows, :]))
+        _, mixed, norm = joined(sweep(query, key, value, LAST_CHUNK), (top_ref[rows, :], acc_ref[rows, :]))
         out_ref[block, :, :] = (mixed / norm).astype(BF16).reshape(BLOCK, COLS, HEAD_DIM)
 
     each_block(visit)
@@ -388,7 +390,7 @@
         class_weight.reshape(9 * CLASSES, CHANNELS), class_bias.reshape(CLASSES, 1), labels,
     )
     everyone = lax.all_to_all(sums, seq, 0, 0, tiled=True)
-    loss = jnp.sum(everyone[:, 0, 0]).reshape(1)
+    loss = jnp.sum(everyone, axis=(0, 1))[:1]
     return logits, losses, loss
 
 

time: 185 us -> 184 us (level)
  transfers between devices with their start and end apart: 4 -> 4, of which waited for: 2 -> 3; matrix products, arithmetic and copies ran while one was open for 0% -> 0% of each run, Pallas kernels for 5% -> 5%
where the time goes in v7:
time: 184 us; the launch traced here: 183 us
  blocking collectives  152 us (83%)
  Pallas kernels  15.6 us (8%)
  starting transfers between devices  9.49 us (5%)
  waiting for transfers between devices  4.46 us (2%)
    all_to_all x1, blocking collectives, body(): mine = lax.all_to_all(send, seq, 0, 0, tiled=True)  88.9 us
    all_to_all x1, blocking collectives, body(): returned = lax.all_to_all(attended, seq, 0, 0, tiled=True)  35.5 us
    all_to_all x1, blocking collectives, body(): everyone = lax.all_to_all(sums, seq, 0, 0, tiled=True)  27.9 us
    ppermute x2, starting transfers between devices, body(): attended = attend(mine, lambda x: lax.ppermute(x, ('crop', 'y'), swaps))  5.84 us
    pallas_call x1, Pallas kernels, attend(): pl.pallas_call(own_kernel, in_specs=[VMEM], out_specs=[VMEM, VMEM], out_s...  5.06 us
  transfers between devices with their start and end apart: 4, of which 3 were waited for; matrix products, arithmetic and copies ran while one was open for 0% of the time, Pallas kernels for 5%

profile of v7, /device:TPU:6, one launch (start us, length us, event | category | flops | bytes accessed | tf_op | source)
XLA Modules:
  0.0 183.4 jit_solution(6220642328198643213)
XLA Ops:
  0.6 2.2 %pack.1 = bf16[4,8,192,128]{3,2,1,0:T(8,128)(2,1)S(1)} custom-call(bf16[128,2048]{1,0:T(8,128)(2,1)} %q_hbm.1, bf16[128,2048]{1,0:T(8,128)(2,1)} %k_hbm.1, bf16[128,2048]{1,0:T(8,128)(2,1)} %v_hbm.1, f32[64,128]{1,0:T(8,128)} %constant.6.clone.cos_hbm, f32[64,128]{1,0:T(8,128)} %constant.7.clone.sin_hbm), custom_call_target="tpu_custom_call" | custom-call | tf_op jit(solution)/shard_map/pack/pallas_call | solution.py:104
  2.8 88.9 %all_to_all.15.mine_ref = bf16[32,192,128]{2,1,0:T(8,128)(2,1)S(1)} all-to-all(bf16[32,192,128]{2,1,0:T(8,128)(2,1)S(1)} %bitcast.6), channel_id=1, replica_groups=mesh['crop'=16,'y'=4,'z'=8] {'y','z'}, dimensions={0} | all-to-all | bytes 3145728 | tf_op jit(solution)/shard_map/all_to_all | solution.py:360
  91.8 2.6 %collective-permute-start.1 = (bf16[20,128,128]{2,1,0:T(8,128)(2,1)S(1)}, bf16[20,128,128]{2,1,0:T(8,128)(2,1)S(1)}, u32[]{:S(2)}, u32[]{:S(2)}) collective-permute-start(bf16[20,128,128]{2,1,0:T(8,128)(2,1)S(1)} %slice.13), channel_id=1, source_target_pairs={{0,8},{8,0},{16,24},{24,16},{32,56},{40,48},{48,40},{56,32},{64,72... | collective-permute-start | bytes 1966088 | tf_op jit(solution)/shard_map/ppermute | solution.py:361
  94.4 3.3 %collective-permute-start = (bf16[12,128,128]{2,1,0:T(8,128)(2,1)S(1)}, bf16[12,128,128]{2,1,0:T(8,128)(2,1)S(1)}, u32[]{:S(2)}, u32[]{:S(2)}) collective-permute-start(bf16[12,128,128]{2,1,0:T(8,128)(2,1)S(1)} %slice.12), channel_id=1, source_target_pairs={{0,8},{8,0},{16,24},{24,16},{32,56},{40,48},{48,40},{56,32},{64,72... | collective-permute-start | bytes 1179656 | tf_op jit(solution)/shard_map/ppermute | solution.py:361
  97.7 5.1 %own_keys.1 = (f32[2048,256]{1,0:T(8,128)S(1)}, f32[2048,128]{1,0:T(8,128)S(1)}) custom-call(bf16[32,192,128]{2,1,0:T(8,128)(2,1)S(1)} %all_to_all.15.mine_ref), custom_call_target="tpu_custom_call" | custom-call | flops 3221225472 | bytes 4194304 | tf_op jit(solution)/shard_map/own_keys/pallas_call | solution.py:222
  102.8 1.5 collective-permute-done.1.other_ref
  104.3 3.7 %more_keys.1 = (f32[2048,256]{1,0:T(8,128)S(1)}, f32[2048,128]{1,0:T(8,128)S(1)}) custom-call(bf16[32,192,128]{2,1,0:T(8,128)(2,1)S(1)} %all_to_all.15.mine_ref, bf16[20,128,128]{2,1,0:T(8,128)(2,1)S(1)} %collective-permute-done.1.other_ref, f32[2048,256]{1,0:T(8,128)S(1)} %get-tuple-element.10.acc_ref, f32[2048,128]{1,0:T(8,128)S(1)} %get-tuple-element.11.top_ref), custom_call_target="tpu_custom_call" | custom-call | flops 2013265920 | bytes 4194304 | tf_op jit(solution)/shard_map/more_keys/pallas_call | solution.py:231
  108.0 0.5 collective-permute-done.other_ref
  108.5 2.2 %last_keys.1 = bf16[32,64,128]{2,1,0:T(8,128)(2,1)S(1)} custom-call(bf16[32,192,128]{2,1,0:T(8,128)(2,1)S(1)} %all_to_all.15.mine_ref, bf16[12,128,128]{2,1,0:T(8,128)(2,1)S(1)} %collective-permute-done.other_ref, f32[2048,256]{1,0:T(8,128)S(1)} %get-tuple-element.12.acc_ref, f32[2048,128]{1,0:T(8,128)S(1)} %get-tuple-element.13.top_ref), custom_call_target="tpu_custom_call" | custom-call | flops 1207959552 | bytes 4194304 | tf_op jit(solution)/shard_map/last_keys/pallas_call | solution.py:240
  110.8 0.0 copy-start.6
  110.8 0.0 copy-start
  110.8 0.0 copy-start.2
  110.8 0.0 copy-start.3
  110.8 0.0 copy-start.4
  110.8 35.5 %all_to_all.16.mixed_ref = bf16[32,64,128]{2,1,0:T(8,128)(2,1)S(1)} all-to-all(bf16[32,64,128]{2,1,0:T(8,128)(2,1)S(1)} %last_keys.1), channel_id=1, replica_groups=mesh['crop'=16,'y'=4,'z'=8] {'y','z'}, dimensions={0} | all-to-all | bytes 1048576 | tf_op jit(solution)/shard_map/all_to_all | solution.py:362
  146.3 0.5 features.1.mid_ref
  146.8 3.0 %collective-permute-start.2 = (bf16[128,256]{1,0:T(8,128)(2,1)S(1)}, bf16[128,256]{1,0:T(8,128)(2,1)S(1)}, u32[]{:S(2)}, u32[]{:S(2)}) collective-permute-start(bf16[128,256]{1,0:T(8,128)(2,1)S(1)} %features.1.mid_ref), channel_id=1, source_target_pairs={{0,1},{1,0},{2,3},{3,2},{4,5},{5,4},{6,7},{7,6},{8,9},{9,8},{10,11... | collective-permute-start | bytes 196616 | tf_op jit(solution)/shard_map/ppermute | solution.py:374
  149.8 0.7 collective-permute-start.3
  150.5 0.1 copy.15.class_bias_ref
  150.6 2.4 %collective-permute-done.2.pair_ref = bf16[128,256]{1,0:T(8,128)(2,1)S(1)} collective-permute-done((bf16[128,256]{1,0:T(8,128)(2,1)S(1)}, bf16[128,256]{1,0:T(8,128)(2,1)S(1)}, u32[]{:S(2)}, u32[]{:S(2)}) %collective-permute-start.2) | collective-permute-done | bytes 65568 | tf_op jit(solution)/shard_map/ppermute | solution.py:374
  153.0 0.0 collective-permute-done.3.far_ref
  153.0 2.0 %head.1 = (f32[16,8,256]{2,1,0:T(8,128)}, f32[8,256]{1,0:T(8,128)}, f32[32,1,128]{2,1,0:T(1,128)S(1)}) custom-call(bf16[128,256]{1,0:T(8,128)(2,1)S(1)} %collective-permute-done.2.pair_ref, bf16[128,256]{1,0:T(8,128)(2,1)S(1)} %features.1.mid_ref, bf16[128,256]{1,0:T(8,128)(2,1)S(1)} %collective-permute-done.3.far_ref, bf16[9,256,256]{2,1,0:T(8,128)(2,1)S(1)} %copy-done, ...), custom_call_target="tpu_custom_call" | custom-call | tf_op jit(solution)/shard_map/head/pallas_call | solution.py:376
  155.0 27.9 %all_to_all.17 = f32[32,1,128]{2,1,0:T(1,128)S(1)} all-to-all(f32[32,1,128]{2,1,0:T(1,128)S(1)} %get-tuple-element.16), channel_id=1, replica_groups=mesh['crop'=16,'y'=4,'z'=8] {'y','z'}, dimensions={0} | all-to-all | bytes 32768 | tf_op jit(solution)/shard_map/all_to_all | solution.py:392
  182.9 0.6 reduce_sum.9
  (11 shorter events, 0.1 us)
Async XLA Ops:
  91.8 12.5 %collective-permute-start.1 = (bf16[20,128,128]{2,1,0:T(8,128)(2,1)S(1)}, bf16[20,128,128]{2,1,0:T(8,128)(2,1)S(1)}, u32[]{:S(2)}, u32[]{:S(2)}) collective-permute-start(bf16[20,128,128]{2,1,0:T(8,128)(2,1)S(1)} %slice.13), channel_id=1, source_target_pairs={{0,8},{8,0},{16,24},{24,16},{32,56},{40,48},{48,40},{56,32},{64,72... | collective-permute-start | bytes 1966088 | tf_op jit(solution)/shard_map/ppermute | solution.py:361
  94.4 14.1 %collective-permute-start = (bf16[12,128,128]{2,1,0:T(8,128)(2,1)S(1)}, bf16[12,128,128]{2,1,0:T(8,128)(2,1)S(1)}, u32[]{:S(2)}, u32[]{:S(2)}) collective-permute-start(bf16[12,128,128]{2,1,0:T(8,128)(2,1)S(1)} %slice.12), channel_id=1, source_target_pairs={{0,8},{8,0},{16,24},{24,16},{32,56},{40,48},{48,40},{56,32},{64,72... | collective-permute-start | bytes 1179656 | tf_op jit(solution)/shard_map/ppermute | solution.py:361
  108.5 37.8 %copy-start.1 = (bf16[2048,256]{1,0:T(8,128)(2,1)S(1)}, bf16[2048,256]{1,0:T(8,128)(2,1)}, u32[]{:S(2)}) copy-start(bf16[2048,256]{1,0:T(8,128)(2,1)} %proj_ref.1) | copy-start | bytes 3145732
  108.5 37.8 %copy-start.5 = (f32[256]{0:T(256)S(1)}, f32[256]{0:T(256)}, u32[]{:S(2)}) copy-start(f32[256]{0:T(256)} %param.16) | copy-start | bytes 3076
  110.8 39.7 %copy-start.6 = (f32[16]{0:T(128)S(1)}, f32[16]{0:T(128)}, u32[]{:S(2)}) copy-start(f32[16]{0:T(128)} %param.20) | copy-start | bytes 196
  110.8 42.2 %copy-start = (bf16[9,256,256]{2,1,0:T(8,128)(2,1)S(1)}, bf16[9,256,256]{2,1,0:T(8,128)(2,1)}, u32[]{:S(2)}) copy-start(bf16[9,256,256]{2,1,0:T(8,128)(2,1)} %weight_ref.1) | copy-start | bytes 3538948
  110.8 42.2 %copy-start.2 = (bf16[9,16,256]{2,1,0:T(8,128)(2,1)S(1)}, bf16[9,16,256]{2,1,0:T(8,128)(2,1)}, u32[]{:S(2)}) copy-start(bf16[9,16,256]{2,1,0:T(8,128)(2,1)} %param.19) | copy-start | bytes 221188
  110.8 42.2 %copy-start.3 = (s32[8,256]{1,0:T(8,128)S(1)}, s32[8,256]{1,0:T(8,128)}, u32[]{:S(2)}) copy-start(s32[8,256]{1,0:T(8,128)} %labels_ref.1) | copy-start | bytes 24580
  110.8 42.2 %copy-start.4 = (f32[256]{0:T(256)S(1)}, f32[256]{0:T(256)}, u32[]{:S(2)}) copy-start(f32[256]{0:T(256)} %param.18) | copy-start | bytes 3076
  146.8 6.2 %collective-permute-start.2 = (bf16[128,256]{1,0:T(8,128)(2,1)S(1)}, bf16[128,256]{1,0:T(8,128)(2,1)S(1)}, u32[]{:S(2)}, u32[]{:S(2)}) collective-permute-start(bf16[128,256]{1,0:T(8,128)(2,1)S(1)} %features.1.mid_ref), channel_id=1, source_target_pairs={{0,1},{1,0},{2,3},{3,2},{4,5},{5,4},{6,7},{7,6},{8,9},{9,8},{10,11... | collective-permute-start | bytes 196616 | tf_op jit(solution)/shard_map/ppermute | solution.py:374
  149.8 3.2 %collective-permute-start.3 = (bf16[128,256]{1,0:T(8,128)(2,1)S(1)}, bf16[128,256]{1,0:T(8,128)(2,1)S(1)}, u32[]{:S(2)}, u32[]{:S(2)}) collective-permute-start(bf16[128,256]{1,0:T(8,128)(2,1)S(1)} %features.1.mid_ref), channel_id=1, source_target_pairs={{1,2},{2,1},{3,4},{4,3},{5,6},{6,5},{7,8},{8,7},{9,10},{10,9},{11,... | collective-permute-start | bytes 196616 | tf_op jit(solution)/shard_map/ppermute | solution.py:373

commit v8 on v7

--- a/solution.py
+++ b/solution.py
@@ -378,9 +378,9 @@
         in_specs=[VMEM] * 8,
         out_specs=[VMEM] * 3,
         out_shape=[
-            jax.ShapeDtypeStruct((CLASSES, rows, pixels), F32),
-            jax.ShapeDtypeStruct((rows, pixels), F32),
-            jax.ShapeDtypeStruct((SEQ, 1, HEAD_DIM), F32),
+            pltpu.VMEM((CLASSES, rows, pixels), F32),
+            pltpu.VMEM((rows, pixels), F32),
+            pltpu.VMEM((SEQ, 1, HEAD_DIM), F32),
         ],
         scratch_shapes=[pltpu.VMEM((3 * strip_tokens, CHANNELS), BF16)],
         compiler_params=limit(12),

time: 184 us -> 184 us (level)
  blocking collectives: 152 us -> 124 us
  starting transfers between devices: 9.49 us -> 25.1 us
  waiting for transfers between devices: 4.46 us -> 15.7 us
    all_to_all x1 -> x0, blocking collectives: 27.9 us -> none  [body(): everyone = lax.all_to_all(sums, seq, 0, 0, tiled=True)]
    all_to_all x0 -> x1, starting transfers between devices: none -> 15.6 us  [body(): everyone = lax.all_to_all(sums, seq, 0, 0, tiled=True)]
    all_to_all x0 -> x1, waiting for transfers between devices: none -> 11.3 us  [body(): everyone = lax.all_to_all(sums, seq, 0, 0, tiled=True)]
  transfers between devices with their start and end apart: 4 -> 5, of which waited for: 3 -> 4; matrix products, arithmetic and copies ran while one was open for 0% -> 1% of each run, Pallas kernels for 5% -> 5%
where the time goes in v8:
time: 184 us
  blocking collectives  124 us (67%)
  starting transfers between devices  25.1 us (14%)
  Pallas kernels  15.7 us (9%)
  waiting for transfers between devices  15.7 us (9%)
    all_to_all x1, blocking collectives, body(): mine = lax.all_to_all(send, seq, 0, 0, tiled=True)  88.9 us
    all_to_all x1, blocking collectives, body(): returned = lax.all_to_all(attended, seq, 0, 0, tiled=True)  35.5 us
    all_to_all x1, starting transfers between devices, body(): everyone = lax.all_to_all(sums, seq, 0, 0, tiled=True)  15.6 us
    all_to_all x1, waiting for transfers between devices, body(): everyone = lax.all_to_all(sums, seq, 0, 0, tiled=True)  11.3 us
    ppermute x2, starting transfers between devices, body(): attended = attend(mine, lambda x: lax.ppermute(x, ('crop', 'y'), swaps))  5.84 us
    pallas_call x1, Pallas kernels, attend(): pl.pallas_call(own_kernel, in_specs=[VMEM], out_specs=[VMEM, VMEM], out_s...  5.06 us
  transfers between devices with their start and end apart: 5, of which 4 were waited for; matrix products, arithmetic and copies ran while one was open for 1% of the time, Pallas kernels for 5%

profile of v8, /device:TPU:6, one launch (start us, length us, event | category | flops | bytes accessed | tf_op | source)
XLA Modules:
  0.0 183.7 jit_solution(16814606458665713191)
XLA Ops:
  0.6 2.2 %pack.1 = bf16[4,8,192,128]{3,2,1,0:T(8,128)(2,1)S(1)} custom-call(bf16[128,2048]{1,0:T(8,128)(2,1)} %q_hbm.1, bf16[128,2048]{1,0:T(8,128)(2,1)} %k_hbm.1, bf16[128,2048]{1,0:T(8,128)(2,1)} %v_hbm.1, f32[64,128]{1,0:T(8,128)} %constant.6.clone.cos_hbm, f32[64,128]{1,0:T(8,128)} %constant.7.clone.sin_hbm), custom_call_target="tpu_custom_call" | custom-call | tf_op jit(solution)/shard_map/pack/pallas_call | solution.py:104
  2.8 88.9 %all_to_all.15.mine_ref = bf16[32,192,128]{2,1,0:T(8,128)(2,1)S(1)} all-to-all(bf16[32,192,128]{2,1,0:T(8,128)(2,1)S(1)} %bitcast.6), channel_id=1, replica_groups=mesh['crop'=16,'y'=4,'z'=8] {'y','z'}, dimensions={0} | all-to-all | bytes 3145728 | tf_op jit(solution)/shard_map/all_to_all | solution.py:360
  91.8 2.6 %collective-permute-start.1 = (bf16[20,128,128]{2,1,0:T(8,128)(2,1)S(1)}, bf16[20,128,128]{2,1,0:T(8,128)(2,1)S(1)}, u32[]{:S(2)}, u32[]{:S(2)}) collective-permute-start(bf16[20,128,128]{2,1,0:T(8,128)(2,1)S(1)} %slice.13), channel_id=1, source_target_pairs={{0,8},{8,0},{16,24},{24,16},{32,56},{40,48},{48,40},{56,32},{64,72... | collective-permute-start | bytes 1966088 | tf_op jit(solution)/shard_map/ppermute | solution.py:361
  94.4 3.3 %collective-permute-start = (bf16[12,128,128]{2,1,0:T(8,128)(2,1)S(1)}, bf16[12,128,128]{2,1,0:T(8,128)(2,1)S(1)}, u32[]{:S(2)}, u32[]{:S(2)}) collective-permute-start(bf16[12,128,128]{2,1,0:T(8,128)(2,1)S(1)} %slice.12), channel_id=1, source_target_pairs={{0,8},{8,0},{16,24},{24,16},{32,56},{40,48},{48,40},{56,32},{64,72... | collective-permute-start | bytes 1179656 | tf_op jit(solution)/shard_map/ppermute | solution.py:361
  97.7 5.1 %own_keys.1 = (f32[2048,256]{1,0:T(8,128)S(1)}, f32[2048,128]{1,0:T(8,128)S(1)}) custom-call(bf16[32,192,128]{2,1,0:T(8,128)(2,1)S(1)} %all_to_all.15.mine_ref), custom_call_target="tpu_custom_call" | custom-call | flops 3221225472 | bytes 4194304 | tf_op jit(solution)/shard_map/own_keys/pallas_call | solution.py:222
  102.8 1.5 collective-permute-done.1.other_ref
  104.3 3.7 %more_keys.1 = (f32[2048,256]{1,0:T(8,128)S(1)}, f32[2048,128]{1,0:T(8,128)S(1)}) custom-call(bf16[32,192,128]{2,1,0:T(8,128)(2,1)S(1)} %all_to_all.15.mine_ref, bf16[20,128,128]{2,1,0:T(8,128)(2,1)S(1)} %collective-permute-done.1.other_ref, f32[2048,256]{1,0:T(8,128)S(1)} %get-tuple-element.10.acc_ref, f32[2048,128]{1,0:T(8,128)S(1)} %get-tuple-element.11.top_ref), custom_call_target="tpu_custom_call" | custom-call | flops 2013265920 | bytes 4194304 | tf_op jit(solution)/shard_map/more_keys/pallas_call | solution.py:231
  108.0 0.5 collective-permute-done.other_ref
  108.5 2.2 %last_keys.1 = bf16[32,64,128]{2,1,0:T(8,128)(2,1)S(1)} custom-call(bf16[32,192,128]{2,1,0:T(8,128)(2,1)S(1)} %all_to_all.15.mine_ref, bf16[12,128,128]{2,1,0:T(8,128)(2,1)S(1)} %collective-permute-done.other_ref, f32[2048,256]{1,0:T(8,128)S(1)} %get-tuple-element.12.acc_ref, f32[2048,128]{1,0:T(8,128)S(1)} %get-tuple-element.13.top_ref), custom_call_target="tpu_custom_call" | custom-call | flops 1207959552 | bytes 4194304 | tf_op jit(solution)/shard_map/last_keys/pallas_call | solution.py:240
  110.8 0.0 copy-start.6
  110.8 0.0 copy-start
  110.8 0.0 copy-start.4
  110.8 35.5 %all_to_all.16.mixed_ref = bf16[32,64,128]{2,1,0:T(8,128)(2,1)S(1)} all-to-all(bf16[32,64,128]{2,1,0:T(8,128)(2,1)S(1)} %last_keys.1), channel_id=1, replica_groups=mesh['crop'=16,'y'=4,'z'=8] {'y','z'}, dimensions={0} | all-to-all | bytes 1048576 | tf_op jit(solution)/shard_map/all_to_all | solution.py:362
  146.3 0.5 features.1.mid_ref
  146.8 3.0 %collective-permute-start.2 = (bf16[128,256]{1,0:T(8,128)(2,1)S(1)}, bf16[128,256]{1,0:T(8,128)(2,1)S(1)}, u32[]{:S(2)}, u32[]{:S(2)}) collective-permute-start(bf16[128,256]{1,0:T(8,128)(2,1)S(1)} %features.1.mid_ref), channel_id=1, source_target_pairs={{0,1},{1,0},{2,3},{3,2},{4,5},{5,4},{6,7},{7,6},{8,9},{9,8},{10,11... | collective-permute-start | bytes 196616 | tf_op jit(solution)/shard_map/ppermute | solution.py:374
  149.8 0.7 collective-permute-start.3
  150.5 0.1 copy.15.class_bias_ref
  150.6 2.4 %collective-permute-done.2.pair_ref = bf16[128,256]{1,0:T(8,128)(2,1)S(1)} collective-permute-done((bf16[128,256]{1,0:T(8,128)(2,1)S(1)}, bf16[128,256]{1,0:T(8,128)(2,1)S(1)}, u32[]{:S(2)}, u32[]{:S(2)}) %collective-permute-start.2) | collective-permute-done | bytes 65568 | tf_op jit(solution)/shard_map/ppermute | solution.py:374
  153.0 2.0 %head.1 = (f32[16,8,256]{2,1,0:T(8,128)S(1)}, f32[8,256]{1,0:T(8,128)S(1)}, f32[32,1,128]{2,1,0:T(1,128)}) custom-call(bf16[128,256]{1,0:T(8,128)(2,1)S(1)} %collective-permute-done.2.pair_ref, bf16[128,256]{1,0:T(8,128)(2,1)S(1)} %features.1.mid_ref, bf16[128,256]{1,0:T(8,128)(2,1)S(1)} %collective-permute-done.3.far_ref, bf16[9,256,256]{2,1,0:T(8,128)(2,1)S(1)} %copy-done, ...), custom_call_target="tpu_custom_call" | custom-call | tf_op jit(solution)/shard_map/head/pallas_call | solution.py:376
  155.1 15.6 %all-to-all-start.2 = ((f32[32,1,128]{2,1,0:T(1,128)}), f32[32,1,128]{2,1,0:T(1,128)S(1)}, u32[]{:S(2)}, u32[]{:S(2)}) async-start(f32[32,1,128]{2,1,0:T(1,128)} %get-tuple-element.16), calls=%async_computation.2 | async-start | bytes 32768 | tf_op jit(solution)/shard_map/all_to_all | solution.py:392
  170.7 0.7 copy.16
  171.3 0.6 copy.17
  171.9 11.3 %all-to-all-done.2 = f32[32,1,128]{2,1,0:T(1,128)S(1)} async-done(((f32[32,1,128]{2,1,0:T(1,128)}), f32[32,1,128]{2,1,0:T(1,128)S(1)}, u32[]{:S(2)}, u32[]{:S(2)}) %all-to-all-start.2) | async-done | bytes 16416 | tf_op jit(solution)/shard_map/all_to_all | solution.py:392
  183.2 0.6 reduce_sum.9
  (14 shorter events, 0.1 us)
Async XLA Ops:
  91.8 12.5 %collective-permute-start.1 = (bf16[20,128,128]{2,1,0:T(8,128)(2,1)S(1)}, bf16[20,128,128]{2,1,0:T(8,128)(2,1)S(1)}, u32[]{:S(2)}, u32[]{:S(2)}) collective-permute-start(bf16[20,128,128]{2,1,0:T(8,128)(2,1)S(1)} %slice.13), channel_id=1, source_target_pairs={{0,8},{8,0},{16,24},{24,16},{32,56},{40,48},{48,40},{56,32},{64,72... | collective-permute-start | bytes 1966088 | tf_op jit(solution)/shard_map/ppermute | solution.py:361
  94.4 14.1 %collective-permute-start = (bf16[12,128,128]{2,1,0:T(8,128)(2,1)S(1)}, bf16[12,128,128]{2,1,0:T(8,128)(2,1)S(1)}, u32[]{:S(2)}, u32[]{:S(2)}) collective-permute-start(bf16[12,128,128]{2,1,0:T(8,128)(2,1)S(1)} %slice.12), channel_id=1, source_target_pairs={{0,8},{8,0},{16,24},{24,16},{32,56},{40,48},{48,40},{56,32},{64,72... | collective-permute-start | bytes 1179656 | tf_op jit(solution)/shard_map/ppermute | solution.py:361
  108.5 37.8 %copy-start.1 = (bf16[2048,256]{1,0:T(8,128)(2,1)S(1)}, bf16[2048,256]{1,0:T(8,128)(2,1)}, u32[]{:S(2)}) copy-start(bf16[2048,256]{1,0:T(8,128)(2,1)} %proj_ref.1) | copy-start | bytes 3145732
  108.5 37.8 %copy-start.5 = (f32[256]{0:T(256)S(1)}, f32[256]{0:T(256)}, u32[]{:S(2)}) copy-start(f32[256]{0:T(256)} %param.16) | copy-start | bytes 3076
  110.8 39.7 %copy-start.6 = (f32[16]{0:T(128)S(1)}, f32[16]{0:T(128)}, u32[]{:S(2)}) copy-start(f32[16]{0:T(128)} %param.20) | copy-start | bytes 196
  110.8 42.2 %copy-start = (bf16[9,256,256]{2,1,0:T(8,128)(2,1)S(1)}, bf16[9,256,256]{2,1,0:T(8,128)(2,1)}, u32[]{:S(2)}) copy-start(bf16[9,256,256]{2,1,0:T(8,128)(2,1)} %weight_ref.1) | copy-start | bytes 3538948
  110.8 42.2 %copy-start.2 = (bf16[9,16,256]{2,1,0:T(8,128)(2,1)S(1)}, bf16[9,16,256]{2,1,0:T(8,128)(2,1)}, u32[]{:S(2)}) copy-start(bf16[9,16,256]{2,1,0:T(8,128)(2,1)} %param.19) | copy-start | bytes 221188
  110.8 42.2 %copy-start.3 = (s32[8,256]{1,0:T(8,128)S(1)}, s32[8,256]{1,0:T(8,128)}, u32[]{:S(2)}) copy-start(s32[8,256]{1,0:T(8,128)} %labels_ref.1) | copy-start | bytes 24580
  110.8 42.2 %copy-start.4 = (f32[256]{0:T(256)S(1)}, f32[256]{0:T(256)}, u32[]{:S(2)}) copy-start(f32[256]{0:T(256)} %param.18) | copy-start | bytes 3076
  146.8 6.2 %collective-permute-start.2 = (bf16[128,256]{1,0:T(8,128)(2,1)S(1)}, bf16[128,256]{1,0:T(8,128)(2,1)S(1)}, u32[]{:S(2)}, u32[]{:S(2)}) collective-permute-start(bf16[128,256]{1,0:T(8,128)(2,1)S(1)} %features.1.mid_ref), channel_id=1, source_target_pairs={{0,1},{1,0},{2,3},{3,2},{4,5},{5,4},{6,7},{7,6},{8,9},{9,8},{10,11... | collective-permute-start | bytes 196616 | tf_op jit(solution)/shard_map/ppermute | solution.py:374
  149.8 3.2 %collective-permute-start.3 = (bf16[128,256]{1,0:T(8,128)(2,1)S(1)}, bf16[128,256]{1,0:T(8,128)(2,1)S(1)}, u32[]{:S(2)}, u32[]{:S(2)}) collective-permute-start(bf16[128,256]{1,0:T(8,128)(2,1)S(1)} %features.1.mid_ref), channel_id=1, source_target_pairs={{1,2},{2,1},{3,4},{4,3},{5,6},{6,5},{7,8},{8,7},{9,10},{10,9},{11,... | collective-permute-start | bytes 196616 | tf_op jit(solution)/shard_map/ppermute | solution.py:373
  155.1 28.1 %all-to-all-start.2 = ((f32[32,1,128]{2,1,0:T(1,128)}), f32[32,1,128]{2,1,0:T(1,128)S(1)}, u32[]{:S(2)}, u32[]{:S(2)}) async-start(f32[32,1,128]{2,1,0:T(1,128)} %get-tuple-element.16), calls=%async_computation.2 | async-start | bytes 32768 | tf_op jit(solution)/shard_map/all_to_all | solution.py:392

commit v9 on v7

--- a/solution.py
+++ b/solution.py
@@ -312,18 +312,24 @@
     pixels = UPSCALE * COLS
     source = lax.broadcasted_iota(jnp.int32, (COLS, pixels), 0)
     target = lax.broadcasted_iota(jnp.int32, (COLS, pixels), 1)
-    spread_sum = None
-    for s, side in enumerate(sides):
+    expands = []
+    for s in range(3):
         first = UPSCALE * source - s + 1
-        expand = jnp.where((target >= first) & (target < first + UPSCALE), 1.0, 0.0).astype(BF16)
-        parts = []
-        for _ in range(3):
-            parts.append(side.astype(BF16))
-            side = side - parts[-1].astype(F32)
-        terms = jnp.dot(jnp.concatenate(parts, axis=0), expand, preferred_element_type=F32)
-        count = side.shape[0]
-        term = terms[:count] + terms[count : 2 * count] + terms[2 * count :]
-        spread_sum = term if spread_sum is None else spread_sum + term
+        expands.append(
+            jnp.where((target >= first) & (target < first + UPSCALE), 1.0, 0.0).astype(BF16)
+        )
+    side = jnp.concatenate(sides, axis=1)
+    parts = []
+    for _ in range(3):
+        parts.append(side.astype(BF16))
+        side = side - parts[-1].astype(F32)
+    terms = jnp.dot(
+        jnp.concatenate(parts, axis=0),
+        jnp.concatenate(expands, axis=0),
+        preferred_element_type=F32,
+    )
+    count = side.shape[0]
+    spread_sum = terms[:count] + terms[count : 2 * count] + terms[2 * count :]
     class_ids = lax.broadcasted_iota(jnp.int32, (CLASSES, pixels), 0)
     loss_sum = jnp.zeros((1, pixels), F32)
     for combo in range(3 * strip):

time: 184 us -> 184 us (level)
  no operation moved by 1% of the time
where the time goes in v9:
time: 184 us; the launch traced here: 183 us
  blocking collectives  152 us (83%)
  Pallas kernels  15.5 us (8%)
  starting transfers between devices  9.49 us (5%)
  waiting for transfers between devices  4.46 us (2%)
    all_to_all x1, blocking collectives, body(): mine = lax.all_to_all(send, seq, 0, 0, tiled=True)  88.9 us
    all_to_all x1, blocking collectives, body(): returned = lax.all_to_all(attended, seq, 0, 0, tiled=True)  35.5 us
    all_to_all x1, blocking collectives, body(): everyone = lax.all_to_all(sums, seq, 0, 0, tiled=True)  27.9 us
    ppermute x2, starting transfers between devices, body(): attended = attend(mine, lambda x: lax.ppermute(x, ('crop', 'y'), swaps))  5.84 us
    pallas_call x1, Pallas kernels, attend(): pl.pallas_call(own_kernel, in_specs=[VMEM], out_specs=[VMEM, VMEM], out_s...  5.06 us
  transfers between devices with their start and end apart: 4, of which 3 were waited for; matrix products, arithmetic and copies ran while one was open for 0% of the time, Pallas kernels for 5%

profile of v9, /device:TPU:6, one launch (start us, length us, event | category | flops | bytes accessed | tf_op | source)
XLA Modules:
  0.0 183.3 jit_solution(17097562079868040496)
XLA Ops:
  0.6 2.2 %pack.1 = bf16[4,8,192,128]{3,2,1,0:T(8,128)(2,1)S(1)} custom-call(bf16[128,2048]{1,0:T(8,128)(2,1)} %q_hbm.1, bf16[128,2048]{1,0:T(8,128)(2,1)} %k_hbm.1, bf16[128,2048]{1,0:T(8,128)(2,1)} %v_hbm.1, f32[64,128]{1,0:T(8,128)} %constant.6.clone.cos_hbm, f32[64,128]{1,0:T(8,128)} %constant.7.clone.sin_hbm), custom_call_target="tpu_custom_call" | custom-call | tf_op jit(solution)/shard_map/pack/pallas_call | solution.py:104
  2.8 88.9 %all_to_all.15.mine_ref = bf16[32,192,128]{2,1,0:T(8,128)(2,1)S(1)} all-to-all(bf16[32,192,128]{2,1,0:T(8,128)(2,1)S(1)} %bitcast.6), channel_id=1, replica_groups=mesh['crop'=16,'y'=4,'z'=8] {'y','z'}, dimensions={0} | all-to-all | bytes 3145728 | tf_op jit(solution)/shard_map/all_to_all | solution.py:366
  91.8 2.6 %collective-permute-start.1 = (bf16[20,128,128]{2,1,0:T(8,128)(2,1)S(1)}, bf16[20,128,128]{2,1,0:T(8,128)(2,1)S(1)}, u32[]{:S(2)}, u32[]{:S(2)}) collective-permute-start(bf16[20,128,128]{2,1,0:T(8,128)(2,1)S(1)} %slice.13), channel_id=1, source_target_pairs={{0,8},{8,0},{16,24},{24,16},{32,56},{40,48},{48,40},{56,32},{64,72... | collective-permute-start | bytes 1966088 | tf_op jit(solution)/shard_map/ppermute | solution.py:367
  94.4 3.3 %collective-permute-start = (bf16[12,128,128]{2,1,0:T(8,128)(2,1)S(1)}, bf16[12,128,128]{2,1,0:T(8,128)(2,1)S(1)}, u32[]{:S(2)}, u32[]{:S(2)}) collective-permute-start(bf16[12,128,128]{2,1,0:T(8,128)(2,1)S(1)} %slice.12), channel_id=1, source_target_pairs={{0,8},{8,0},{16,24},{24,16},{32,56},{40,48},{48,40},{56,32},{64,72... | collective-permute-start | bytes 1179656 | tf_op jit(solution)/shard_map/ppermute | solution.py:367
  97.7 5.1 %own_keys.1 = (f32[2048,256]{1,0:T(8,128)S(1)}, f32[2048,128]{1,0:T(8,128)S(1)}) custom-call(bf16[32,192,128]{2,1,0:T(8,128)(2,1)S(1)} %all_to_all.15.mine_ref), custom_call_target="tpu_custom_call" | custom-call | flops 3221225472 | bytes 4194304 | tf_op jit(solution)/shard_map/own_keys/pallas_call | solution.py:222
  102.8 1.5 collective-permute-done.1.other_ref
  104.3 3.7 %more_keys.1 = (f32[2048,256]{1,0:T(8,128)S(1)}, f32[2048,128]{1,0:T(8,128)S(1)}) custom-call(bf16[32,192,128]{2,1,0:T(8,128)(2,1)S(1)} %all_to_all.15.mine_ref, bf16[20,128,128]{2,1,0:T(8,128)(2,1)S(1)} %collective-permute-done.1.other_ref, f32[2048,256]{1,0:T(8,128)S(1)} %get-tuple-element.10.acc_ref, f32[2048,128]{1,0:T(8,128)S(1)} %get-tuple-element.11.top_ref), custom_call_target="tpu_custom_call" | custom-call | flops 2013265920 | bytes 4194304 | tf_op jit(solution)/shard_map/more_keys/pallas_call | solution.py:231
  108.0 0.5 collective-permute-done.other_ref
  108.5 2.2 %last_keys.1 = bf16[32,64,128]{2,1,0:T(8,128)(2,1)S(1)} custom-call(bf16[32,192,128]{2,1,0:T(8,128)(2,1)S(1)} %all_to_all.15.mine_ref, bf16[12,128,128]{2,1,0:T(8,128)(2,1)S(1)} %collective-permute-done.other_ref, f32[2048,256]{1,0:T(8,128)S(1)} %get-tuple-element.12.acc_ref, f32[2048,128]{1,0:T(8,128)S(1)} %get-tuple-element.13.top_ref), custom_call_target="tpu_custom_call" | custom-call | flops 1207959552 | bytes 4194304 | tf_op jit(solution)/shard_map/last_keys/pallas_call | solution.py:240
  110.8 0.0 copy-start.6
  110.8 0.0 copy-start
  110.8 0.0 copy-start.2
  110.8 0.0 copy-start.3
  110.8 0.0 copy-start.4
  110.8 35.5 %all_to_all.16.mixed_ref = bf16[32,64,128]{2,1,0:T(8,128)(2,1)S(1)} all-to-all(bf16[32,64,128]{2,1,0:T(8,128)(2,1)S(1)} %last_keys.1), channel_id=1, replica_groups=mesh['crop'=16,'y'=4,'z'=8] {'y','z'}, dimensions={0} | all-to-all | bytes 1048576 | tf_op jit(solution)/shard_map/all_to_all | solution.py:368
  146.3 0.5 features.1.mid_ref
  146.8 3.0 %collective-permute-start.2 = (bf16[128,256]{1,0:T(8,128)(2,1)S(1)}, bf16[128,256]{1,0:T(8,128)(2,1)S(1)}, u32[]{:S(2)}, u32[]{:S(2)}) collective-permute-start(bf16[128,256]{1,0:T(8,128)(2,1)S(1)} %features.1.mid_ref), channel_id=1, source_target_pairs={{0,1},{1,0},{2,3},{3,2},{4,5},{5,4},{6,7},{7,6},{8,9},{9,8},{10,11... | collective-permute-start | bytes 196616 | tf_op jit(solution)/shard_map/ppermute | solution.py:380
  149.8 0.7 collective-permute-start.3
  150.5 0.1 copy.15.class_bias_ref
  150.6 2.4 %collective-permute-done.2.pair_ref = bf16[128,256]{1,0:T(8,128)(2,1)S(1)} collective-permute-done((bf16[128,256]{1,0:T(8,128)(2,1)S(1)}, bf16[128,256]{1,0:T(8,128)(2,1)S(1)}, u32[]{:S(2)}, u32[]{:S(2)}) %collective-permute-start.2) | collective-permute-done | bytes 65568 | tf_op jit(solution)/shard_map/ppermute | solution.py:380
  153.0 0.0 collective-permute-done.3.far_ref
  153.0 1.8 %head.1 = (f32[16,8,256]{2,1,0:T(8,128)}, f32[8,256]{1,0:T(8,128)}, f32[32,1,128]{2,1,0:T(1,128)S(1)}) custom-call(bf16[128,256]{1,0:T(8,128)(2,1)S(1)} %collective-permute-done.2.pair_ref, bf16[128,256]{1,0:T(8,128)(2,1)S(1)} %features.1.mid_ref, bf16[128,256]{1,0:T(8,128)(2,1)S(1)} %collective-permute-done.3.far_ref, bf16[9,256,256]{2,1,0:T(8,128)(2,1)S(1)} %copy-done, ...), custom_call_target="tpu_custom_call" | custom-call | tf_op jit(solution)/shard_map/head/pallas_call | solution.py:382
  154.9 27.9 %all_to_all.17 = f32[32,1,128]{2,1,0:T(1,128)S(1)} all-to-all(f32[32,1,128]{2,1,0:T(1,128)S(1)} %get-tuple-element.16), channel_id=1, replica_groups=mesh['crop'=16,'y'=4,'z'=8] {'y','z'}, dimensions={0} | all-to-all | bytes 32768 | tf_op jit(solution)/shard_map/all_to_all | solution.py:398
  182.7 0.6 reduce_sum.9
  (11 shorter events, 0.1 us)
Async XLA Ops:
  91.8 12.5 %collective-permute-start.1 = (bf16[20,128,128]{2,1,0:T(8,128)(2,1)S(1)}, bf16[20,128,128]{2,1,0:T(8,128)(2,1)S(1)}, u32[]{:S(2)}, u32[]{:S(2)}) collective-permute-start(bf16[20,128,128]{2,1,0:T(8,128)(2,1)S(1)} %slice.13), channel_id=1, source_target_pairs={{0,8},{8,0},{16,24},{24,16},{32,56},{40,48},{48,40},{56,32},{64,72... | collective-permute-start | bytes 1966088 | tf_op jit(solution)/shard_map/ppermute | solution.py:367
  94.4 14.1 %collective-permute-start = (bf16[12,128,128]{2,1,0:T(8,128)(2,1)S(1)}, bf16[12,128,128]{2,1,0:T(8,128)(2,1)S(1)}, u32[]{:S(2)}, u32[]{:S(2)}) collective-permute-start(bf16[12,128,128]{2,1,0:T(8,128)(2,1)S(1)} %slice.12), channel_id=1, source_target_pairs={{0,8},{8,0},{16,24},{24,16},{32,56},{40,48},{48,40},{56,32},{64,72... | collective-permute-start | bytes 1179656 | tf_op jit(solution)/shard_map/ppermute | solution.py:367
  108.5 37.8 %copy-start.1 = (bf16[2048,256]{1,0:T(8,128)(2,1)S(1)}, bf16[2048,256]{1,0:T(8,128)(2,1)}, u32[]{:S(2)}) copy-start(bf16[2048,256]{1,0:T(8,128)(2,1)} %proj_ref.1) | copy-start | bytes 3145732
  108.5 37.8 %copy-start.5 = (f32[256]{0:T(256)S(1)}, f32[256]{0:T(256)}, u32[]{:S(2)}) copy-start(f32[256]{0:T(256)} %param.16) | copy-start | bytes 3076
  110.8 39.7 %copy-start.6 = (f32[16]{0:T(128)S(1)}, f32[16]{0:T(128)}, u32[]{:S(2)}) copy-start(f32[16]{0:T(128)} %param.20) | copy-start | bytes 196
  110.8 42.2 %copy-start = (bf16[9,256,256]{2,1,0:T(8,128)(2,1)S(1)}, bf16[9,256,256]{2,1,0:T(8,128)(2,1)}, u32[]{:S(2)}) copy-start(bf16[9,256,256]{2,1,0:T(8,128)(2,1)} %weight_ref.1) | copy-start | bytes 3538948
  110.8 42.2 %copy-start.2 = (bf16[9,16,256]{2,1,0:T(8,128)(2,1)S(1)}, bf16[9,16,256]{2,1,0:T(8,128)(2,1)}, u32[]{:S(2)}) copy-start(bf16[9,16,256]{2,1,0:T(8,128)(2,1)} %param.19) | copy-start | bytes 221188
  110.8 42.2 %copy-start.3 = (s32[8,256]{1,0:T(8,128)S(1)}, s32[8,256]{1,0:T(8,128)}, u32[]{:S(2)}) copy-start(s32[8,256]{1,0:T(8,128)} %labels_ref.1) | copy-start | bytes 24580
  110.8 42.2 %copy-start.4 = (f32[256]{0:T(256)S(1)}, f32[256]{0:T(256)}, u32[]{:S(2)}) copy-start(f32[256]{0:T(256)} %param.18) | copy-start | bytes 3076
  146.8 6.2 %collective-permute-start.2 = (bf16[128,256]{1,0:T(8,128)(2,1)S(1)}, bf16[128,256]{1,0:T(8,128)(2,1)S(1)}, u32[]{:S(2)}, u32[]{:S(2)}) collective-permute-start(bf16[128,256]{1,0:T(8,128)(2,1)S(1)} %features.1.mid_ref), channel_id=1, source_target_pairs={{0,1},{1,0},{2,3},{3,2},{4,5},{5,4},{6,7},{7,6},{8,9},{9,8},{10,11... | collective-permute-start | bytes 196616 | tf_op jit(solution)/shard_map/ppermute | solution.py:380
  149.8 3.2 %collective-permute-start.3 = (bf16[128,256]{1,0:T(8,128)(2,1)S(1)}, bf16[128,256]{1,0:T(8,128)(2,1)S(1)}, u32[]{:S(2)}, u32[]{:S(2)}) collective-permute-start(bf16[128,256]{1,0:T(8,128)(2,1)S(1)} %features.1.mid_ref), channel_id=1, source_target_pairs={{1,2},{2,1},{3,4},{4,3},{5,6},{6,5},{7,8},{8,7},{9,10},{10,9},{11,... | collective-permute-start | bytes 196616 | tf_op jit(solution)/shard_map/ppermute | solution.py:379
